TPU v7x, 32 devices: a whole 2x2x4 slice. The times are simulated.
32 devices in a mesh: fsdp: 4 (over y, x), context: 4 (over z), tensor: 2 (over core).
Axes of the slice: x: 2, y: 2, z: 4, core: 2. Of those that a mesh axis runs over, the one named last changes fastest.
Arguments:
- tokens: bfloat16 [2, 4096, 2048], P(None, ('fsdp', 'context')), may hold values from -6 to 6
- cotangent: bfloat16 [2, 4096, 2048], P(None, ('fsdp', 'context')), may hold values from -6 to 6
- seg_parent: int32 [2, 32], P(None, 'fsdp'), may hold values from -1 to 7, as said below
- positions: int32 [2, 4096], P(None, 'fsdp'), may hold values from 0 to 895, as said below
- norm_gain: bfloat16 [2, 2048], P(None, 'fsdp'), may hold values from 0.5 to 1.5
- norm_bias: bfloat16 [2, 2048], P(None, 'fsdp'), may hold values from -1.1953125 to 1.1953125
- w_qkv: bfloat16 [3, 2048, 2048], P(None, 'fsdp', 'tensor'), may hold values from -0.125 to 0.125
- bias_qv: bfloat16 [2, 2048], P(None, ('tensor', 'fsdp')), may hold values from -1.1953125 to 1.1953125
- w_out: bfloat16 [2048, 2048], P('tensor', 'fsdp'), may hold values from -0.25 to 0.25
- bias_out: bfloat16 [2048], P('fsdp'), may hold values from -1.1953125 to 1.1953125
- w_up: bfloat16 [2048, 8192], P('fsdp', 'tensor'), may hold values from -0.125 to 0.125
- bias_up: bfloat16 [8192], P(('tensor', 'fsdp')), may hold values from -1.1953125 to 1.1953125
- w_down: bfloat16 [8192, 2048], P('tensor', 'fsdp'), may hold values from -0.0625 to 0.0625
- bias_down: bfloat16 [2048], P('fsdp'), may hold values from -1.1953125 to 1.1953125
Outputs:
- layer_out: bfloat16 [2, 4096, 2048], P(None, ('fsdp', 'context'))
- grad_tokens: bfloat16 [2, 4096, 2048], P(None, ('fsdp', 'context'))
- grad_norm_gain: float32 [2, 2048], P(None, 'fsdp')
- grad_norm_bias: float32 [2, 2048], P(None, 'fsdp')
- grad_w_qkv: float32 [3, 2048, 2048], P(None, 'fsdp', 'tensor')
- grad_bias_qv: float32 [2, 2048], P(None, ('tensor', 'fsdp'))
- grad_w_out: float32 [2048, 2048], P('tensor', 'fsdp')
- grad_bias_out: float32 [2048], P('fsdp')
- grad_w_up: float32 [2048, 8192], P('fsdp', 'tensor')
- grad_bias_up: float32 [8192], P(('tensor', 'fsdp'))
- grad_w_down: float32 [8192, 2048], P('tensor', 'fsdp')
- grad_bias_down: float32 [2048], P('fsdp')
Inputs may be any that keep to these rules, and one draw needn't show every extreme that they name: `seg_parent`: each micro-batch holds 4 trees of 8 entries; a tree is a trunk of 5 segments in a chain from a root, 1 branches whose parent is the trunk's last segment, and 2 leaves whose parent is each branch; which slot holds which segment is a permutation drawn from the seed for each tree. `positions`: A token's position is the depth of its segment in its tree times 128 plus its place within the segment.
All inputs are finite; a program needn't handle non-finite values.
Results may differ from a plain program's by a relative error of at most 0.02.
Values may be sent and summed in bfloat16 or wider, within the bound.
No kernel may reach another device: no remote copies, remote signals or barrier semaphores. Data moves between devices by JAX's collectives and lax.ppermute only.
A program may use at most 384 MiB of HBM per device.

v0:
```python
from functools import partial

import jax
import jax.numpy as jnp
from jax import lax
from jax.sharding import PartitionSpec as P

HEADS = 32
HEAD_DIM = 64
SEG = 128
TRUNK_SEGS = 5
MICRO = 2


HIGHEST_DOT = lax.Precision.HIGHEST
NEG_FILL = -1e30


def product(left_op, right_op):
    return jnp.dot(left_op, right_op, preferred_element_type=jnp.float32)


def across_rows(left_op, right_op):
    return lax.dot_general(
        left_op, right_op, (((0,), (0,)), ((), ())), preferred_element_type=jnp.float32
    )


def across_last(left_op, right_op):
    return lax.dot_general(
        left_op, right_op, (((1,), (1,)), ((), ())), preferred_element_type=jnp.float32
    )


def accumulate(previous, term):
    return previous + term


def norm_rows(values_in, gain, shift):
    row_mean = jnp.mean(values_in, axis=-1, keepdims=True)
    centred = values_in - row_mean
    variance = jnp.mean(centred * centred, axis=-1, keepdims=True)
    return centred * lax.rsqrt(variance + 1e-05) * gain + shift


def ancestry_table(parents):
    slot_ids = jnp.arange(parents.shape[0], dtype=jnp.int32)
    parent_step = (parents[:, None] == slot_ids[None, :]).astype(jnp.float32)
    reach_now = jnp.eye(parents.shape[0], dtype=jnp.float32)
    reached = reach_now
    for depth_step in range(TRUNK_SEGS + 1):
        reach_now = jnp.dot(reach_now, parent_step, precision=HIGHEST_DOT)
        reached = reached + reach_now
    return reached > 0.5


def exact_gelu(pre_act):
    return jax.nn.gelu(pre_act, approximate=False)


def head_first(matrix):
    return matrix.reshape(matrix.shape[0], matrix.shape[1] // HEAD_DIM, HEAD_DIM).transpose(1, 0, 2)


def rows_first(stacked):
    return stacked.transpose(1, 0, 2).reshape(stacked.shape[1], stacked.shape[0] * stacked.shape[2])


def masked_scores(queries, key_rows, head_slope, allowed, offsets):
    raw_scores = jnp.einsum("qd,kd->qk", queries, key_rows, preferred_element_type=jnp.float32)
    return jnp.where(allowed, raw_scores * HEAD_DIM ** (-0.5) + head_slope * offsets, NEG_FILL)


def head_forward(packed, allowed, offsets):
    queries, key_rows, values, head_slope = packed
    scores = masked_scores(queries, key_rows, head_slope, allowed, offsets)
    highest = jnp.max(scores, axis=-1, keepdims=True)
    raised = jnp.exp(scores - highest)
    row_total = jnp.sum(raised, axis=-1, keepdims=True)
    probabilities = (raised / row_total).astype(jnp.bfloat16)
    attended = product(probabilities, values)
    return (attended, (highest + jnp.log(row_total))[:, 0], probabilities)


def head_backward(packed, allowed, offsets):
    queries, key_rows, values, grad_out, head_slope, log_total = packed
    scores = masked_scores(queries, key_rows, head_slope, allowed, offsets)
    probabilities = jnp.exp(scores - log_total[:, None])
    grad_probs = jnp.einsum("qd,kd->qk", grad_out, values, preferred_element_type=jnp.float32)
    centre = jnp.sum(probabilities * grad_probs, axis=-1, keepdims=True)
    grad_scores = (probabilities * (grad_probs - centre)).astype(jnp.bfloat16)
    grad_queries = product(grad_scores, key_rows) * HEAD_DIM ** (-0.5)
    return (grad_queries, grad_scores)


def layer_pass(gathered, running, hidden_bf, grad_bf, parents, places, first_slot, slopes):
    norm_gains, norm_shifts, w_qkv, bias_qv, w_out, bias_out, w_up, bias_up, w_down, bias_down = (
        gathered
    )
    local_rows = hidden_bf.shape[0]
    hidden_in = hidden_bf.astype(jnp.float32)
    normed_f, norm_back = jax.vjp(
        norm_rows, hidden_in, norm_gains[0].astype(jnp.float32), norm_shifts[0].astype(jnp.float32)
    )
    normed = normed_f.astype(jnp.bfloat16)
    queries = (product(normed, w_qkv[0]) + bias_qv[0].astype(jnp.float32)).astype(jnp.bfloat16)
    key_rows = product(normed, w_qkv[1]).astype(jnp.bfloat16)
    values = (product(normed, w_qkv[2]) + bias_qv[1].astype(jnp.float32)).astype(jnp.bfloat16)
    all_keys, all_values = (
        lax.all_gather(key_rows, "context", axis=0, tiled=True),
        lax.all_gather(values, "context", axis=0, tiled=True),
    )
    ancestry = ancestry_table(parents)
    own_rows = lax.dynamic_slice_in_dim(ancestry, first_slot, local_rows // SEG, 0)
    allowed_slots = jnp.repeat(jnp.repeat(own_rows, SEG, axis=0), SEG, axis=1)
    query_places = lax.dynamic_slice_in_dim(places, first_slot * SEG, local_rows, 0)
    allowed = allowed_slots & (places[None, :] <= query_places[:, None])
    offsets = (places[None, :] - query_places[:, None]).astype(jnp.float32)
    head_queries = head_first(queries)
    head_keys = head_first(all_keys)
    head_values = head_first(all_values)
    head_out, log_total, kept_probs = lax.map(
        partial(head_forward, allowed=allowed, offsets=offsets),
        (head_queries, head_keys, head_values, slopes),
    )
    attended = rows_first(head_out).astype(jnp.bfloat16)
    branch = lax.psum(product(attended, w_out).astype(jnp.bfloat16), "tensor").astype(
        jnp.float32
    ) + bias_out.astype(jnp.float32)
    middle = hidden_in + branch
    normed_two_f, norm_two_back = jax.vjp(
        norm_rows, middle, norm_gains[1].astype(jnp.float32), norm_shifts[1].astype(jnp.float32)
    )
    normed_two = normed_two_f.astype(jnp.bfloat16)
    pre_act = product(normed_two, w_up) + bias_up.astype(jnp.float32)
    activated_f, gelu_back = jax.vjp(exact_gelu, pre_act)
    activated = activated_f.astype(jnp.bfloat16)
    layer_out = middle + (
        lax.psum(product(activated, w_down).astype(jnp.bfloat16), "tensor").astype(jnp.float32)
        + bias_down.astype(jnp.float32)
    )
    grad_w_down = across_rows(activated, grad_bf)
    grad_bias_down = jnp.sum(grad_bf.astype(jnp.float32), axis=0)
    grad_pre = gelu_back(across_last(grad_bf, w_down))[0].astype(jnp.bfloat16)
    grad_w_up = across_rows(normed_two, grad_pre)
    grad_bias_up = jnp.sum(grad_pre.astype(jnp.float32), axis=0)
    grad_normed_two = lax.psum(across_last(grad_pre, w_up).astype(jnp.bfloat16), "tensor").astype(
        jnp.float32
    )
    grad_middle_norm, grad_gain_two, grad_shift_two = norm_two_back(grad_normed_two)
    grad_middle = grad_bf.astype(jnp.float32) + grad_middle_norm
    grad_branch = grad_middle.astype(jnp.bfloat16)
    grad_w_out = across_rows(attended, grad_branch)
    grad_bias_out = jnp.sum(grad_branch.astype(jnp.float32), axis=0)
    grad_attended = across_last(grad_branch, w_out).astype(jnp.bfloat16)
    head_grads = head_first(grad_attended)
    grad_head_queries, grad_scores = lax.map(
        partial(head_backward, allowed=allowed, offsets=offsets),
        (head_queries, head_keys, head_values, head_grads, slopes, log_total),
    )
    grad_queries = rows_first(grad_head_queries).astype(jnp.bfloat16)
    grad_keys_part = jnp.einsum(
        "hqk,hqd->khd", grad_scores, head_queries, preferred_element_type=jnp.float32
    ) * HEAD_DIM ** (-0.5)
    grad_values_part = jnp.einsum(
        "hqk,hqd->khd", kept_probs, head_grads, preferred_element_type=jnp.float32
    )
    key_grads = lax.psum_scatter(
        jnp.stack(
            [
                grad_keys_part.reshape(local_rows * lax.axis_size("context"), -1),
                grad_values_part.reshape(local_rows * lax.axis_size("context"), -1),
            ],
            axis=1,
        ).astype(jnp.bfloat16),
        "context",
        scatter_dimension=0,
        tiled=True,
    ).astype(jnp.float32)
    grad_keys = key_grads[:, 0].astype(jnp.bfloat16)
    grad_values = key_grads[:, 1].astype(jnp.bfloat16)
    grad_w_qkv = jnp.stack(
        [
            across_rows(normed, grad_queries),
            across_rows(normed, grad_keys),
            across_rows(normed, grad_values),
        ]
    )
    grad_bias_qv = jnp.stack(
        [
            jnp.sum(grad_queries.astype(jnp.float32), axis=0),
            jnp.sum(grad_values.astype(jnp.float32), axis=0),
        ]
    )
    grad_normed = lax.psum(
        (
            across_last(grad_queries, w_qkv[0])
            + across_last(grad_keys, w_qkv[1])
            + across_last(grad_values, w_qkv[2])
        ).astype(jnp.bfloat16),
        "tensor",
    ).astype(jnp.float32)
    grad_input_norm, grad_gain_one, grad_shift_one = norm_back(grad_normed)
    grad_tokens = grad_middle + grad_input_norm
    fresh = (
        jnp.stack([grad_gain_one, grad_gain_two]),
        jnp.stack([grad_shift_one, grad_shift_two]),
        grad_w_qkv,
        grad_bias_qv,
        grad_w_out,
        grad_bias_out,
        grad_w_up,
        grad_bias_up,
        grad_w_down,
        grad_bias_down,
    )
    if running is None:
        summed = fresh
    else:
        summed = tuple((accumulate(previous, term) for previous, term in zip(running, fresh)))
    return (layer_out.astype(jnp.bfloat16), grad_tokens.astype(jnp.bfloat16), summed)


def per_device(
    tokens,
    cotangent,
    seg_parent,
    positions,
    norm_gain,
    norm_bias,
    w_qkv,
    bias_qv,
    w_out,
    bias_out,
    w_up,
    bias_up,
    w_down,
    bias_down,
):
    local_rows = tokens.shape[1]
    first_slot = lax.axis_index("context") * (local_rows // SEG)
    local_heads = w_qkv.shape[2] // HEAD_DIM
    head_ids = lax.axis_index("tensor") * local_heads + jnp.arange(local_heads, dtype=jnp.int32)
    slopes = jnp.exp2(-8.0 * (head_ids + 1).astype(jnp.float32) / HEADS)
    gathered = None
    outputs = []
    input_grads = []
    totals = None
    for batch_index in range(MICRO):
        gathered = (
            lax.all_gather(norm_gain, "fsdp", axis=1, tiled=True),
            lax.all_gather(norm_bias, "fsdp", axis=1, tiled=True),
            lax.all_gather(w_qkv, "fsdp", axis=1, tiled=True),
            lax.all_gather(bias_qv, "fsdp", axis=1, tiled=True),
            lax.all_gather(w_out, "fsdp", axis=1, tiled=True),
            lax.all_gather(bias_out, "fsdp", axis=0, tiled=True),
            lax.all_gather(w_up, "fsdp", axis=0, tiled=True),
            lax.all_gather(bias_up, "fsdp", axis=0, tiled=True),
            lax.all_gather(w_down, "fsdp", axis=1, tiled=True),
            lax.all_gather(bias_down, "fsdp", axis=0, tiled=True),
        )
        out_rows, grad_rows, totals = layer_pass(
            gathered,
            totals,
            tokens[batch_index],
            cotangent[batch_index],
            seg_parent[batch_index],
            positions[batch_index],
            first_slot,
            slopes,
        )
        outputs.append(out_rows)
        input_grads.append(grad_rows)
    shard_sums = (
        lax.psum_scatter(
            totals[0].astype(jnp.bfloat16), "fsdp", scatter_dimension=1, tiled=True
        ).astype(jnp.float32),
        lax.psum_scatter(
            totals[1].astype(jnp.bfloat16), "fsdp", scatter_dimension=1, tiled=True
        ).astype(jnp.float32),
        lax.psum_scatter(
            totals[2].astype(jnp.bfloat16), "fsdp", scatter_dimension=1, tiled=True
        ).astype(jnp.float32),
        lax.psum_scatter(
            totals[3].astype(jnp.bfloat16), "fsdp", scatter_dimension=1, tiled=True
        ).astype(jnp.float32),
        lax.psum_scatter(
            totals[4].astype(jnp.bfloat16), "fsdp", scatter_dimension=1, tiled=True
        ).astype(jnp.float32),
        lax.psum_scatter(
            totals[5].astype(jnp.bfloat16), "fsdp", scatter_dimension=0, tiled=True
        ).astype(jnp.float32),
        lax.psum_scatter(
            totals[6].astype(jnp.bfloat16), "fsdp", scatter_dimension=0, tiled=True
        ).astype(jnp.float32),
        lax.psum_scatter(
            totals[7].astype(jnp.bfloat16), "fsdp", scatter_dimension=0, tiled=True
        ).astype(jnp.float32),
        lax.psum_scatter(
            totals[8].astype(jnp.bfloat16), "fsdp", scatter_dimension=1, tiled=True
        ).astype(jnp.float32),
        lax.psum_scatter(
            totals[9].astype(jnp.bfloat16), "fsdp", scatter_dimension=0, tiled=True
        ).astype(jnp.float32),
    )
    reduced = (
        lax.psum(shard_sums[0].astype(jnp.bfloat16), "context").astype(jnp.float32),
        lax.psum(shard_sums[1].astype(jnp.bfloat16), "context").astype(jnp.float32),
        lax.psum(shard_sums[2].astype(jnp.bfloat16), "context").astype(jnp.float32),
        lax.psum(shard_sums[3].astype(jnp.bfloat16), "context").astype(jnp.float32),
        lax.psum(shard_sums[4].astype(jnp.bfloat16), "context").astype(jnp.float32),
        lax.psum(shard_sums[5].astype(jnp.bfloat16), "context").astype(jnp.float32),
        lax.psum(shard_sums[6].astype(jnp.bfloat16), "context").astype(jnp.float32),
        lax.psum(shard_sums[7].astype(jnp.bfloat16), "context").astype(jnp.float32),
        lax.psum(shard_sums[8].astype(jnp.bfloat16), "context").astype(jnp.float32),
        lax.psum(shard_sums[9].astype(jnp.bfloat16), "context").astype(jnp.float32),
    )
    return (
        jnp.stack(outputs),
        jnp.stack(input_grads),
        reduced[0],
        reduced[1],
        reduced[2],
        reduced[3],
        reduced[4],
        reduced[5],
        reduced[6],
        reduced[7],
        reduced[8],
        reduced[9],
    )


def solution(mesh):
    in_specs = (
        P(None, ("fsdp", "context"), None),
        P(None, ("fsdp", "context"), None),
        P(None, "fsdp"),
        P(None, "fsdp"),
        P(None, "fsdp"),
        P(None, "fsdp"),
        P(None, "fsdp", "tensor"),
        P(None, ("tensor", "fsdp")),
        P("tensor", "fsdp"),
        P("fsdp"),
        P("fsdp", "tensor"),
        P(("tensor", "fsdp")),
        P("tensor", "fsdp"),
        P("fsdp"),
    )
    out_specs = (
        P(None, ("fsdp", "context"), None),
        P(None, ("fsdp", "context"), None),
        P(None, "fsdp"),
        P(None, "fsdp"),
        P(None, "fsdp", "tensor"),
        P(None, ("tensor", "fsdp")),
        P("tensor", "fsdp"),
        P("fsdp"),
        P("fsdp", "tensor"),
        P(("tensor", "fsdp")),
        P("tensor", "fsdp"),
        P("fsdp"),
    )
    return jax.shard_map(
        per_device, mesh=mesh, in_specs=in_specs, out_specs=out_specs, check_vma=False
    )
```

profile of v0, /device:TPU:0, one launch (start us, length us, event | category | flops | bytes accessed | tf_op | source)
XLA Modules:
  0.0 2462.3 jit_solution(751354175220968647)
XLA Ops:
  8.0 9.6 all_gather.53
  17.6 7.9 all_gather.52
  26.4 108.7 %all-gather.11.cloned.1.call-done = bf16[3,2048,1024]{2,1,0:T(8,128)(2,1)} async-done(((bf16[3,512,1024]{2,1,0:T(8,128)(2,1)}), bf16[3,2048,1024]{2,1,0:T(8,128)(2,1)}) %all-gather.11.cloned.1.call-update) | async-done | bytes 12582928 | tf_op jit(solution)/shard_map/all_gather | solution.py:253
  139.5 8.0 all_gather.55
  160.1 25.4 %all-gather.13.cloned.1.call-done = bf16[1024,1024]{1,0:T(8,128)(2,1)} async-done(((bf16[256,1024]{1,0:T(8,128)(2,1)}), bf16[1024,1024]{1,0:T(8,128)(2,1)}) %all-gather.13.cloned.1.call-update) | async-done | bytes 2097168 | tf_op jit(solution)/shard_map/all_gather | solution.py:110
  194.2 38.1 %all-gather.15.cloned.1.call-done = bf16[1024,1024]{1,0:T(8,128)(2,1)} async-done(((bf16[256,1024]{1,0:T(8,128)(2,1)}), bf16[1024,1024]{1,0:T(8,128)(2,1)}) %all-gather.15.cloned.1.call-update) | async-done | bytes 2097168 | tf_op jit(solution)/shard_map/all_gather | solution.py:111
  236.3 4.9 copy.65
  246.6 104.7 %while.60 = (s32[]{:T(128)}, bf16[16,256,64]{1,2,0:T(8,128)(2,1)}, f32[16,256]{1,0:T(8,128)S(1)}, bf16[16,256,1024]{2,1,0:T(8,128)(2,1)}, bf16[16,256,64]{2,1,0:...) while((s32[]{:T(128)}, bf16[16,256,64]{1,2,0:T(8,128)(2,1)}, ...), condition=%wide.region_5.6_spmd.clone.clone, body=%wide.region_2.5_spmd.clone.clone.sunk | while | flops 71565056 | bytes 5920409 | solution.py:122
  356.0 8.5 all-gather
  364.5 9.8 all-reduce.14.cloned.1.call-done
  390.1 37.8 %all-gather.23.cloned.1.call-done = bf16[1024,1024]{1,0:T(8,128)(2,1)} async-done(((bf16[256,1024]{1,0:T(8,128)(2,1)}), bf16[1024,1024]{1,0:T(8,128)(2,1)}) %all-gather.23.cloned.1.call-update) | async-done | bytes 2097168 | tf_op jit(solution)/shard_map/all_gather | solution.py:110
  436.7 38.1 %all-gather.25.cloned.1.call-done = bf16[1024,1024]{1,0:T(8,128)(2,1)} async-done(((bf16[256,1024]{1,0:T(8,128)(2,1)}), bf16[1024,1024]{1,0:T(8,128)(2,1)}) %all-gather.25.cloned.1.call-update) | async-done | bytes 2097168 | tf_op jit(solution)/shard_map/all_gather | solution.py:111
  488.9 104.7 %while.61 = (s32[]{:T(128)}, bf16[16,256,64]{1,2,0:T(8,128)(2,1)}, f32[16,256]{1,0:T(8,128)S(1)}, bf16[16,256,1024]{2,1,0:T(8,128)(2,1)}, bf16[16,256,64]{2,1,0:...) while((s32[]{:T(128)}, bf16[16,256,64]{1,2,0:T(8,128)(2,1)}, ...), condition=%wide.region_15.16_spmd.clone.clone, body=%wide.region_12.15_spmd.clone.clone.sunk | while | flops 71565056 | bytes 5920409 | solution.py:122
  599.7 8.2 all_gather.61
  607.9 8.8 all-reduce.16.cloned.1.call-done
  619.6 157.6 %all-gather.19.cloned.1.call-done = bf16[2048,4096]{1,0:T(8,128)(2,1)} async-done(((bf16[512,4096]{1,0:T(8,128)(2,1)}), bf16[2048,4096]{1,0:T(8,128)(2,1)}) %all-gather.19.cloned.1.call-update) | async-done | bytes 16777232 | tf_op jit(solution)/shard_map/all_gather | solution.py:257
  777.2 13.2 convolution_add_fusion
  791.6 6.3 convolution_add_fusion.1
  797.9 138.3 %all-gather.21.cloned.1.call-done = bf16[4096,2048]{1,0:T(8,128)(2,1)} async-done(((bf16[4096,512]{1,0:T(8,128)(2,1)}), bf16[4096,2048]{1,0:T(8,128)(2,1)}) %all-gather.21.cloned.1.call-update) | async-done | bytes 16777232 | tf_op jit(solution)/shard_map/all_gather | solution.py:259
  936.2 20.1 convert_reduce_fusion.1
  956.3 11.9 convolution_convert_fusion.1
  968.3 19.9 convert_reduce_fusion
  988.1 11.9 convolution_convert_fusion
  1000.1 21.4 all-reduce.22.cloned.1.call-done
  1040.1 121.1 %while.62 = (s32[]{:T(128)}, bf16[16,256,64]{1,2,0:T(8,128)(2,1)S(1)}, bf16[16,256,1024]{2,1,0:T(8,128)(2,1)}, bf16[16,256,64]{2,1,0:T(8,128)(2,1)}, bf16[16,102...) while((s32[]{:T(128)}, ...), condition=%wide.region_25.26_spmd.clone.clone, body=%wide.region_23.25_spmd.clone.clone.sunk | while | flops 104349440 | bytes 8306329 | solution.py:157
  1161.2 5.2 convolution_convert_fusion.7
  1180.8 121.3 %while.63 = (s32[]{:T(128)}, bf16[16,256,64]{1,2,0:T(8,128)(2,1)S(1)}, bf16[16,256,1024]{2,1,0:T(8,128)(2,1)}, bf16[16,256,64]{2,1,0:T(8,128)(2,1)}, bf16[16,102...) while((s32[]{:T(128)}, ...), condition=%wide.region_35.36_spmd.clone.clone, body=%wide.region_33.35_spmd.clone.clone.sunk | while | flops 104349440 | bytes 8306329 | solution.py:157
  1302.1 5.2 convolution_convert_fusion.6
  1312.1 17.7 convolution_convert_fusion.2
  1329.9 17.1 convolution_convert_fusion.3
  1361.3 28.9 %reduce-scatter.18.cloned.1.call-done = bf16[256,2,1024]{0,2,1:T(8,128)(2,1)} async-done(((bf16[1024,2,1024]{0,2,1:T(8,128)(2,1)}), bf16[256,2,1024]{0,2,1:T(8,128)(2,1)}) %reduce-scatter.18.cloned.1.call-update) | async-done | bytes 1048592 | tf_op jit(solution)/shard_map/reduce_scatter | solution.py:168
  1409.7 17.0 fusion.233
  1426.7 19.4 add_convert_fusion.1
  1446.2 21.1 fusion.176
  1467.3 25.7 %add_convert_fusion = bf16[4096,2048]{1,0:T(8,128)(2,1)} fusion(f32[4096,2048]{1,0:T(8,128)} %fusion.176, bf16[2,256,2048]{2,1,0:T(8,128)(2,1)} %param.23, f32[256,4096]{1,0:T(8,128)} %convolution_add_fusion), kind=kOutput, calls=%fused_computation.104 | convolution fusion | flops 4379901952 | bytes 55574528 | tf_op jit(solution)/shard_map/dot_general | solution.py:24
  1498.5 4.8 convolution_bitcast_fusion.6
  1503.3 4.8 convolution_bitcast_fusion.2
  1512.8 15.5 fusion.80
  1540.1 102.7 %reduce-scatter.24.cloned.1.call-done = bf16[512,4096]{1,0:T(8,128)(2,1)} async-done(((bf16[2048,4096]{1,0:T(8,128)(2,1)}), bf16[512,4096]{1,0:T(8,128)(2,1)}) %reduce-scatter.24.cloned.1.call-update) | async-done | bytes 4194320 | tf_op jit(solution)/shard_map/reduce_scatter | solution.py:293
  1642.8 157.0 %reduce-scatter.26.cloned.1.call-done = bf16[4096,512]{1,0:T(8,128)(2,1)} async-done(((bf16[4096,2048]{1,0:T(8,128)(2,1)}), bf16[4096,512]{1,0:T(8,128)(2,1)}) %reduce-scatter.26.cloned.1.call-update) | async-done | bytes 4194320 | tf_op jit(solution)/shard_map/reduce_scatter | solution.py:299
  1799.8 124.0 %reduce-scatter.20.cloned.1.call-done = bf16[3,512,1024]{2,1,0:T(8,128)(2,1)} async-done(((bf16[3,2048,1024]{2,1,0:T(8,128)(2,1)}), bf16[3,512,1024]{2,1,0:T(8,128)(2,1)}) %reduce-scatter.20.cloned.1.call-update) | async-done | bytes 3145744 | tf_op jit(solution)/shard_map/reduce_scatter | solution.py:281
  1924.5 7.9 all-gather.1
  1936.3 15.1 all-reduce.5
  1962.3 17.3 reduce-scatter.28.cloned.1.call-done
  1980.6 27.5 %reduce-scatter.30.cloned.1.call-done = bf16[512,2]{1,0:T(8,128)(2,1)} async-done(((bf16[2048,2]{1,0:T(8,128)(2,1)}), bf16[512,2]{1,0:T(8,128)(2,1)}) %reduce-scatter.30.cloned.1.call-update) | async-done | bytes 2064
  2009.0 12.3 all-reduce.3
  2024.9 414.2 %all-reduce.18.cloned.1.call-done = (bf16[3,512,1024]{2,1,0:T(8,128)(2,1)}, bf16[1024,512]{1,0:T(8,128)(2,1)}, bf16[512,4096]{1,0:T(8,128)(2,1)}, bf16[4096,512]{1,0:T(8,128)(2,1)}) async-done(((bf16[3,512,1024]{2,1,0:T(8,128)(2,1)}, bf16[1024,512]{1,0:T(8,128)(2,1)}, bf16[512,4096]{1,0:T(8,128)(2,1)}, bf16[4096,512]{1,0:T(8,128)(2,1)}), (bf16[3,512,1024]{2,1,0:T(8,128)(2,1)}, bf16[1024,512]{1,0:T(8,128)(2,1)}, ...) | async-done | bytes 12582928 | tf_op jit(solution)/shard_map/psum | solution.py:309
  2439.0 5.5 convert_element_type.469
  (895 shorter events, 662.9 us)
Async XLA Ops:
  7.2 127.9 %all-gather.11.cloned.1.call-start = ((), (), s32[]{:S(2)}) async-start(), calls=%async_computation.9 | async-start | bytes 15728640 | tf_op jit(solution)/shard_map/all_gather | solution.py:253
  7.9 177.6 %all-gather.13.cloned.1.call-start = ((), (), s32[]{:S(2)}) async-start(), calls=%async_computation.10 | async-start | bytes 2621440 | tf_op jit(solution)/shard_map/all_gather | solution.py:110
  25.9 129.2 %copy-start.54 = (f32[256]{0:T(256)}, f32[256]{0:T(256)S(1)}, u32[]{:S(2)}) copy-start(f32[256]{0:T(256)S(1)} %broadcast_multiply_fusion.3) | copy-start | bytes 3076
  26.3 113.1 %copy-start.90 = (f32[256]{0:T(256)}, f32[256]{0:T(256)S(1)}, u32[]{:S(2)}) copy-start(f32[256]{0:T(256)S(1)} %fusion.133) | copy-start | bytes 3076
  26.3 128.7 %copy-start.59 = (f32[256]{0:T(256)}, f32[256]{0:T(256)S(1)}, u32[]{:S(2)}) copy-start(f32[256]{0:T(256)S(1)} %fusion.229) | copy-start | bytes 3076
  26.4 358.7 %copy-start.42 = (f32[1,2048]{1,0:T(1,128)}, f32[1,2048]{1,0:T(1,128)S(1)}, u32[]{:S(2)}) copy-start(f32[1,2048]{1,0:T(1,128)S(1)} %get-tuple-element.762) | copy-start | bytes 24580
  26.4 764.1 %copy-start.50 = (f32[1,2048]{1,0:T(1,128)}, f32[1,2048]{1,0:T(1,128)S(1)}, u32[]{:S(2)}) copy-start(f32[1,2048]{1,0:T(1,128)S(1)} %get-tuple-element.761) | copy-start | bytes 24580
  26.4 358.6 %copy-start.27 = (f32[1,2048]{1,0:T(1,128)}, f32[1,2048]{1,0:T(1,128)S(1)}, u32[]{:S(2)}) copy-start(f32[1,2048]{1,0:T(1,128)S(1)} %get-tuple-element.760) | copy-start | bytes 24580
  26.4 1002.5 %copy-start.48 = (f32[1,2048]{1,0:T(1,128)}, f32[1,2048]{1,0:T(1,128)S(1)}, u32[]{:S(2)}) copy-start(f32[1,2048]{1,0:T(1,128)S(1)} %get-tuple-element.759) | copy-start | bytes 24580
  139.4 92.9 %all-gather.15.cloned.1.call-start = ((), (), s32[]{:S(2)}) async-start(), calls=%async_computation.11 | async-start | bytes 2621440 | tf_op jit(solution)/shard_map/all_gather | solution.py:111
  152.0 199.3 %all-gather.17.cloned.1.call-start = ((), (), s32[]{:S(2)}) async-start(), calls=%async_computation.12 | async-start | bytes 5242880 | tf_op jit(solution)/shard_map/all_gather | solution.py:255
  152.6 221.7 %all-reduce.14.cloned.1.call-start = ((), (), s32[]{:S(2)}) async-start(), calls=%async_computation.13 | async-start | bytes 2097152 | tf_op jit(solution)/shard_map/psum | solution.py:127
  158.8 35.4 %copy-start.19 = (bf16[256,1024]{0,1:T(8,128)(2,1)}, bf16[256,1024]{0,1:T(8,128)(2,1)S(1)}, u32[]{:S(2)}) copy-start(bf16[256,1024]{0,1:T(8,128)(2,1)S(1)} %copy.60) | copy-start | bytes 1572868
  351.3 24.9 %copy-start.38 = (pred[256,8]{1,0:T(8,128)(4,1)}, pred[256,8]{1,0:T(8,128)(4,1)S(1)}, u32[]{:S(2)}) copy-start(pred[256,8]{1,0:T(8,128)(4,1)S(1)} %get-tuple-element.1315) | copy-start | bytes 6148
  351.3 25.0 %copy-start.76 = (f32[16,256]{1,0:T(8,128)}, f32[16,256]{1,0:T(8,128)S(1)}, u32[]{:S(2)}) copy-start(f32[16,256]{1,0:T(8,128)S(1)} %get-tuple-element.1163) | copy-start | bytes 49156
  351.3 25.0 %copy-start.95 = (s32[1024]{0:T(1024)}, s32[1024]{0:T(1024)S(1)}, u32[]{:S(2)}) copy-start(s32[1024]{0:T(1024)S(1)} %get-tuple-element.1365) | copy-start | bytes 12292
  351.3 25.0 %copy-start.102 = (s32[256]{0:T(256)}, s32[256]{0:T(256)S(1)}, u32[]{:S(2)}) copy-start(s32[256]{0:T(256)S(1)} %get-tuple-element.1366) | copy-start | bytes 3076
  356.0 72.0 %all-gather.23.cloned.1.call-start = ((), (), s32[]{:S(2)}) async-start(), calls=%async_computation.16 | async-start | bytes 2621440 | tf_op jit(solution)/shard_map/all_gather | solution.py:110
  364.5 664.4 %copy-start.44 = (f32[4,1,512]{2,1,0:T(1,128)}, f32[4,1,512]{2,1,0:T(1,128)S(1)}, u32[]{:S(2)}) copy-start(f32[4,1,512]{2,1,0:T(1,128)S(1)} %convert_element_type.492) | copy-start | bytes 24580
  364.5 20.5 copy-start.52
  380.6 94.2 %all-gather.25.cloned.1.call-start = ((), (), s32[]{:S(2)}) async-start(), calls=%async_computation.17 | async-start | bytes 2621440 | tf_op jit(solution)/shard_map/all_gather | solution.py:111
  385.0 231.8 %all-reduce.16.cloned.1.call-start = ((), (), s32[]{:S(2)}) async-start(), calls=%async_computation.18 | async-start | bytes 2097152 | tf_op jit(solution)/shard_map/psum | solution.py:127
  388.8 47.9 %copy-start.21 = (bf16[256,1024]{0,1:T(8,128)(2,1)}, bf16[256,1024]{0,1:T(8,128)(2,1)S(1)}, u32[]{:S(2)}) copy-start(bf16[256,1024]{0,1:T(8,128)(2,1)S(1)} %copy.66) | copy-start | bytes 1572868
  598.3 178.9 %all-gather.19.cloned.1.call-start = ((), (), s32[]{:S(2)}) async-start(), calls=%async_computation.14 | async-start | bytes 20971520 | tf_op jit(solution)/shard_map/all_gather | solution.py:257
  599.1 337.2 %all-gather.21.cloned.1.call-start = ((), (), s32[]{:S(2)}) async-start(), calls=%async_computation.15 | async-start | bytes 20971520 | tf_op jit(solution)/shard_map/all_gather | solution.py:259
  599.6 421.9 %all-reduce.22.cloned.1.call-start = ((), (), s32[]{:S(2)}) async-start(), calls=%async_computation.30 | async-start | bytes 4194304 | tf_op jit(solution)/shard_map/psum | solution.py:147
  607.9 421.0 %copy-start.56 = (f32[256]{0:T(256)}, f32[256]{0:T(256)S(1)}, u32[]{:S(2)}) copy-start(f32[256]{0:T(256)S(1)} %broadcast_multiply_fusion.2) | copy-start | bytes 3076
  619.0 410.0 %copy-start.63 = (f32[256]{0:T(256)}, f32[256]{0:T(256)S(1)}, u32[]{:S(2)}) copy-start(f32[256]{0:T(256)S(1)} %broadcast_multiply_fusion) | copy-start | bytes 3076
  619.6 409.4 %copy-start.68 = (f32[256]{0:T(256)}, f32[256]{0:T(256)S(1)}, u32[]{:S(2)}) copy-start(f32[256]{0:T(256)S(1)} %fusion.232) | copy-start | bytes 3076
  619.6 409.4 %copy-start.65 = (f32[256]{0:T(256)}, f32[256]{0:T(256)S(1)}, u32[]{:S(2)}) copy-start(f32[256]{0:T(256)S(1)} %fusion.230) | copy-start | bytes 3076
  1000.1 352.2 %reduce-scatter.16.cloned.1.call-start = ((), (), s32[]{:S(2)}) async-start(), calls=%async_computation.19 | async-start | bytes 5242880 | tf_op jit(solution)/shard_map/reduce_scatter | solution.py:168
  1161.2 185.8 %copy-start.25 = (bf16[16,256,64]{1,2,0:T(8,128)(2,1)}, bf16[16,256,64]{1,2,0:T(8,128)(2,1)S(1)}, u32[]{:S(2)}) copy-start(bf16[16,256,64]{1,2,0:T(8,128)(2,1)S(1)} %get-tuple-element.239) | copy-start | bytes 1572868
  1171.2 219.0 %reduce-scatter.18.cloned.1.call-start = ((), (), s32[]{:S(2)}) async-start(), calls=%async_computation.20 | async-start | bytes 5242880 | tf_op jit(solution)/shard_map/reduce_scatter | solution.py:168
  1302.1 47.6 %copy-start.23 = (bf16[16,256,64]{1,2,0:T(8,128)(2,1)}, bf16[16,256,64]{1,2,0:T(8,128)(2,1)S(1)}, u32[]{:S(2)}) copy-start(bf16[16,256,64]{1,2,0:T(8,128)(2,1)S(1)} %get-tuple-element.243) | copy-start | bytes 1572868
  1312.1 220.6 %all-reduce.20.cloned.1.call-start = ((), (), s32[]{:S(2)}) async-start(), calls=%async_computation.29 | async-start | bytes 8388608 | tf_op jit(solution)/shard_map/psum | solution.py:139
  1312.1 34.9 %slice-start = ((s8[12582912]{0:T(1024)(128)(4,1)}), s8[4194304]{0:T(1024)(128)(4,1)S(1)}, s32[]{:S(2)}) async-start(s8[12582912]{0:T(1024)(128)(4,1)} %bitcast.589), calls=%async_computation.31 | async-start | bytes 8388608
  1312.1 34.9 %slice-start.1 = ((s8[12582912]{0:T(1024)(128)(4,1)}), s8[4194304]{0:T(1024)(128)(4,1)S(1)}, s32[]{:S(2)}) async-start(s8[12582912]{0:T(1024)(128)(4,1)} %bitcast.589), calls=%async_computation.32 | async-start | bytes 8388608
  1399.1 141.0 %reduce-scatter.22.cloned.1.call-start = ((), (), s32[]{:S(2)}) async-start(), calls=%async_computation.22 | async-start | bytes 5242880 | tf_op jit(solution)/shard_map/reduce_scatter | solution.py:287
  1407.1 235.7 %reduce-scatter.24.cloned.1.call-start = ((), (), s32[]{:S(2)}) async-start(), calls=%async_computation.23 | async-start | bytes 20971520 | tf_op jit(solution)/shard_map/reduce_scatter | solution.py:293
  1446.2 353.7 %reduce-scatter.26.cloned.1.call-start = ((), (), s32[]{:S(2)}) async-start(), calls=%async_computation.24 | async-start | bytes 20971520 | tf_op jit(solution)/shard_map/reduce_scatter | solution.py:299
  1493.1 430.7 %reduce-scatter.20.cloned.1.call-start = ((), (), s32[]{:S(2)}) async-start(), calls=%async_computation.21 | async-start | bytes 15728640 | tf_op jit(solution)/shard_map/reduce_scatter | solution.py:281
  1528.3 423.3 %reduce-scatter.32.cloned.1.call-start = ((), (), s32[]{:S(2)}) async-start(), calls=%async_computation.27 | async-start | bytes 327680
  1532.4 447.1 %reduce-scatter.28.cloned.1.call-start = ((), (), s32[]{:S(2)}) async-start(), calls=%async_computation.25 | async-start | bytes 655360
  1538.8 469.2 %reduce-scatter.30.cloned.1.call-start = ((), (), s32[]{:S(2)}) async-start(), calls=%async_computation.26 | async-start | bytes 655360
  1540.0 899.0 %all-reduce.18.cloned.1.call-start = ((), (), s32[]{:S(2)}) async-start(), calls=%async_computation.28 | async-start | bytes 25165824 | tf_op jit(solution)/shard_map/psum | solution.py:309
  1923.9 28.7 %copy-start.10 = (bf16[256,2048]{1,0:T(8,128)(2,1)S(1)}, bf16[256,2048]{1,0:T(8,128)(2,1)}, u32[]{:S(2)}) copy-start(bf16[256,2048]{1,0:T(8,128)(2,1)} %all-reduce.16.cloned.1.call-done) | copy-start | bytes 3145732
  1923.9 28.7 %copy-start.81 = (f32[256]{0:T(256)S(1)}, f32[256]{0:T(256)}, u32[]{:S(2)}) copy-start(f32[256]{0:T(256)} %copy-done.80) | copy-start | bytes 3076
  1923.9 28.7 %copy-start.89 = (f32[256]{0:T(256)S(1)}, f32[256]{0:T(256)}, u32[]{:S(2)}) copy-start(f32[256]{0:T(256)} %copy-done.88) | copy-start | bytes 3076
  (87 other events, 499.6 us)
Sparse Core Ops, SparseCore 0:
  9.9 125.2 all-gather.10
  139.6 45.9 all-gather.12
  187.7 44.6 all-gather.14
  234.1 51.2 all-gather.16
  356.1 18.1 all-reduce.13
  380.7 47.1 all-gather.22
  430.1 44.6 all-gather.24
  598.4 18.3 all-reduce.15
  618.6 158.5 all-gather.18
  778.9 157.2 all-gather.20
  1000.2 21.2 all-reduce.21
  1171.3 77.9 reduce-scatter.15
  1312.2 77.9 reduce-scatter.17
  1399.2 29.2 all-reduce.19
  1431.9 53.8 reduce-scatter.21
  1489.0 153.7 reduce-scatter.23
  1646.0 153.7 reduce-scatter.25
  1803.1 120.7 reduce-scatter.19
  1927.4 24.0 reduce-scatter.31
  1954.7 24.7 reduce-scatter.27
  1983.2 24.7 reduce-scatter.29
  2010.9 428.0 all-reduce.17
where the time goes:
time: 2480 us; the launch traced here: 2460 us
  waiting for transfers between devices  1460 us (59%)
  matrix products  597 us (24%)
  local copies, waits for them, and re-layouts  157 us (6%)
  other arithmetic  152 us (6%)
  blocking collectives  77.5 us (3%)
    psum x1, waiting for transfers between devices, per_device(): lax.psum(shard_sums[2].astype(jnp.bfloat16), 'context').astype(jnp.float32)  414 us
    dot_general x76, matrix products, product(): return jnp.dot(left_op, right_op, preferred_element_type=jnp.float32)  190 us
    all_gather x1, waiting for transfers between devices, per_device(): lax.all_gather(w_up, 'fsdp', axis=0, tiled=True)  158 us
    reduce_scatter x1, waiting for transfers between devices, per_device(): lax.psum_scatter(totals[8].astype(jnp.bfloat16), 'fsdp', scatter_dimensio...  157 us
    dot_general x64, matrix products, masked_scores(): jnp.einsum('qd,kd->qk', queries, key_rows, preferred_element_type=jnp.flo...  150 us
    all_gather x1, waiting for transfers between devices, per_device(): lax.all_gather(w_down, 'fsdp', axis=1, tiled=True)  138 us
    reduce_scatter x1, waiting for transfers between devices, per_device(): lax.psum_scatter(totals[2].astype(jnp.bfloat16), 'fsdp', scatter_dimensio...  124 us
    all_gather x1, waiting for transfers between devices, per_device(): lax.all_gather(w_qkv, 'fsdp', axis=1, tiled=True)  109 us
  transfers between devices with their start and end apart: 22, of which 17 were waited for; matrix products, arithmetic and copies ran while one was open for 21% of the time, Pallas kernels for 0%

commit v1 on v0

v1 whole, which is shorter than its diff:
```python
from functools import partial

import jax
import jax.numpy as jnp
from jax import lax
from jax.experimental import pallas as pl
from jax.experimental.pallas import tpu as pltpu
from jax.sharding import PartitionSpec as P

HEADS = 32
HEAD_DIM = 64
SEG = 128
TREE_SEGS = 8
LAST_DEPTH = 6
MICRO = 2
PAIR = 2 * HEAD_DIM
NEG_FILL = -1e30
F32 = jnp.float32
BF16 = jnp.bfloat16


def dot_nn(left, right):
    return lax.dot_general(left, right, (((1,), (0,)), ((), ())), preferred_element_type=F32)


def dot_tn(left, right):
    return lax.dot_general(left, right, (((0,), (0,)), ((), ())), preferred_element_type=F32)


def dot_nt(left, right):
    return lax.dot_general(left, right, (((1,), (1,)), ((), ())), preferred_element_type=F32)


def swap_cores(value):
    return lax.ppermute(value, "tensor", [(0, 1), (1, 0)])


def xor_send(value, step):
    size = lax.axis_size("fsdp")
    return lax.ppermute(value, "fsdp", [(i, i ^ step) for i in range(size)])


def ring_send(value, step):
    size = lax.axis_size("context")
    return lax.ppermute(value, "context", [(i, (i + step) % size) for i in range(size)])


def line_gather(value):
    size = lax.axis_size("context")
    index = lax.axis_index("context")
    upward, downward = [value], [value]
    for step in range(1, size):
        upward.append(
            lax.ppermute(upward[-1], "context", [(i, i + 1) for i in range(step - 1, size - 1)])
        )
        downward.append(
            lax.ppermute(downward[-1], "context", [(i + 1, i) for i in range(0, size - step)])
        )
    blocks = [value]
    for step in range(1, size):
        blocks.append(jnp.where(index + step < size, downward[step], upward[size - step]))
    return blocks


def gather_rows(value):
    return [value] + [xor_send(value, k) for k in range(1, lax.axis_size("fsdp"))]


def place(pieces, axis):
    index = lax.axis_index("fsdp")
    width = pieces[0].shape[axis]
    shape = list(pieces[0].shape)
    shape[axis] = width * len(pieces)
    whole = jnp.zeros(shape, pieces[0].dtype)
    for k, piece in enumerate(pieces):
        whole = lax.dynamic_update_slice_in_dim(whole, piece, (index ^ k) * width, axis)
    return whole


def pick(whole, k, axis):
    width = whole.shape[axis] // lax.axis_size("fsdp")
    return lax.dynamic_slice_in_dim(whole, (lax.axis_index("fsdp") ^ k) * width, width, axis)


def exchange(whole, axis):
    blocks = [pick(whole, 0, axis)]
    for k in range(1, lax.axis_size("fsdp")):
        blocks.append(xor_send(pick(whole, k, axis), k))
    return blocks


def sum_blocks(own, pieces):
    total = own.astype(F32)
    for k, piece in enumerate(pieces, 1):
        total = total + xor_send(piece.astype(BF16), k).astype(F32)
    return total


def head_lanes(rows):
    return lax.broadcasted_iota(jnp.int32, (rows, PAIR), 1) < HEAD_DIM


def split_heads(value):
    first = head_lanes(value.shape[0])
    zero = jnp.zeros_like(value)
    return jnp.concatenate([jnp.where(first, value, zero), jnp.where(first, zero, value)], axis=0)


def join_heads(stacked):
    first = head_lanes(SEG)
    return jnp.where(first, stacked[:SEG], stacked[SEG:])


def probabilities(stacked_queries, keys, block, slope_a, slope_b):
    width = (block + 1) * SEG
    scores = dot_nt(stacked_queries, keys)
    row = lax.broadcasted_iota(jnp.int32, (2 * SEG, 1), 0)
    column = lax.broadcasted_iota(jnp.int32, (1, width), 1)
    local = jnp.where(row < SEG, row, row - SEG)
    slope = jnp.where(row < SEG, slope_a, slope_b)
    place_row = local + min(block, LAST_DEPTH) * SEG
    place_column = jnp.where(column < (LAST_DEPTH + 1) * SEG, column, column - SEG)
    scores = scores + slope * (place_column - place_row).astype(F32)
    allowed = column <= local + block * SEG
    if block == LAST_DEPTH + 1:
        allowed = allowed & ((column < LAST_DEPTH * SEG) | (column >= (LAST_DEPTH + 1) * SEG))
    scores = jnp.where(allowed, scores, NEG_FILL)
    raised = jnp.exp(scores - jnp.max(scores, axis=-1, keepdims=True))
    return raised * (1.0 / jnp.sum(raised, axis=-1, keepdims=True))


def attention_forward(order, slopes, qkv_ref, out_ref, keys, values):
    pair = pl.program_id(0)
    slope_a, slope_b = slopes[2 * pair], slopes[2 * pair + 1]
    for block in range(TREE_SEGS):
        rows = pl.ds(block * SEG, SEG)
        keys[rows, :] = qkv_ref[order[block], :, PAIR : 2 * PAIR]
        values[rows, :] = qkv_ref[order[block], :, 2 * PAIR : 3 * PAIR]
    for block in range(TREE_SEGS):
        seen = pl.ds(0, (block + 1) * SEG)
        queries = split_heads(qkv_ref[order[block], :, :PAIR] * BF16(HEAD_DIM**-0.5))
        probs = probabilities(queries, keys[seen, :], block, slope_a, slope_b)
        mixed = dot_nn(probs.astype(BF16), values[seen, :])
        out_ref[order[block]] = join_heads(mixed).astype(BF16)


def attention_backward(order, slopes, qkv_ref, grad_ref, out_ref, keys, values, grad_keys, grad_values):
    pair = pl.program_id(0)
    slope_a, slope_b = slopes[2 * pair], slopes[2 * pair + 1]
    for block in range(TREE_SEGS):
        rows = pl.ds(block * SEG, SEG)
        keys[rows, :] = qkv_ref[order[block], :, PAIR : 2 * PAIR]
        values[rows, :] = qkv_ref[order[block], :, 2 * PAIR : 3 * PAIR]
    grad_keys[...] = jnp.zeros_like(grad_keys)
    grad_values[...] = jnp.zeros_like(grad_values)
    for block in range(TREE_SEGS):
        seen = pl.ds(0, (block + 1) * SEG)
        queries = split_heads(qkv_ref[order[block], :, :PAIR] * BF16(HEAD_DIM**-0.5))
        grads = split_heads(grad_ref[order[block]])
        probs = probabilities(queries, keys[seen, :], block, slope_a, slope_b)
        grad_probs = dot_nt(grads, values[seen, :])
        centre = jnp.sum(probs * grad_probs, axis=-1, keepdims=True)
        grad_scores = (probs * (grad_probs - centre)).astype(BF16)
        grad_queries = join_heads(dot_nn(grad_scores, keys[seen, :])) * HEAD_DIM**-0.5
        out_ref[order[block], :, :PAIR] = grad_queries.astype(BF16)
        grad_keys[seen, :] += dot_tn(grad_scores, queries)
        grad_values[seen, :] += dot_tn(probs.astype(BF16), grads)
    for block in range(TREE_SEGS):
        rows = pl.ds(block * SEG, SEG)
        out_ref[order[block], :, PAIR : 2 * PAIR] = grad_keys[rows, :].astype(BF16)
        out_ref[order[block], :, 2 * PAIR : 3 * PAIR] = grad_values[rows, :].astype(BF16)


def block_of(width):
    return pl.BlockSpec((TREE_SEGS, SEG, width), lambda pair, *scalars: (0, 0, pair))


def attend(order, slopes, qkv):
    pairs = qkv.shape[1] // (3 * PAIR)
    rows = TREE_SEGS * SEG
    out = pl.pallas_call(
        attention_forward,
        out_shape=jax.ShapeDtypeStruct((TREE_SEGS, SEG, pairs * PAIR), BF16),
        grid_spec=pltpu.PrefetchScalarGridSpec(
            num_scalar_prefetch=2,
            grid=(pairs,),
            in_specs=[block_of(3 * PAIR)],
            out_specs=block_of(PAIR),
            scratch_shapes=[pltpu.VMEM((rows, PAIR), BF16)] * 2,
        ),
        compiler_params=pltpu.CompilerParams(vmem_limit_bytes=48 << 20),
        cost_estimate=pl.CostEstimate(
            flops=pairs * 8 * rows * rows * PAIR,
            transcendentals=pairs * rows * rows,
            bytes_accessed=8 * rows * pairs * PAIR,
        ),
        name="attend",
    )(order, slopes, qkv.reshape(TREE_SEGS, SEG, -1))
    return out.reshape(rows, pairs * PAIR)


def attend_back(order, slopes, qkv, grad):
    pairs = qkv.shape[1] // (3 * PAIR)
    rows = TREE_SEGS * SEG
    out = pl.pallas_call(
        attention_backward,
        out_shape=jax.ShapeDtypeStruct((TREE_SEGS, SEG, pairs * 3 * PAIR), BF16),
        grid_spec=pltpu.PrefetchScalarGridSpec(
            num_scalar_prefetch=2,
            grid=(pairs,),
            in_specs=[block_of(3 * PAIR), block_of(PAIR)],
            out_specs=block_of(3 * PAIR),
            scratch_shapes=[pltpu.VMEM((rows, PAIR), BF16)] * 2 + [pltpu.VMEM((rows, PAIR), F32)] * 2,
        ),
        compiler_params=pltpu.CompilerParams(vmem_limit_bytes=48 << 20),
        cost_estimate=pl.CostEstimate(
            flops=pairs * 20 * rows * rows * PAIR,
            transcendentals=pairs * rows * rows,
            bytes_accessed=14 * rows * pairs * PAIR,
        ),
        name="attend_back",
    )(order, slopes, qkv.reshape(TREE_SEGS, SEG, -1), grad.reshape(TREE_SEGS, SEG, -1))
    return out.reshape(rows, pairs * 3 * PAIR)


def normalise(rows):
    centred = rows - jnp.mean(rows, axis=-1, keepdims=True)
    scale = lax.rsqrt(jnp.mean(centred * centred, axis=-1, keepdims=True) + 1e-05)
    return centred * scale, scale


def norm_back(unit, scale, gain, upstream):
    weighted = upstream * gain
    centre = jnp.mean(weighted, axis=-1, keepdims=True)
    along = jnp.mean(weighted * unit, axis=-1, keepdims=True)
    return scale * (weighted - centre - unit * along)


def normal_cdf(value):
    return 0.5 * (1.0 + lax.erf(value * 0.7071067811865476))


def normal_pdf(value):
    return 0.3989422804014327 * jnp.exp(-0.5 * value * value)


def both_micros(mine):
    other = swap_cores(mine)
    first = lax.axis_index("tensor") == 0
    return jnp.stack([jnp.where(first, mine, other), jnp.where(first, other, mine)])


def per_device(
    tokens,
    cotangent,
    seg_parent,
    positions,
    norm_gain,
    norm_bias,
    w_qkv,
    bias_qv,
    w_out,
    bias_out,
    w_up,
    bias_up,
    w_down,
    bias_down,
):
    planes, groups = lax.axis_size("context"), lax.axis_size("fsdp")
    plane, group, core = (lax.axis_index(name) for name in ("context", "fsdp", "tensor"))
    rows, width = tokens.shape[1], tokens.shape[2]
    part = width // groups
    half = w_qkv.shape[2]
    columns = half // planes
    pairs = columns // PAIR
    hidden = w_up.shape[1] // groups
    slots = rows // SEG

    mine = lax.dynamic_index_in_dim(tokens, core, 0, keepdims=False)
    mine_cot = lax.dynamic_index_in_dim(cotangent, core, 0, keepdims=False)
    tree = jnp.concatenate(line_gather(mine), axis=0)

    packed = jnp.concatenate(
        [
            norm_gain,
            norm_bias,
            bias_out[None],
            bias_down[None],
            bias_qv.reshape(1, part),
            bias_up.reshape(-1, part),
        ],
        axis=0,
    )
    small = lax.all_gather(packed, ("tensor", "fsdp"), axis=0, tiled=False).astype(F32)
    small = small.reshape(2, groups, packed.shape[0], part)
    spread = lax.dynamic_index_in_dim(small, core, 0, keepdims=False)[:, :6]
    spread = spread.transpose(1, 0, 2).reshape(6, width)
    gain_one, gain_two, shift_one, shift_two, out_shift, down_shift = (
        spread[i : i + 1] for i in range(6)
    )
    head_shift = small[:, :, 6].reshape(2, groups, 2, part // 2).transpose(0, 2, 1, 3)
    head_shift = lax.dynamic_slice_in_dim(
        head_shift.reshape(2, 2, half), plane * columns, columns, 2
    ).reshape(2, 2, pairs, PAIR)
    head_shift = jnp.stack(
        [head_shift[:, 0], jnp.zeros_like(head_shift[:, 0]), head_shift[:, 1]], axis=2
    ).reshape(2, pairs * 3 * PAIR)
    up_shift = lax.dynamic_index_in_dim(small, group, 1, keepdims=False)[:, 7:].reshape(2, hidden)

    def own_first(both):
        return jnp.where(core == 0, both, both[::-1])

    head_shift = own_first(head_shift).reshape(1, -1)
    up_shift = own_first(up_shift)

    chosen = lax.dynamic_slice_in_dim(w_qkv, plane * columns, columns, 2)
    chosen = chosen.reshape(3, part, pairs, PAIR).transpose(1, 2, 0, 3).reshape(part, 3 * columns)
    heads_own = lax.all_gather(chosen, "fsdp", axis=0, tiled=True)
    w_heads = jnp.concatenate([heads_own, swap_cores(heads_own)], axis=1)
    out_own = lax.all_gather(w_out, "fsdp", axis=1, tiled=True)
    out_other = swap_cores(out_own)

    up_own = place(exchange(w_up, 1), 0)
    down_own = place(exchange(w_down, 0), 1)
    up_other, down_other = swap_cores(up_own), swap_cores(down_own)
    all_cot = jnp.concatenate(gather_rows(mine_cot), axis=0)

    depth = lax.dynamic_index_in_dim(positions, core, 0, keepdims=False)[::SEG] // SEG
    depth = jnp.roll(depth, -plane * slots)
    ids = jnp.arange(TREE_SEGS, dtype=jnp.int32)
    before = (depth[None, :] < depth[:, None]) | (
        (depth[None, :] == depth[:, None]) & (ids[None, :] < ids[:, None])
    )
    rank = jnp.sum(before.astype(jnp.int32), axis=1)
    order = jnp.sum(jnp.where(rank[None, :] == ids[:, None], ids[None, :], 0), axis=1)
    local_heads = columns // HEAD_DIM
    head_ids = plane * local_heads + jnp.arange(local_heads, dtype=jnp.int32)
    own_ids = core * (half // HEAD_DIM) + head_ids
    other_ids = (1 - core) * (half // HEAD_DIM) + head_ids
    slopes = jnp.exp2(-8.0 * (jnp.concatenate([own_ids, other_ids]) + 1).astype(F32) / HEADS)

    tree_unit, _ = normalise(tree.astype(F32))
    normed = (tree_unit * gain_one + shift_one).astype(BF16)
    qkv = (dot_nn(normed, w_heads) + head_shift).astype(BF16)
    mixed = attend(order, slopes, qkv)
    arrived = [mixed[:rows]]
    for k in range(1, planes):
        arrived.append(ring_send(mixed[k * rows : (k + 1) * rows], k))
    attended = jnp.stack(arrived[::-1], axis=0)
    attended = jnp.roll(attended, plane + 1, axis=0)
    attended = attended.reshape(planes, rows, 2, columns).transpose(2, 1, 0, 3)
    attended = attended.reshape(2, rows, half)
    middle = mine.astype(F32) + (
        dot_nn(attended[0], out_own) + dot_nn(attended[1], out_other) + out_shift
    )
    unit_two, scale_two = normalise(middle)
    normed_two = (unit_two * gain_two + shift_two).astype(BF16)
    all_two = jnp.concatenate(gather_rows(normed_two), axis=0)

    def unit(w_up_half, w_down_half, shift):
        pre = dot_nn(all_two, w_up_half) + shift
        below = normal_cdf(pre)
        active = (pre * below).astype(BF16)
        back = dot_nt(all_cot, w_down_half) * (below + pre * normal_pdf(pre))
        return active, back.astype(BF16)

    active_own, back_own = unit(up_own, down_own, up_shift[0:1])
    active_other, back_other = unit(up_other, down_other, up_shift[1:2])

    grad_two = dot_nt(back_own, up_own) + dot_nt(back_other, up_other)
    blocks = [grad_two[k * rows : (k + 1) * rows] for k in range(groups)]
    grad_two = sum_blocks(blocks[0], blocks[1:])
    grad_middle = mine_cot.astype(F32) + norm_back(unit_two, scale_two, gain_two, grad_two)
    grad_branch = grad_middle.astype(BF16)
    grad_mixed = jnp.stack(
        [
            dot_nt(grad_branch, out_own).astype(BF16).reshape(rows, planes, columns),
            dot_nt(grad_branch, out_other).astype(BF16).reshape(rows, planes, columns),
        ],
        axis=1,
    )
    grad_mixed = grad_mixed.transpose(2, 0, 1, 3).reshape(planes, rows, 2 * columns)
    grad_mixed = jnp.roll(grad_mixed, -plane, axis=0)
    back_rows = [grad_mixed[0]]
    for k in range(1, planes):
        back_rows.append(ring_send(grad_mixed[k], k))
    grad_tree = jnp.concatenate(back_rows[:1] + back_rows[:0:-1], axis=0)

    layer_out = dot_nn(active_own, down_own) + dot_nn(active_other, down_other)
    blocks = [layer_out[k * rows : (k + 1) * rows] for k in range(groups)]
    layer_out = middle + (sum_blocks(blocks[0], blocks[1:]) + down_shift)
    layer_out = both_micros(layer_out.astype(BF16))

    grad_down = swap_cores(dot_tn(active_other, all_cot).astype(BF16))
    grad_down = (dot_tn(active_own, all_cot) + grad_down.astype(F32)).astype(BF16)
    grad_down = lax.psum_scatter(grad_down, "context", scatter_dimension=0, tiled=True)
    grad_down = place([piece[None] for piece in exchange(grad_down, 1)], 0)
    grad_up = swap_cores(dot_tn(all_two, back_other).astype(BF16))
    grad_up = (dot_tn(all_two, back_own) + grad_up.astype(F32)).astype(BF16)
    grad_up = grad_up.reshape(groups, planes, part // planes, hidden).transpose(1, 0, 2, 3)
    grad_up = lax.psum_scatter(grad_up, "context", scatter_dimension=0, tiled=True)[0]
    grad_up = exchange(grad_up, 0)
    grad_up = place([piece[0] for piece in grad_up], 1)
    g_down = lax.all_gather(grad_down, "context", axis=1, tiled=False)
    g_up = lax.all_gather(grad_up, "context", axis=0, tiled=True)

    grad_out = swap_cores(dot_tn(attended[1], grad_branch).astype(BF16))
    grad_out = dot_tn(attended[0], grad_branch) + grad_out.astype(F32)
    grad_out = sum_blocks(
        pick(grad_out, 0, 1), [pick(grad_out, k, 1) for k in range(1, groups)]
    )
    g_out = lax.psum(grad_out.astype(BF16), "context")

    grad_qkv = attend_back(order, slopes, qkv, grad_tree)
    grad_normed = dot_nt(grad_qkv, w_heads)
    grad_first = [grad_normed[:rows]]
    for k in range(1, planes):
        sent = grad_normed[k * rows : (k + 1) * rows].astype(BF16)
        grad_first.append(ring_send(sent, k).astype(F32))
    grad_first = sum(grad_first[1:], grad_first[0])
    unit_one, scale_one = normalise(mine.astype(F32))
    grad_tokens = grad_middle + norm_back(unit_one, scale_one, gain_one, grad_first)
    grad_tokens = both_micros(grad_tokens.astype(BF16))

    grad_heads = dot_tn(normed, grad_qkv)
    grad_other = swap_cores(grad_heads[:, 3 * columns :].astype(BF16))
    grad_heads = grad_heads[:, : 3 * columns] + grad_other.astype(F32)
    grad_heads = sum_blocks(
        pick(grad_heads, 0, 0), [pick(grad_heads, k, 0) for k in range(1, groups)]
    ).astype(BF16)
    g_heads = lax.all_gather(grad_heads, "context", axis=0, tiled=False)

    head_sums = jnp.sum(grad_qkv.astype(F32), axis=0).reshape(2, pairs, 3, PAIR)
    head_sums = jnp.stack([head_sums[:, :, 0], head_sums[:, :, 2]], axis=1)
    head_sums = own_first(head_sums.reshape(2, 2, columns)).transpose(1, 0, 2)
    head_row = lax.dynamic_update_slice_in_dim(
        jnp.zeros((2, 2, half), F32), head_sums, plane * columns, 2
    )
    up_sums = own_first(
        jnp.stack([jnp.sum(side.astype(F32), axis=0) for side in (back_own, back_other)])
    )
    up_row = lax.dynamic_update_slice_in_dim(
        jnp.zeros((2, groups * hidden), F32), up_sums, group * hidden, 1
    )
    vectors = jnp.concatenate(
        [
            jnp.sum(grad_normed * tree_unit, axis=0),
            jnp.sum(grad_two * unit_two, axis=0),
            jnp.sum(grad_normed, axis=0),
            jnp.sum(grad_two, axis=0),
            jnp.sum(grad_branch.astype(F32), axis=0),
            jnp.sum(mine_cot.astype(F32), axis=0),
            head_row.reshape(-1),
            up_row.reshape(-1),
        ]
    )
    vectors = lax.psum(vectors, ("fsdp", "context", "tensor")).reshape(-1, width)

    def share(whole):
        return lax.dynamic_slice_in_dim(whole, group * part, part, whole.ndim - 1)

    g_gain = share(vectors[0:2])
    g_shift = share(vectors[2:4])
    g_out_shift = share(vectors[4])
    g_down_shift = share(vectors[5])
    g_qv = lax.dynamic_slice_in_dim(
        vectors[6:8], (core * groups + group) * (part // 2), part // 2, 1
    )
    g_up_shift = lax.dynamic_slice_in_dim(
        vectors[8:].reshape(-1), (core * groups + group) * hidden, hidden, 0
    )
    g_heads = g_heads.reshape(planes, part, pairs, 3, PAIR).transpose(3, 1, 0, 2, 4)
    return (
        layer_out,
        grad_tokens,
        g_gain,
        g_shift,
        g_heads.reshape(3, part, half).astype(F32),
        g_qv,
        g_out.astype(F32),
        g_out_shift,
        g_up.astype(F32),
        g_up_shift,
        g_down.reshape(groups * hidden, part).astype(F32),
        g_down_shift,
    )


def solution(mesh):
    rows = P(None, ("fsdp", "context"), None)
    params = (
        P(None, "fsdp"),
        P(None, "fsdp"),
        P(None, "fsdp", "tensor"),
        P(None, ("tensor", "fsdp")),
        P("tensor", "fsdp"),
        P("fsdp"),
        P("fsdp", "tensor"),
        P(("tensor", "fsdp")),
        P("tensor", "fsdp"),
        P("fsdp"),
    )
    in_specs = (rows, rows, P(None, "fsdp"), P(None, "fsdp")) + params
    return jax.shard_map(
        per_device, mesh=mesh, in_specs=in_specs, out_specs=(rows, rows) + params, check_vma=False
    )
```

time: 2480 us -> 1300 us (0.52)
  waiting for transfers between devices: 1460 us -> 751 us
  matrix products: 597 us -> 167 us
  other arithmetic: 152 us -> 54.8 us
  starting transfers between devices: 1.48 us -> 77 us
  local copies, waits for them, and re-layouts: 157 us -> 94 us
  Pallas kernels: 0 us -> 46.7 us
    dot_general x212 -> x21, matrix products: 597 us -> 167 us  [the longest x7 64.3 us: dot_nt(): lax.dot_general(left, right, (((1,), (1,)), ((), ())), preferred_element_...]
    all_gather x8 -> x5, waiting for transfers between devices: 544 us -> 185 us  [the longest x1 74.2 us: per_device(): g_down = lax.all_gather(grad_down, 'context', axis=1, tiled=False)]
    reduce_scatter x6 -> x1, waiting for transfers between devices: 413 us -> 60.7 us  [per_device(): lax.psum_scatter(grad_down, 'context', scatter_dimension=0, tiled=True)]
    ppermute x0 -> x55, waiting for transfers between devices: none -> 290 us  [the longest x30 231 us: xor_send(): return lax.ppermute(value, 'fsdp', [(i, i ^ step) for i in range(size)])]
    psum x5 -> x2, waiting for transfers between devices: 454 us -> 215 us  [the longest x1 161 us: per_device(): lax.psum(vectors, ('fsdp', 'context', 'tensor')).reshape(-1, width)]
    ppermute x0 -> x55, starting transfers between devices: none -> 76.7 us  [the longest x30 32.4 us: xor_send(): return lax.ppermute(value, 'fsdp', [(i, i ^ step) for i in range(size)])]
    dynamic_update_slice x64 -> x2, other arithmetic: 65.4 us -> 0.04 us  [the longest x1 0.03 us: per_device(): lax.dynamic_update_slice_in_dim(jnp.zeros((2, groups * hidden), F32), up_...]
    dynamic_slice x99 -> x13, local copies, waits for them, and re-layouts: 60 us -> 10 us  [the longest x4 5.86 us: pick(): lax.dynamic_slice_in_dim(whole, (lax.axis_index('fsdp') ^ k) * width, wid...]
  transfers between devices with their start and end apart: 22 -> 63, of which waited for: 17 -> 29; matrix products, arithmetic and copies ran while one was open for 21% -> 19% of each run, Pallas kernels for 0% -> 4%
where the time goes in v1:
time: 1300 us; the launch traced here: 1290 us
  waiting for transfers between devices  751 us (58%)
  matrix products  167 us (13%)
  local copies, waits for them, and re-layouts  94 us (7%)
  blocking collectives  80 us (6%)
  starting transfers between devices  77 us (6%)
  other arithmetic  54.8 us (4%)
  Pallas kernels  46.7 us (4%)
  between operations  16.8 us (1%)
    ppermute x30, waiting for transfers between devices, xor_send(): return lax.ppermute(value, 'fsdp', [(i, i ^ step) for i in range(size)])  231 us
    psum x1, waiting for transfers between devices, per_device(): lax.psum(vectors, ('fsdp', 'context', 'tensor')).reshape(-1, width)  161 us
    all_gather x1, blocking collectives, per_device(): lax.all_gather(packed, ('tensor', 'fsdp'), axis=0, tiled=False).astype(F32)  80 us
    all_gather x1, waiting for transfers between devices, per_device(): g_down = lax.all_gather(grad_down, 'context', axis=1, tiled=False)  74.2 us
    dot_general x7, matrix products, dot_nt(): lax.dot_general(left, right, (((1,), (1,)), ((), ())), preferred_element_...  64.3 us
    reduce_scatter x1, waiting for transfers between devices, per_device(): lax.psum_scatter(grad_down, 'context', scatter_dimension=0, tiled=True)  60.7 us
    dot_general x7, matrix products, dot_nn(): lax.dot_general(left, right, (((1,), (0,)), ((), ())), preferred_element_...  55.3 us
    psum x1, waiting for transfers between devices, per_device(): g_out = lax.psum(grad_out.astype(BF16), 'context')  54.1 us
  transfers between devices with their start and end apart: 63, of which 29 were waited for; matrix products, arithmetic and copies ran while one was open for 19% of the time, Pallas kernels for 4%

profile of v1, /device:TPU:0, one launch (start us, length us, event | category | flops | bytes accessed | tf_op | source)
XLA Modules:
  0.0 1287.9 jit_solution(9060658790248047123)
XLA Ops:
  15.8 6.5 collective-permute-start.1
  36.3 80.0 %all-gather.2 = bf16[8,9,512]{2,1,0:T(8,128)(2,1)S(1)} all-gather(bf16[1,9,512]{2,1,0:T(8,128)(2,1)S(1)} %bitcast.188), channel_id=2, replica_groups=mesh['fsdp'=4,'context'=4,'tensor'=2] {'tensor','fsdp'}, dimensions={0}, use_global_device_ids=true | all-gather | bytes 82944 | tf_op jit(solution)/shard_map/all_gather | solution.py:294
  122.1 22.1 %collective-permute-done.4 = bf16[256,2048]{1,0:T(8,128)(2,1)} collective-permute-done((bf16[256,2048]{1,0:T(8,128)(2,1)}, bf16[256,2048]{1,0:T(8,128)(2,1)}, u32[]{:S(2)}, u32[]{:S(2)}) %collective-permute-start.4) | collective-permute-done | bytes 1048608 | tf_op jit(solution)/shard_map/ppermute | solution.py:57
  153.6 9.0 collective-permute-done.16
  179.8 6.7 all-gather.11.cloned.1.call-done
  190.7 13.4 %add_convert_fusion.2 = bf16[1024,1536]{1,0:T(8,128)(2,1)S(1)} fusion(bf16[2048,1536]{0,1:T(8,128)(2,1)} %constant_dynamic-update-slice_fusion.8, f32[1536]{0:T(1024)S(1)} %add.358, f32[2048]{0:T(1024)S(1)} %bitcast.203, f32[2048]{0:T(1024)S(1)} %bitcast.191, f32[1024]{0:T(1024)S(1)} %add_rsqrt_fusion, f32[1024]{0:T(1024)S(1)} %broadcast_multiply_fusion, ...), kind=kOutput, calls=%fused_computation.18 | convolution fusion | flops 6472859648 | bytes 13662208 | tf_op jit(solution)/shard_map/dot_general | solution.py:23
  204.2 17.9 %attend.1 = bf16[8,128,512]{2,1,0:T(8,128)(2,1)S(1)} custom-call(s32[8]{0:T(128)S(1)} %select_reduce_fusion.order, f32[8]{0:T(128)S(1)} %fusion.56.slopes, bf16[8,128,1536]{2,1,0:T(8,128)(2,1)S(1)} %bitcast.160), custom_call_target="tpu_custom_call" | custom-call | flops 4294967296 | bytes 4194304 | tf_op jit(solution)/shard_map/attend/pallas_call | solution.py:181
  222.3 16.6 %collective-permute-start.7 = (bf16[256,512]{0,1:T(8,128)(2,1)S(1)}, bf16[256,512]{0,1:T(8,128)(2,1)S(1)}, u32[]{:S(2)}, u32[]{:S(2)}) collective-permute-start(bf16[256,512]{0,1:T(8,128)(2,1)S(1)} %copy.62), channel_id=1, source_target_pairs={{0,6},{2,0},{4,2},{6,4},{1,7},{3,1},{5,3},{7,5},{8,14},{10,8},{12,... | collective-permute-start | bytes 786440 | tf_op jit(solution)/shard_map/ppermute | solution.py:45
  245.6 15.0 %collective-permute-done.8 = bf16[256,512]{0,1:T(8,128)(2,1)S(1)} collective-permute-done((bf16[256,512]{0,1:T(8,128)(2,1)S(1)}, bf16[256,512]{0,1:T(8,128)(2,1)S(1)}, u32[]{:S(2)}, u32[]{:S(2)}) %collective-permute-start.8) | collective-permute-done | bytes 262176 | tf_op jit(solution)/shard_map/ppermute | solution.py:45
  274.3 20.7 %collective-permute-done.13 = bf16[256,2048]{1,0:T(8,128)(2,1)} collective-permute-done((bf16[256,2048]{1,0:T(8,128)(2,1)S(1)}, bf16[256,2048]{1,0:T(8,128)(2,1)}, u32[]{:S(2)}, u32[]{:S(2)}) %collective-permute-start.13) | collective-permute-done | bytes 1048608 | tf_op jit(solution)/shard_map/ppermute | solution.py:40
  295.0 42.7 %collective-permute-done.12 = bf16[256,2048]{1,0:T(8,128)(2,1)} collective-permute-done((bf16[256,2048]{1,0:T(8,128)(2,1)S(1)}, bf16[256,2048]{1,0:T(8,128)(2,1)}, u32[]{:S(2)}, u32[]{:S(2)}) %collective-permute-start.12) | collective-permute-done | bytes 1048608 | tf_op jit(solution)/shard_map/ppermute | solution.py:40
  337.8 9.9 multiply_convert_fusion
  347.6 8.4 fusion.61
  360.4 8.7 convert_reduce_fusion.2
  369.2 10.0 fusion.80
  379.2 12.4 convert_reduce_fusion.3
  391.7 9.6 fusion.76
  405.1 8.9 fusion.79
  414.0 9.8 fusion.77
  429.2 22.0 %collective-permute-done.30 = bf16[256,2048]{1,0:T(8,128)(2,1)S(1)} collective-permute-done((bf16[256,2048]{1,0:T(8,128)(2,1)S(1)}, bf16[256,2048]{1,0:T(8,128)(2,1)S(1)}, u32[]{:S(2)}, u32[]{:S(2)}) %collective-permute-start.30) | collective-permute-done | bytes 1048608 | tf_op jit(solution)/shard_map/ppermute | solution.py:40
  454.1 19.5 %collective-permute-done.24 = bf16[256,2048]{1,0:T(8,128)(2,1)S(1)} collective-permute-done((bf16[256,2048]{1,0:T(8,128)(2,1)S(1)}, bf16[256,2048]{1,0:T(8,128)(2,1)S(1)}, u32[]{:S(2)}, u32[]{:S(2)}) %collective-permute-start.24) | collective-permute-done | bytes 1048608 | tf_op jit(solution)/shard_map/ppermute | solution.py:40
  473.6 20.7 %collective-permute-done.23 = bf16[256,2048]{1,0:T(8,128)(2,1)S(1)} collective-permute-done((bf16[256,2048]{1,0:T(8,128)(2,1)S(1)}, bf16[256,2048]{1,0:T(8,128)(2,1)S(1)}, u32[]{:S(2)}, u32[]{:S(2)}) %collective-permute-start.23) | collective-permute-done | bytes 1048608 | tf_op jit(solution)/shard_map/ppermute | solution.py:40
  500.4 8.8 convolution_convert_fusion.2
  509.2 6.6 convolution_convert_fusion.1
  521.7 9.2 add_convert_fusion.1
  531.0 14.2 %collective-permute-done.46 = bf16[1024,512]{1,0:T(8,128)(2,1)S(1)} collective-permute-done((bf16[1024,512]{1,0:T(8,128)(2,1)S(1)}, bf16[1024,512]{1,0:T(8,128)(2,1)S(1)}, u32[]{:S(2)}, u32[]{:S(2)}) %collective-permute-start.46) | collective-permute-done | bytes 1048608 | tf_op jit(solution)/shard_map/ppermute | solution.py:40
  545.2 21.5 %collective-permute-done.45 = bf16[1024,512]{1,0:T(8,128)(2,1)S(1)} collective-permute-done((bf16[1024,512]{1,0:T(8,128)(2,1)S(1)}, bf16[1024,512]{1,0:T(8,128)(2,1)S(1)}, u32[]{:S(2)}, u32[]{:S(2)}) %collective-permute-start.45) | collective-permute-done | bytes 1048608 | tf_op jit(solution)/shard_map/ppermute | solution.py:40
  587.3 10.2 add_convert_fusion
  597.6 17.4 %collective-permute-done.33 = bf16[256,512]{1,0:T(8,128)(2,1)S(1)} collective-permute-done((bf16[256,512]{1,0:T(8,128)(2,1)S(1)}, bf16[256,512]{1,0:T(8,128)(2,1)S(1)}, u32[]{:S(2)}, u32[]{:S(2)}) %collective-permute-start.33) | collective-permute-done | bytes 262176 | tf_op jit(solution)/shard_map/ppermute | solution.py:45
  616.4 28.8 %attend_back.1 = bf16[8,128,1536]{2,1,0:T(8,128)(2,1)S(1)} custom-call(s32[8]{0:T(128)S(1)} %copy-done.6, f32[8]{0:T(128)S(1)} %copy-done.4, bf16[8,128,1536]{2,1,0:T(8,128)(2,1)} %bitcast.161, bf16[8,128,512]{2,1,0:T(8,128)(2,1)S(1)} %bitcast.159), custom_call_target="tpu_custom_call" | custom-call | flops 10737418240 | bytes 7340032 | tf_op jit(solution)/shard_map/attend_back/pallas_call | solution.py:205
  645.3 10.4 fusion.57
  661.2 16.2 %fusion.62 = (f32[2048]{0:T(1024)S(1)}, f32[2048]{0:T(1024)S(1)}, bf16[1024,2048]{1,0:T(8,128)(2,1)}, f32[1024,2048]{1,0:T(8,128)}) fusion(f32[1024]{0:T(1024)S(1)} %copy-done.49, f32[1024]{0:T(1024)S(1)} %copy-done.44, bf16[256,2048]{1,0:T(8,128)(2,1)} %copy-done.15, bf16[256,2048]{1,0:T(8,128)(2,1)} %copy-done.13, bf16[256,2048]{1,0:T(8,128)(2,1)} %copy-done.18, ...), kind=kOutput, calls=%fused_computation.222 | convolution fusion | flops 6471806976 | bytes 26238976 | tf_op jit(solution)/shard_map/dot_general | solution.py:31
  688.6 17.2 %collective-permute-done.42 = bf16[512,768]{1,0:T(8,128)(2,1)S(1)} collective-permute-done((bf16[512,768]{1,0:T(8,128)(2,1)}, bf16[512,768]{1,0:T(8,128)(2,1)S(1)}, u32[]{:S(2)}, u32[]{:S(2)}) %collective-permute-start.42) | collective-permute-done | bytes 786464 | tf_op jit(solution)/shard_map/ppermute | solution.py:40
  705.8 16.5 %collective-permute-done.41 = bf16[512,768]{1,0:T(8,128)(2,1)S(1)} collective-permute-done((bf16[512,768]{1,0:T(8,128)(2,1)}, bf16[512,768]{1,0:T(8,128)(2,1)S(1)}, u32[]{:S(2)}, u32[]{:S(2)}) %collective-permute-start.41) | collective-permute-done | bytes 786464 | tf_op jit(solution)/shard_map/ppermute | solution.py:40
  726.4 54.1 %all-reduce.7.cloned.1.call-done = (bf16[1024,512]{1,0:T(8,128)(2,1)}, bf16[4,4,128,1024]{3,2,0,1:T(8,128)(2,1)}) async-done(((bf16[1024,512]{1,0:T(8,128)(2,1)}, bf16[4,4,128,1024]{3,2,0,1:T(8,128)(2,1)}), (bf16[1024,512]{1,0:T(8,128)(2,1)}, bf16[4,4,128,1024]{3,2,0,1:T(8,128)(2,1)})) %all-reduce.7.cloned.1.call-update) | async-done | bytes 5242896 | tf_op jit(solution)/shard_map/psum | solution.py:412
  790.9 5.6 collective-permute-done.49
  797.7 60.7 %reduce-scatter.5.cloned.1.call-done = bf16[256,2048]{1,0:T(8,128)(2,1)} async-done(((bf16[1024,2048]{1,0:T(8,128)(2,1)}), bf16[256,2048]{1,0:T(8,128)(2,1)}) %reduce-scatter.5.cloned.1.call-update) | async-done | bytes 1048592 | tf_op jit(solution)/shard_map/reduce_scatter | solution.py:396
  868.9 5.7 collective-permute-done.53
  884.8 161.3 %all-reduce.5.cloned.1.call-done = f32[24576]{0:T(1024)} async-done(((f32[24576]{0:T(1024)}), f32[24576]{0:T(1024)}) %all-reduce.5.cloned.1.call-update) | async-done | bytes 98320 | tf_op jit(solution)/shard_map/psum | solution.py:457
  1059.5 52.6 %all-gather.17.cloned.1.call-done = bf16[2048,768]{1,0:T(8,128)(2,1)} async-done(((bf16[512,768]{1,0:T(8,128)(2,1)}), bf16[2048,768]{1,0:T(8,128)(2,1)}) %all-gather.17.cloned.1.call-update) | async-done | bytes 3145744 | tf_op jit(solution)/shard_map/all_gather | solution.py:431
  1112.1 5.5 copy.67
  1117.6 8.5 reshape.255
  1126.1 7.4 copy.68
  1133.5 6.7 copy.69
  1141.8 51.3 %all-gather.13.cloned.1.call-done = bf16[512,4096]{1,0:T(8,128)(2,1)} async-done(((bf16[128,4096]{1,0:T(8,128)(2,1)}), bf16[512,4096]{1,0:T(8,128)(2,1)}) %all-gather.13.cloned.1.call-update) | async-done | bytes 4194320 | tf_op jit(solution)/shard_map/all_gather | solution.py:405
  1193.1 6.8 convert_element_type.252
  1200.0 74.2 %all-gather.15.cloned.1.call-done = bf16[4,4,256,512]{3,2,1,0:T(8,128)(2,1)} async-done(((bf16[4,1,256,512]{3,2,1,0:T(8,128)(2,1)}), bf16[4,4,256,512]{3,2,1,0:T(8,128)(2,1)}) %all-gather.15.cloned.1.call-update) | async-done | bytes 4194320 | tf_op jit(solution)/shard_map/all_gather | solution.py:404
  1274.1 6.8 bitcast_convert_fusion
  (419 shorter events, 196.3 us)
Async XLA Ops:
  7.2 159.6 %all-gather.9.cloned.1.call-start = ((), (), s32[]{:S(2)}) async-start(), calls=%async_computation.1 | async-start | bytes 3932160 | tf_op jit(solution)/shard_map/all_gather | solution.py:318
  12.5 174.1 %all-gather.11.cloned.1.call-start = ((), (), s32[]{:S(2)}) async-start(), calls=%async_computation.2 | async-start | bytes 5242880 | tf_op jit(solution)/shard_map/all_gather | solution.py:320
  14.5 102.6 %collective-permute-start = (bf16[256,2048]{1,0:T(8,128)(2,1)S(1)}, bf16[256,2048]{1,0:T(8,128)(2,1)}, u32[]{:S(2)}, u32[]{:S(2)}) collective-permute-start(bf16[256,2048]{1,0:T(8,128)(2,1)S(1)} %get-tuple-element.68), channel_id=1, source_target_pairs={{2,0},{4,2},{6,4},{3,1},{5,3},{7,5},{10,8},{12,10},{14,12},{11,9},... | collective-permute-start | bytes 3145736 | tf_op jit(solution)/shard_map/ppermute | solution.py:57
  15.8 103.0 %collective-permute-start.1 = (bf16[256,2048]{1,0:T(8,128)(2,1)S(1)}, bf16[256,2048]{1,0:T(8,128)(2,1)}, u32[]{:S(2)}, u32[]{:S(2)}) collective-permute-start(bf16[256,2048]{1,0:T(8,128)(2,1)S(1)} %get-tuple-element.68), channel_id=1, source_target_pairs={{0,2},{2,4},{4,6},{1,3},{3,5},{5,7},{8,10},{10,12},{12,14},{9,11},... | collective-permute-start | bytes 3145736 | tf_op jit(solution)/shard_map/ppermute | solution.py:54
  26.6 93.6 %collective-permute-start.14 = (bf16[512,1024]{1,0:T(8,128)(2,1)}, bf16[512,1024]{1,0:T(8,128)(2,1)}, u32[]{:S(2)}, u32[]{:S(2)}) collective-permute-start(bf16[512,1024]{1,0:T(8,128)(2,1)} %get-tuple-element.94), channel_id=1, source_target_pairs={{0,8},{8,0},{16,24},{24,16},{1,9},{9,1},{17,25},{25,17},{2,10},{10... | collective-permute-start | bytes 3145736 | tf_op jit(solution)/shard_map/ppermute | solution.py:40
  28.5 121.5 %collective-permute-start.15 = (bf16[512,1024]{1,0:T(8,128)(2,1)}, bf16[512,1024]{1,0:T(8,128)(2,1)}, u32[]{:S(2)}, u32[]{:S(2)}) collective-permute-start(bf16[512,1024]{1,0:T(8,128)(2,1)} %get-tuple-element.96), channel_id=1, source_target_pairs={{0,16},{8,24},{16,0},{24,8},{1,17},{9,25},{17,1},{25,9},{2,18},{10... | collective-permute-start | bytes 3145736 | tf_op jit(solution)/shard_map/ppermute | solution.py:40
  34.4 113.3 %collective-permute-start.17 = (bf16[1024,512]{1,0:T(8,128)(2,1)}, bf16[1024,512]{1,0:T(8,128)(2,1)}, u32[]{:S(2)}, u32[]{:S(2)}) collective-permute-start(bf16[1024,512]{1,0:T(8,128)(2,1)} %get-tuple-element.90), channel_id=1, source_target_pairs={{0,8},{8,0},{16,24},{24,16},{1,9},{9,1},{17,25},{25,17},{2,10},{10... | collective-permute-start | bytes 3145736 | tf_op jit(solution)/shard_map/ppermute | solution.py:40
  36.0 744.5 %all-reduce.7.cloned.1.call-start = ((), (), s32[]{:S(2)}) async-start(), calls=%async_computation.8 | async-start | bytes 10485760 | tf_op jit(solution)/shard_map/psum | solution.py:412
  117.1 27.0 %collective-permute-start.4 = (bf16[256,2048]{1,0:T(8,128)(2,1)}, bf16[256,2048]{1,0:T(8,128)(2,1)}, u32[]{:S(2)}, u32[]{:S(2)}) collective-permute-start(bf16[256,2048]{1,0:T(8,128)(2,1)} %collective-permute-done), channel_id=1, source_target_pairs={{2,0},{4,2},{3,1},{5,3},{10,8},{12,10},{11,9},{13,11},{18,16},{20,... | collective-permute-start | bytes 3145736 | tf_op jit(solution)/shard_map/ppermute | solution.py:57
  118.8 43.9 %collective-permute-start.16 = (bf16[512,1024]{1,0:T(8,128)(2,1)S(1)}, bf16[512,1024]{1,0:T(8,128)(2,1)}, u32[]{:S(2)}, u32[]{:S(2)}) collective-permute-start(bf16[512,1024]{1,0:T(8,128)(2,1)S(1)} %get-tuple-element.93), channel_id=1, source_target_pairs={{0,24},{8,16},{16,8},{24,0},{1,25},{9,17},{17,9},{25,1},{2,26},{10... | collective-permute-start | bytes 3145736 | tf_op jit(solution)/shard_map/ppermute | solution.py:40
  120.1 44.8 %collective-permute-start.2 = (bf16[256,2048]{1,0:T(8,128)(2,1)}, bf16[256,2048]{1,0:T(8,128)(2,1)}, u32[]{:S(2)}, u32[]{:S(2)}) collective-permute-start(bf16[256,2048]{1,0:T(8,128)(2,1)} %collective-permute-done.1), channel_id=1, source_target_pairs={{2,4},{4,6},{3,5},{5,7},{10,12},{12,14},{11,13},{13,15},{18,20},{2... | collective-permute-start | bytes 3145736 | tf_op jit(solution)/shard_map/ppermute | solution.py:54
  144.1 26.1 %collective-permute-start.5 = (bf16[256,2048]{1,0:T(8,128)(2,1)}, bf16[256,2048]{1,0:T(8,128)(2,1)}, u32[]{:S(2)}, u32[]{:S(2)}) collective-permute-start(bf16[256,2048]{1,0:T(8,128)(2,1)} %collective-permute-done.4), channel_id=1, source_target_pairs={{2,0},{3,1},{10,8},{11,9},{18,16},{19,17},{26,24},{27,25}} | collective-permute-start | bytes 3145736 | tf_op jit(solution)/shard_map/ppermute | solution.py:57
  147.7 91.5 %collective-permute-start.18 = (bf16[1024,512]{1,0:T(8,128)(2,1)}, bf16[1024,512]{1,0:T(8,128)(2,1)}, u32[]{:S(2)}, u32[]{:S(2)}) collective-permute-start(bf16[1024,512]{1,0:T(8,128)(2,1)} %get-tuple-element.92), channel_id=1, source_target_pairs={{0,16},{8,24},{16,0},{24,8},{1,17},{9,25},{17,1},{25,9},{2,18},{10... | collective-permute-start | bytes 3145736 | tf_op jit(solution)/shard_map/ppermute | solution.py:40
  149.9 89.3 %collective-permute-start.19 = (bf16[1024,512]{1,0:T(8,128)(2,1)}, bf16[1024,512]{1,0:T(8,128)(2,1)}, u32[]{:S(2)}, u32[]{:S(2)}) collective-permute-start(bf16[1024,512]{1,0:T(8,128)(2,1)} %get-tuple-element.89), channel_id=1, source_target_pairs={{0,24},{8,16},{16,8},{24,0},{1,25},{9,17},{17,9},{25,1},{2,26},{10... | collective-permute-start | bytes 3145736 | tf_op jit(solution)/shard_map/ppermute | solution.py:40
  170.2 103.5 %collective-permute-start.20 = (bf16[2048,1024]{1,0:T(8,128)(2,1)}, bf16[2048,1024]{1,0:T(8,128)(2,1)}, u32[]{:S(2)}, u32[]{:S(2)}) collective-permute-start(bf16[2048,1024]{1,0:T(8,128)(2,1)} %constant_dynamic-update-slice_fusion.5), channel_id=1, source_target_pairs={{0,1},{1,0},{2,3},{3,2},{4,5},{5,4},{6,7},{7,6},{8,9},{9,8},{10,11... | collective-permute-start | bytes 12582920 | tf_op jit(solution)/shard_map/ppermute | solution.py:35
  186.6 76.7 %collective-permute-start.10 = (bf16[1024,2048]{1,0:T(8,128)(2,1)}, bf16[1024,2048]{1,0:T(8,128)(2,1)}, u32[]{:S(2)}, u32[]{:S(2)}) collective-permute-start(bf16[1024,2048]{1,0:T(8,128)(2,1)} %all-gather.11.cloned.1.call-done), channel_id=1, source_target_pairs={{0,1},{1,0},{2,3},{3,2},{4,5},{5,4},{6,7},{7,6},{8,9},{9,8},{10,11... | collective-permute-start | bytes 12582920 | tf_op jit(solution)/shard_map/ppermute | solution.py:35
  222.3 23.3 %collective-permute-start.7 = (bf16[256,512]{0,1:T(8,128)(2,1)S(1)}, bf16[256,512]{0,1:T(8,128)(2,1)S(1)}, u32[]{:S(2)}, u32[]{:S(2)}) collective-permute-start(bf16[256,512]{0,1:T(8,128)(2,1)S(1)} %copy.62), channel_id=1, source_target_pairs={{0,6},{2,0},{4,2},{6,4},{1,7},{3,1},{5,3},{7,5},{8,14},{10,8},{12,... | collective-permute-start | bytes 786440 | tf_op jit(solution)/shard_map/ppermute | solution.py:45
  245.6 114.8 %collective-permute-start.21 = (bf16[1024,2048]{1,0:T(8,128)(2,1)}, bf16[1024,2048]{1,0:T(8,128)(2,1)}, u32[]{:S(2)}, u32[]{:S(2)}) collective-permute-start(bf16[1024,2048]{1,0:T(8,128)(2,1)} %constant_dynamic-update-slice_fusion.2), channel_id=1, source_target_pairs={{0,1},{1,0},{2,3},{3,2},{4,5},{5,4},{6,7},{7,6},{8,9},{9,8},{10,11... | collective-permute-start | bytes 12582920 | tf_op jit(solution)/shard_map/ppermute | solution.py:35
  267.8 27.1 %collective-permute-start.13 = (bf16[256,2048]{1,0:T(8,128)(2,1)S(1)}, bf16[256,2048]{1,0:T(8,128)(2,1)}, u32[]{:S(2)}, u32[]{:S(2)}) collective-permute-start(bf16[256,2048]{1,0:T(8,128)(2,1)S(1)} %add_convert_fusion.4), channel_id=1, source_target_pairs={{0,24},{8,16},{16,8},{24,0},{1,25},{9,17},{17,9},{25,1},{2,26},{10... | collective-permute-start | bytes 3145736 | tf_op jit(solution)/shard_map/ppermute | solution.py:40
  268.5 69.3 %collective-permute-start.12 = (bf16[256,2048]{1,0:T(8,128)(2,1)S(1)}, bf16[256,2048]{1,0:T(8,128)(2,1)}, u32[]{:S(2)}, u32[]{:S(2)}) collective-permute-start(bf16[256,2048]{1,0:T(8,128)(2,1)S(1)} %add_convert_fusion.4), channel_id=1, source_target_pairs={{0,16},{8,24},{16,0},{24,8},{1,17},{9,25},{17,1},{25,9},{2,18},{10... | collective-permute-start | bytes 3145736 | tf_op jit(solution)/shard_map/ppermute | solution.py:40
  269.3 68.5 %collective-permute-start.11 = (bf16[256,2048]{1,0:T(8,128)(2,1)S(1)}, bf16[256,2048]{1,0:T(8,128)(2,1)}, u32[]{:S(2)}, u32[]{:S(2)}) collective-permute-start(bf16[256,2048]{1,0:T(8,128)(2,1)S(1)} %add_convert_fusion.4), channel_id=1, source_target_pairs={{0,8},{8,0},{16,24},{24,16},{1,9},{9,1},{17,25},{25,17},{2,10},{10... | collective-permute-start | bytes 3145736 | tf_op jit(solution)/shard_map/ppermute | solution.py:40
  273.7 82.4 %collective-permute-start.28 = (bf16[256,2048]{1,0:T(8,128)(2,1)S(1)}, bf16[256,2048]{1,0:T(8,128)(2,1)S(1)}, u32[]{:S(2)}, u32[]{:S(2)}) collective-permute-start(bf16[256,2048]{1,0:T(8,128)(2,1)S(1)} %get-tuple-element.62), channel_id=1, source_target_pairs={{0,24},{8,16},{16,8},{24,0},{1,25},{9,17},{17,9},{25,1},{2,26},{10... | collective-permute-start | bytes 3145736 | tf_op jit(solution)/shard_map/ppermute | solution.py:40
  295.0 65.5 %collective-permute-start.27 = (bf16[256,2048]{1,0:T(8,128)(2,1)S(1)}, bf16[256,2048]{1,0:T(8,128)(2,1)S(1)}, u32[]{:S(2)}, u32[]{:S(2)}) collective-permute-start(bf16[256,2048]{1,0:T(8,128)(2,1)S(1)} %get-tuple-element.62), channel_id=1, source_target_pairs={{0,16},{8,24},{16,0},{24,8},{1,17},{9,25},{17,1},{25,9},{2,18},{10... | collective-permute-start | bytes 3145736 | tf_op jit(solution)/shard_map/ppermute | solution.py:40
  337.7 22.7 %collective-permute-start.26 = (bf16[256,2048]{1,0:T(8,128)(2,1)S(1)}, bf16[256,2048]{1,0:T(8,128)(2,1)S(1)}, u32[]{:S(2)}, u32[]{:S(2)}) collective-permute-start(bf16[256,2048]{1,0:T(8,128)(2,1)S(1)} %get-tuple-element.62), channel_id=1, source_target_pairs={{0,8},{8,0},{16,24},{24,16},{1,9},{9,1},{17,25},{25,17},{2,10},{10... | collective-permute-start | bytes 3145736 | tf_op jit(solution)/shard_map/ppermute | solution.py:40
  401.5 27.1 %collective-permute-start.31 = (bf16[256,2048]{1,0:T(8,128)(2,1)S(1)}, bf16[256,2048]{1,0:T(8,128)(2,1)S(1)}, u32[]{:S(2)}, u32[]{:S(2)}) collective-permute-start(bf16[256,2048]{1,0:T(8,128)(2,1)S(1)} %get-tuple-element.84), channel_id=1, source_target_pairs={{0,24},{8,16},{16,8},{24,0},{1,25},{9,17},{17,9},{25,1},{2,26},{10... | collective-permute-start | bytes 3145736 | tf_op jit(solution)/shard_map/ppermute | solution.py:40
  402.8 48.4 %collective-permute-start.30 = (bf16[256,2048]{1,0:T(8,128)(2,1)S(1)}, bf16[256,2048]{1,0:T(8,128)(2,1)S(1)}, u32[]{:S(2)}, u32[]{:S(2)}) collective-permute-start(bf16[256,2048]{1,0:T(8,128)(2,1)S(1)} %get-tuple-element.85), channel_id=1, source_target_pairs={{0,16},{8,24},{16,0},{24,8},{1,17},{9,25},{17,1},{25,9},{2,18},{10... | collective-permute-start | bytes 3145736 | tf_op jit(solution)/shard_map/ppermute | solution.py:40
  403.7 47.5 %collective-permute-start.29 = (bf16[256,2048]{1,0:T(8,128)(2,1)S(1)}, bf16[256,2048]{1,0:T(8,128)(2,1)S(1)}, u32[]{:S(2)}, u32[]{:S(2)}) collective-permute-start(bf16[256,2048]{1,0:T(8,128)(2,1)S(1)} %get-tuple-element.83), channel_id=1, source_target_pairs={{0,8},{8,0},{16,24},{24,16},{1,9},{9,1},{17,25},{25,17},{2,10},{10... | collective-permute-start | bytes 3145736 | tf_op jit(solution)/shard_map/ppermute | solution.py:40
  424.1 49.5 %collective-permute-start.24 = (bf16[256,2048]{1,0:T(8,128)(2,1)S(1)}, bf16[256,2048]{1,0:T(8,128)(2,1)S(1)}, u32[]{:S(2)}, u32[]{:S(2)}) collective-permute-start(bf16[256,2048]{1,0:T(8,128)(2,1)S(1)} %get-tuple-element.87), channel_id=1, source_target_pairs={{0,24},{8,16},{16,8},{24,0},{1,25},{9,17},{17,9},{25,1},{2,26},{10... | collective-permute-start | bytes 3145736 | tf_op jit(solution)/shard_map/ppermute | solution.py:40
  425.4 68.9 %collective-permute-start.23 = (bf16[256,2048]{1,0:T(8,128)(2,1)S(1)}, bf16[256,2048]{1,0:T(8,128)(2,1)S(1)}, u32[]{:S(2)}, u32[]{:S(2)}) collective-permute-start(bf16[256,2048]{1,0:T(8,128)(2,1)S(1)} %get-tuple-element.88), channel_id=1, source_target_pairs={{0,16},{8,24},{16,0},{24,8},{1,17},{9,25},{17,1},{25,9},{2,18},{10... | collective-permute-start | bytes 3145736 | tf_op jit(solution)/shard_map/ppermute | solution.py:40
  428.6 65.7 %collective-permute-start.22 = (bf16[256,2048]{1,0:T(8,128)(2,1)S(1)}, bf16[256,2048]{1,0:T(8,128)(2,1)S(1)}, u32[]{:S(2)}, u32[]{:S(2)}) collective-permute-start(bf16[256,2048]{1,0:T(8,128)(2,1)S(1)} %get-tuple-element.86), channel_id=1, source_target_pairs={{0,8},{8,0},{16,24},{24,16},{1,9},{9,1},{17,25},{25,17},{2,10},{10... | collective-permute-start | bytes 3145736 | tf_op jit(solution)/shard_map/ppermute | solution.py:40
  515.9 71.4 %collective-permute-start.51 = (bf16[1024,2048]{1,0:T(8,128)(2,1)}, bf16[1024,2048]{1,0:T(8,128)(2,1)}, u32[]{:S(2)}, u32[]{:S(2)}) collective-permute-start(bf16[1024,2048]{1,0:T(8,128)(2,1)} %convolution_convert_fusion.1), channel_id=1, source_target_pairs={{0,1},{1,0},{2,3},{3,2},{4,5},{5,4},{6,7},{7,6},{8,9},{9,8},{10,11... | collective-permute-start | bytes 12582920 | tf_op jit(solution)/shard_map/ppermute | solution.py:35
  518.1 27.0 %collective-permute-start.46 = (bf16[1024,512]{1,0:T(8,128)(2,1)S(1)}, bf16[1024,512]{1,0:T(8,128)(2,1)S(1)}, u32[]{:S(2)}, u32[]{:S(2)}) collective-permute-start(bf16[1024,512]{1,0:T(8,128)(2,1)S(1)} %get-tuple-element.71), channel_id=1, source_target_pairs={{0,24},{8,16},{16,8},{24,0},{1,25},{9,17},{17,9},{25,1},{2,26},{10... | collective-permute-start | bytes 3145736 | tf_op jit(solution)/shard_map/ppermute | solution.py:40
  519.9 46.8 %collective-permute-start.45 = (bf16[1024,512]{1,0:T(8,128)(2,1)S(1)}, bf16[1024,512]{1,0:T(8,128)(2,1)S(1)}, u32[]{:S(2)}, u32[]{:S(2)}) collective-permute-start(bf16[1024,512]{1,0:T(8,128)(2,1)S(1)} %get-tuple-element.72), channel_id=1, source_target_pairs={{0,16},{8,24},{16,0},{24,8},{1,17},{9,25},{17,1},{25,9},{2,18},{10... | collective-permute-start | bytes 3145736 | tf_op jit(solution)/shard_map/ppermute | solution.py:40
  521.0 45.7 %collective-permute-start.44 = (bf16[1024,512]{1,0:T(8,128)(2,1)S(1)}, bf16[1024,512]{1,0:T(8,128)(2,1)S(1)}, u32[]{:S(2)}, u32[]{:S(2)}) collective-permute-start(bf16[1024,512]{1,0:T(8,128)(2,1)S(1)} %get-tuple-element.70), channel_id=1, source_target_pairs={{0,8},{8,0},{16,24},{24,16},{1,9},{9,1},{17,25},{25,17},{2,10},{10... | collective-permute-start | bytes 3145736 | tf_op jit(solution)/shard_map/ppermute | solution.py:40
  568.3 290.1 %reduce-scatter.5.cloned.1.call-start = ((), (), s32[]{:S(2)}) async-start(), calls=%async_computation.5 | async-start | bytes 5242880 | tf_op jit(solution)/shard_map/reduce_scatter | solution.py:396
  581.9 33.1 %collective-permute-start.33 = (bf16[256,512]{1,0:T(8,128)(2,1)S(1)}, bf16[256,512]{1,0:T(8,128)(2,1)S(1)}, u32[]{:S(2)}, u32[]{:S(2)}) collective-permute-start(bf16[256,512]{1,0:T(8,128)(2,1)S(1)} %get-tuple-element.106), channel_id=1, source_target_pairs={{0,4},{2,6},{4,0},{6,2},{1,5},{3,7},{5,1},{7,3},{8,12},{10,14},{12... | collective-permute-start | bytes 786440 | tf_op jit(solution)/shard_map/ppermute | solution.py:45
  584.4 31.8 %collective-permute-start.32 = (bf16[256,512]{1,0:T(8,128)(2,1)S(1)}, bf16[256,512]{1,0:T(8,128)(2,1)S(1)}, u32[]{:S(2)}, u32[]{:S(2)}) collective-permute-start(bf16[256,512]{1,0:T(8,128)(2,1)S(1)} %get-tuple-element.107), channel_id=1, source_target_pairs={{0,6},{2,0},{4,2},{6,4},{1,7},{3,1},{5,3},{7,5},{8,14},{10,8},{12,... | collective-permute-start | bytes 786440 | tf_op jit(solution)/shard_map/ppermute | solution.py:45
  597.5 448.7 %all-reduce.5.cloned.1.call-start = ((), (), s32[]{:S(2)}) async-start(), calls=%async_computation.3 | async-start | bytes 196608 | tf_op jit(solution)/shard_map/psum | solution.py:457
  684.4 21.5 %collective-permute-start.42 = (bf16[512,768]{1,0:T(8,128)(2,1)}, bf16[512,768]{1,0:T(8,128)(2,1)S(1)}, u32[]{:S(2)}, u32[]{:S(2)}) collective-permute-start(bf16[512,768]{1,0:T(8,128)(2,1)} %get-tuple-element.75), channel_id=1, source_target_pairs={{0,24},{8,16},{16,8},{24,0},{1,25},{9,17},{17,9},{25,1},{2,26},{10... | collective-permute-start | bytes 2359304 | tf_op jit(solution)/shard_map/ppermute | solution.py:40
  685.7 36.6 %collective-permute-start.41 = (bf16[512,768]{1,0:T(8,128)(2,1)}, bf16[512,768]{1,0:T(8,128)(2,1)S(1)}, u32[]{:S(2)}, u32[]{:S(2)}) collective-permute-start(bf16[512,768]{1,0:T(8,128)(2,1)} %get-tuple-element.76), channel_id=1, source_target_pairs={{0,16},{8,24},{16,0},{24,8},{1,17},{9,25},{17,1},{25,9},{2,18},{10... | collective-permute-start | bytes 2359304 | tf_op jit(solution)/shard_map/ppermute | solution.py:40
  687.1 35.2 %collective-permute-start.40 = (bf16[512,768]{1,0:T(8,128)(2,1)S(1)}, bf16[512,768]{1,0:T(8,128)(2,1)S(1)}, u32[]{:S(2)}, u32[]{:S(2)}) collective-permute-start(bf16[512,768]{1,0:T(8,128)(2,1)S(1)} %get-tuple-element.74), channel_id=1, source_target_pairs={{0,8},{8,0},{16,24},{24,16},{1,9},{9,1},{17,25},{25,17},{2,10},{10... | collective-permute-start | bytes 2359304 | tf_op jit(solution)/shard_map/ppermute | solution.py:40
  688.6 423.5 %all-gather.17.cloned.1.call-start = ((), (), s32[]{:S(2)}) async-start(), calls=%async_computation.7 | async-start | bytes 3932160 | tf_op jit(solution)/shard_map/all_gather | solution.py:431
  725.0 468.1 %all-gather.13.cloned.1.call-start = ((), (), s32[]{:S(2)}) async-start(), calls=%async_computation.4 | async-start | bytes 5242880 | tf_op jit(solution)/shard_map/all_gather | solution.py:405
  797.6 476.5 %all-gather.15.cloned.1.call-start = ((), (), s32[]{:S(2)}) async-start(), calls=%async_computation.6 | async-start | bytes 5242880 | tf_op jit(solution)/shard_map/all_gather | solution.py:404
  879.3 171.0 %collective-permute-start.37 = (bf16[256,2048]{1,0:T(8,128)(2,1)}, bf16[256,2048]{1,0:T(8,128)(2,1)}, u32[]{:S(2)}, u32[]{:S(2)}) collective-permute-start(bf16[256,2048]{1,0:T(8,128)(2,1)} %get-tuple-element.81), channel_id=1, source_target_pairs={{0,6},{2,0},{4,2},{6,4},{1,7},{3,1},{5,3},{7,5},{8,14},{10,8},{12,... | collective-permute-start | bytes 3145736 | tf_op jit(solution)/shard_map/ppermute | solution.py:45
  882.2 168.2 %collective-permute-start.36 = (bf16[256,2048]{1,0:T(8,128)(2,1)}, bf16[256,2048]{1,0:T(8,128)(2,1)}, u32[]{:S(2)}, u32[]{:S(2)}) collective-permute-start(bf16[256,2048]{1,0:T(8,128)(2,1)} %get-tuple-element.82), channel_id=1, source_target_pairs={{0,4},{2,6},{4,0},{6,2},{1,5},{3,7},{5,1},{7,3},{8,12},{10,14},{12... | collective-permute-start | bytes 3145736 | tf_op jit(solution)/shard_map/ppermute | solution.py:45
  882.3 168.1 %collective-permute-start.35 = (bf16[256,2048]{1,0:T(8,128)(2,1)}, bf16[256,2048]{1,0:T(8,128)(2,1)}, u32[]{:S(2)}, u32[]{:S(2)}) collective-permute-start(bf16[256,2048]{1,0:T(8,128)(2,1)} %get-tuple-element.80), channel_id=1, source_target_pairs={{0,2},{2,4},{4,6},{6,0},{1,3},{3,5},{5,7},{7,1},{8,10},{10,12},{12... | collective-permute-start | bytes 3145736 | tf_op jit(solution)/shard_map/ppermute | solution.py:45
  884.8 171.3 %collective-permute-start.25 = (bf16[256,2048]{1,0:T(8,128)(2,1)S(1)}, bf16[256,2048]{1,0:T(8,128)(2,1)S(1)}, u32[]{:S(2)}, u32[]{:S(2)}) collective-permute-start(bf16[256,2048]{1,0:T(8,128)(2,1)S(1)} %copy-done.22), channel_id=1, source_target_pairs={{0,1},{1,0},{2,3},{3,2},{4,5},{5,4},{6,7},{7,6},{8,9},{9,8},{10,11... | collective-permute-start | bytes 3145736 | tf_op jit(solution)/shard_map/ppermute | solution.py:35
  (90 other events, 2016.1 us)
Sparse Core Ops, SparseCore 0:
  12.6 70.0 all-gather.8
  84.5 102.0 all-gather.10
  568.4 212.0 all-reduce.6
  782.6 75.7 reduce-scatter.4
  864.8 181.3 all-reduce.4
  1047.7 64.3 all-gather.16
  1113.7 79.3 all-gather.12
  1194.8 79.2 all-gather.14

commit v2 on v1

--- a/solution.py
+++ b/solution.py
@@ -45,25 +45,58 @@
     return lax.ppermute(value, "context", [(i, (i + step) % size) for i in range(size)])
 
 
-def line_gather(value):
-    size = lax.axis_size("context")
-    index = lax.axis_index("context")
-    upward, downward = [value], [value]
-    for step in range(1, size):
-        upward.append(
-            lax.ppermute(upward[-1], "context", [(i, i + 1) for i in range(step - 1, size - 1)])
-        )
-        downward.append(
-            lax.ppermute(downward[-1], "context", [(i + 1, i) for i in range(0, size - step)])
-        )
-    blocks = [value]
-    for step in range(1, size):
-        blocks.append(jnp.where(index + step < size, downward[step], upward[size - step]))
+def line_step(upward, downward):
+    size, step = lax.axis_size("context"), len(upward)
+    above = lax.ppermute(upward[-1], "context", [(i, i + 1) for i in range(step - 1, size - 1)])
+    below = lax.ppermute(downward[-1], "context", [(i + 1, i) for i in range(0, size - step)])
+    return upward + [above], downward + [below]
+
+
+def line_blocks(upward, downward):
+    size, index = lax.axis_size("context"), lax.axis_index("context")
+    blocks = [upward[0]]
+    for k in range(1, size):
+        blocks.append(jnp.where(index + k < size, downward[k], upward[size - k]))
     return blocks
 
 
-def gather_rows(value):
-    return [value] + [xor_send(value, k) for k in range(1, lax.axis_size("fsdp"))]
+def pass_on(*refs):
+    pass
+
+
+def gate(values, *earlier):
+    anywhere = pl.BlockSpec(memory_space=pl.ANY)
+    return pl.pallas_call(
+        pass_on,
+        out_shape=[jax.ShapeDtypeStruct(value.shape, value.dtype) for value in values],
+        in_specs=[anywhere] * (len(values) + len(earlier)),
+        out_specs=[anywhere] * len(values),
+        input_output_aliases={i: i for i in range(len(values))},
+        compiler_params=pltpu.CompilerParams(vmem_limit_bytes=1 << 20),
+        cost_estimate=pl.CostEstimate(flops=1, transcendentals=0, bytes_accessed=1),
+        name="gate",
+    )(*values, *earlier)
+
+
+def zero_from(value):
+    first = value[(slice(0, 1),) * value.ndim].reshape(())
+    return jnp.minimum(jnp.abs(first.astype(F32)).astype(jnp.int32), 0)
+
+
+def gather_first(value):
+    size = lax.axis_size("fsdp")
+    return [xor_send(value, k) for k in ((1, 2) if size == 4 else range(1, size))]
+
+
+def gather_second(blocks):
+    if lax.axis_size("fsdp") != 4:
+        return []
+    middle = blocks[0].shape[0] // 2
+    return [xor_send(blocks[1][:middle], 1), xor_send(blocks[0][middle:], 2)]
+
+
+def gather_blocks(value, first, second):
+    return [value, *first] + ([jnp.concatenate(second, axis=0)] if second else [])
 
 
 def place(pieces, axis):
@@ -77,23 +110,25 @@
     return whole
 
 
-def pick(whole, k, axis):
+def pick(whole, k, axis, offset=0):
     width = whole.shape[axis] // lax.axis_size("fsdp")
-    return lax.dynamic_slice_in_dim(whole, (lax.axis_index("fsdp") ^ k) * width, width, axis)
-
-
-def exchange(whole, axis):
-    blocks = [pick(whole, 0, axis)]
+    start = (lax.axis_index("fsdp") ^ k) * width + offset
+    return lax.dynamic_slice_in_dim(whole, start, width, axis)
+
+
+def exchange(whole, axis, offset=0):
+    blocks = [pick(whole, 0, axis, offset)]
     for k in range(1, lax.axis_size("fsdp")):
-        blocks.append(xor_send(pick(whole, k, axis), k))
+        blocks.append(xor_send(pick(whole, k, axis, offset), k))
     return blocks
 
 
-def sum_blocks(own, pieces):
-    total = own.astype(F32)
-    for k, piece in enumerate(pieces, 1):
-        total = total + xor_send(piece.astype(BF16), k).astype(F32)
-    return total
+def send_blocks(pieces):
+    return [xor_send(piece, k) for k, piece in enumerate(pieces, 1)]
+
+
+def add_up(own, pieces):
+    return sum([piece.astype(F32) for piece in pieces], own.astype(F32))
 
 
 def head_lanes(rows):
@@ -190,9 +225,7 @@
         ),
         compiler_params=pltpu.CompilerParams(vmem_limit_bytes=48 << 20),
         cost_estimate=pl.CostEstimate(
-            flops=pairs * 8 * rows * rows * PAIR,
-            transcendentals=pairs * rows * rows,
-            bytes_accessed=8 * rows * pairs * PAIR,
+            flops=pairs * 32 * rows * rows * PAIR, transcendentals=0, bytes_accessed=1
         ),
         name="attend",
     )(order, slopes, qkv.reshape(TREE_SEGS, SEG, -1))
@@ -214,9 +247,7 @@
         ),
         compiler_params=pltpu.CompilerParams(vmem_limit_bytes=48 << 20),
         cost_estimate=pl.CostEstimate(
-            flops=pairs * 20 * rows * rows * PAIR,
-            transcendentals=pairs * rows * rows,
-            bytes_accessed=14 * rows * pairs * PAIR,
+            flops=pairs * 60 * rows * rows * PAIR, transcendentals=0, bytes_accessed=1
         ),
         name="attend_back",
     )(order, slopes, qkv.reshape(TREE_SEGS, SEG, -1), grad.reshape(TREE_SEGS, SEG, -1))
@@ -274,12 +305,12 @@
     columns = half // planes
     pairs = columns // PAIR
     hidden = w_up.shape[1] // groups
-    slots = rows // SEG
+
+    def rows_of(whole, k):
+        return lax.dynamic_slice_in_dim(whole, ((plane + k) % planes) * rows, rows, 0)
 
     mine = lax.dynamic_index_in_dim(tokens, core, 0, keepdims=False)
     mine_cot = lax.dynamic_index_in_dim(cotangent, core, 0, keepdims=False)
-    tree = jnp.concatenate(line_gather(mine), axis=0)
-
     packed = jnp.concatenate(
         [
             norm_gain,
@@ -291,42 +322,52 @@
         ],
         axis=0,
     )
-    small = lax.all_gather(packed, ("tensor", "fsdp"), axis=0, tiled=False).astype(F32)
-    small = small.reshape(2, groups, packed.shape[0], part)
-    spread = lax.dynamic_index_in_dim(small, core, 0, keepdims=False)[:, :6]
-    spread = spread.transpose(1, 0, 2).reshape(6, width)
+    lines = packed.size // (3 * columns)
+    chosen = lax.dynamic_slice_in_dim(w_qkv, plane * columns, columns, 2)
+    chosen = chosen.reshape(3, part, pairs, PAIR).transpose(1, 2, 0, 3).reshape(part, 3 * columns)
+    chosen = jnp.concatenate(
+        [
+            chosen,
+            packed.reshape(lines, 3 * columns),
+            jnp.zeros((-lines % 32, 3 * columns), BF16),
+        ],
+        axis=0,
+    )
+    up_pieces = [pick(w_up, k, 1) for k in range(groups)]
+    down_rows = lax.dynamic_index_in_dim(
+        w_down.reshape(groups, planes, hidden // planes, part), plane, 1, keepdims=False
+    )
+    down_pieces = [pick(down_rows, k, 0)[0] for k in range(groups)]
+
+    tree = lax.all_gather(mine, "context", axis=0, tiled=True)
+    head_first = gather_first(chosen)
+    rest = gate([*head_first, *up_pieces[1:]])
+    head_first, up_pieces[1:] = rest[: len(head_first)], rest[len(head_first) :]
+    head_second = gather_second(head_first)
+    up_blocks = up_pieces[:1] + send_blocks(up_pieces[1:])
+    tree, mine_cot, *down_pieces = gate([tree, mine_cot, *down_pieces], *head_second)
+    head_blocks = gather_blocks(chosen, head_first, head_second)
+    heads_own = place([block[:part] for block in head_blocks], 0)
+    w_heads = jnp.concatenate([heads_own, swap_cores(heads_own)], axis=1)
+
+    small = [block[part : part + lines].reshape(1, -1, part) for block in head_blocks]
+    small = place(small, 0)
+    small = jnp.stack([small, swap_cores(small)])
+    spread = small[0, :, :6].astype(F32).transpose(1, 0, 2).reshape(6, width)
     gain_one, gain_two, shift_one, shift_two, out_shift, down_shift = (
         spread[i : i + 1] for i in range(6)
     )
-    head_shift = small[:, :, 6].reshape(2, groups, 2, part // 2).transpose(0, 2, 1, 3)
+    head_shift = small[:, :, 6].astype(F32).reshape(2, groups, 2, part // 2).transpose(0, 2, 1, 3)
     head_shift = lax.dynamic_slice_in_dim(
         head_shift.reshape(2, 2, half), plane * columns, columns, 2
     ).reshape(2, 2, pairs, PAIR)
     head_shift = jnp.stack(
         [head_shift[:, 0], jnp.zeros_like(head_shift[:, 0]), head_shift[:, 1]], axis=2
-    ).reshape(2, pairs * 3 * PAIR)
-    up_shift = lax.dynamic_index_in_dim(small, group, 1, keepdims=False)[:, 7:].reshape(2, hidden)
-
-    def own_first(both):
-        return jnp.where(core == 0, both, both[::-1])
-
-    head_shift = own_first(head_shift).reshape(1, -1)
-    up_shift = own_first(up_shift)
-
-    chosen = lax.dynamic_slice_in_dim(w_qkv, plane * columns, columns, 2)
-    chosen = chosen.reshape(3, part, pairs, PAIR).transpose(1, 2, 0, 3).reshape(part, 3 * columns)
-    heads_own = lax.all_gather(chosen, "fsdp", axis=0, tiled=True)
-    w_heads = jnp.concatenate([heads_own, swap_cores(heads_own)], axis=1)
-    out_own = lax.all_gather(w_out, "fsdp", axis=1, tiled=True)
-    out_other = swap_cores(out_own)
-
-    up_own = place(exchange(w_up, 1), 0)
-    down_own = place(exchange(w_down, 0), 1)
-    up_other, down_other = swap_cores(up_own), swap_cores(down_own)
-    all_cot = jnp.concatenate(gather_rows(mine_cot), axis=0)
+    ).reshape(1, 2 * pairs * 3 * PAIR)
+    up_shift = lax.dynamic_index_in_dim(small, group, 1, keepdims=False)[:, 7:]
+    up_shift = up_shift.astype(F32).reshape(2, hidden)
 
     depth = lax.dynamic_index_in_dim(positions, core, 0, keepdims=False)[::SEG] // SEG
-    depth = jnp.roll(depth, -plane * slots)
     ids = jnp.arange(TREE_SEGS, dtype=jnp.int32)
     before = (depth[None, :] < depth[:, None]) | (
         (depth[None, :] == depth[:, None]) & (ids[None, :] < ids[:, None])
@@ -339,13 +380,30 @@
     other_ids = (1 - core) * (half // HEAD_DIM) + head_ids
     slopes = jnp.exp2(-8.0 * (jnp.concatenate([own_ids, other_ids]) + 1).astype(F32) / HEADS)
 
+    mine_out = lax.dynamic_slice_in_dim(w_out, zero_from(mine_cot), half, 0)
+    out_first = gather_first(mine_out)
     tree_unit, _ = normalise(tree.astype(F32))
     normed = (tree_unit * gain_one + shift_one).astype(BF16)
     qkv = (dot_nn(normed, w_heads) + head_shift).astype(BF16)
+    qkv, *rest = gate([qkv, *out_first, *down_pieces[1:]], *up_blocks[1:])
+    out_first, down_pieces[1:] = rest[: len(out_first)], rest[len(out_first) :]
+    out_second = gather_second(out_first)
+    down_blocks = down_pieces[:1] + send_blocks(down_pieces[1:])
     mixed = attend(order, slopes, qkv)
-    arrived = [mixed[:rows]]
+    mixed, mine_cot, *down_blocks = gate([mixed, mine_cot, *down_blocks], *out_second)
+    out_own = place(gather_blocks(mine_out, out_first, out_second), 1)
+    down_rows = place(down_blocks, 1)
+    up_own = place(up_blocks, 0)
+    up_other, out_other = swap_cores(up_own), swap_cores(out_own)
+
+    arrived = [rows_of(mixed, 0)]
     for k in range(1, planes):
-        arrived.append(ring_send(mixed[k * rows : (k + 1) * rows], k))
+        arrived.append(ring_send(rows_of(mixed, k), k))
+    cot_first = gather_first(mine_cot)
+    out_other, *rest = gate([out_other, *arrived, *cot_first])
+    arrived, cot_first = rest[:planes], rest[planes:]
+    down_own = lax.all_gather(down_rows, "context", axis=0, tiled=True)
+    cot_second = gather_second(cot_first)
     attended = jnp.stack(arrived[::-1], axis=0)
     attended = jnp.roll(attended, plane + 1, axis=0)
     attended = attended.reshape(planes, rows, 2, columns).transpose(2, 1, 0, 3)
@@ -355,21 +413,42 @@
     )
     unit_two, scale_two = normalise(middle)
     normed_two = (unit_two * gain_two + shift_two).astype(BF16)
-    all_two = jnp.concatenate(gather_rows(normed_two), axis=0)
-
-    def unit(w_up_half, w_down_half, shift):
-        pre = dot_nn(all_two, w_up_half) + shift
-        below = normal_cdf(pre)
-        active = (pre * below).astype(BF16)
-        back = dot_nt(all_cot, w_down_half) * (below + pre * normal_pdf(pre))
-        return active, back.astype(BF16)
-
-    active_own, back_own = unit(up_own, down_own, up_shift[0:1])
-    active_other, back_other = unit(up_other, down_other, up_shift[1:2])
-
-    grad_two = dot_nt(back_own, up_own) + dot_nt(back_other, up_other)
-    blocks = [grad_two[k * rows : (k + 1) * rows] for k in range(groups)]
-    grad_two = sum_blocks(blocks[0], blocks[1:])
+    (normed_two,) = gate([normed_two], *cot_second)
+    two_first = gate(gather_first(normed_two))
+    two_second = gather_second(two_first)
+    all_two = jnp.concatenate(gather_blocks(normed_two, two_first, two_second), axis=0)
+    all_cot = jnp.concatenate(gather_blocks(mine_cot, cot_first, cot_second), axis=0)
+
+    pre_other = dot_nn(all_two, up_other) + up_shift[1:2]
+    active_other = (pre_other * normal_cdf(pre_other)).astype(BF16)
+    grad_down = swap_cores(dot_tn(active_other, all_cot).astype(BF16))
+    pre_own = dot_nn(all_two, up_own) + up_shift[0:1]
+    active_own = (pre_own * normal_cdf(pre_own)).astype(BF16)
+    grad_down = (dot_tn(active_own, all_cot) + grad_down.astype(F32)).astype(BF16)
+
+    def slope_of(pre):
+        return normal_cdf(pre) + pre * normal_pdf(pre)
+
+    (down_own,) = gate([down_own], grad_down)
+    down_other = swap_cores(down_own)
+    back_other = (dot_nt(all_cot, down_other) * slope_of(pre_other)).astype(BF16)
+    back_own = (dot_nt(all_cot, down_own) * slope_of(pre_own)).astype(BF16)
+
+    grad_two = (dot_nt(back_own, up_own) + dot_nt(back_other, up_other)).astype(BF16)
+    back_other_in = back_other
+    back_other, own_two, *sent = gate(
+        [back_other] + [grad_two[k * rows : (k + 1) * rows] for k in range(groups)]
+    )
+    grad_down = lax.psum_scatter(grad_down, "context", scatter_dimension=0, tiled=True)
+    grad_two = send_blocks(sent)
+    grad_up = swap_cores(dot_tn(all_two, back_other).astype(BF16))
+    grad_up = (dot_tn(all_two, back_own) + grad_up.astype(F32)).astype(BF16)
+    grad_up = grad_up.reshape(groups, planes, part // planes, hidden).transpose(1, 0, 2, 3)
+    grad_up = grad_up.reshape(width, hidden)
+    grad_down, *grad_two = gate([grad_down, *grad_two], grad_up)
+    grad_up = lax.psum_scatter(grad_up, "context", scatter_dimension=0, tiled=True)
+
+    grad_two = add_up(own_two, grad_two)
     grad_middle = mine_cot.astype(F32) + norm_back(unit_two, scale_two, gain_two, grad_two)
     grad_branch = grad_middle.astype(BF16)
     grad_mixed = jnp.stack(
@@ -381,68 +460,38 @@
     )
     grad_mixed = grad_mixed.transpose(2, 0, 1, 3).reshape(planes, rows, 2 * columns)
     grad_mixed = jnp.roll(grad_mixed, -plane, axis=0)
+    grad_down = exchange(grad_down, 1)
+    grad_mixed = gate([grad_mixed[k] for k in range(planes)])
+
     back_rows = [grad_mixed[0]]
     for k in range(1, planes):
         back_rows.append(ring_send(grad_mixed[k], k))
-    grad_tree = jnp.concatenate(back_rows[:1] + back_rows[:0:-1], axis=0)
-
-    layer_out = dot_nn(active_own, down_own) + dot_nn(active_other, down_other)
-    blocks = [layer_out[k * rows : (k + 1) * rows] for k in range(groups)]
-    layer_out = middle + (sum_blocks(blocks[0], blocks[1:]) + down_shift)
-    layer_out = both_micros(layer_out.astype(BF16))
-
-    grad_down = swap_cores(dot_tn(active_other, all_cot).astype(BF16))
-    grad_down = (dot_tn(active_own, all_cot) + grad_down.astype(F32)).astype(BF16)
-    grad_down = lax.psum_scatter(grad_down, "context", scatter_dimension=0, tiled=True)
-    grad_down = place([piece[None] for piece in exchange(grad_down, 1)], 0)
-    grad_up = swap_cores(dot_tn(all_two, back_other).astype(BF16))
-    grad_up = (dot_tn(all_two, back_own) + grad_up.astype(F32)).astype(BF16)
-    grad_up = grad_up.reshape(groups, planes, part // planes, hidden).transpose(1, 0, 2, 3)
-    grad_up = lax.psum_scatter(grad_up, "context", scatter_dimension=0, tiled=True)[0]
-    grad_up = exchange(grad_up, 0)
-    grad_up = place([piece[0] for piece in grad_up], 1)
-    g_down = lax.all_gather(grad_down, "context", axis=1, tiled=False)
-    g_up = lax.all_gather(grad_up, "context", axis=0, tiled=True)
-
     grad_out = swap_cores(dot_tn(attended[1], grad_branch).astype(BF16))
     grad_out = dot_tn(attended[0], grad_branch) + grad_out.astype(F32)
-    grad_out = sum_blocks(
-        pick(grad_out, 0, 1), [pick(grad_out, k, 1) for k in range(1, groups)]
-    )
-    g_out = lax.psum(grad_out.astype(BF16), "context")
-
+    grad_tree = jnp.roll(jnp.stack(back_rows[:1] + back_rows[:0:-1]), plane, axis=0)
+    grad_tree = grad_tree.reshape(planes * rows, 2 * columns)
+    out_blocks = [pick(grad_out, k, 1) for k in range(groups)]
+    out_own_block, out_blocks = out_blocks[0], [piece.astype(BF16) for piece in out_blocks[1:]]
+    grad_tree, grad_up, *grad_down = gate([grad_tree, grad_up, *grad_down])
+    grad_down = place([piece[None] for piece in grad_down], 0)
+
+    down_up, down_down = line_step([grad_down], [grad_down])
+    grad_up = exchange(grad_up.reshape(groups, part // planes, hidden), 0)
     grad_qkv = attend_back(order, slopes, qkv, grad_tree)
+    grad_qkv, down_up[-1], down_down[-1], *rest = gate(
+        [grad_qkv, down_up[-1], down_down[-1], *grad_up, *out_blocks]
+    )
+    grad_up, out_blocks = rest[:groups], rest[groups:]
+
+    grad_up = place([piece[0] for piece in grad_up], 1)
     grad_normed = dot_nt(grad_qkv, w_heads)
-    grad_first = [grad_normed[:rows]]
-    for k in range(1, planes):
-        sent = grad_normed[k * rows : (k + 1) * rows].astype(BF16)
-        grad_first.append(ring_send(sent, k).astype(F32))
-    grad_first = sum(grad_first[1:], grad_first[0])
-    unit_one, scale_one = normalise(mine.astype(F32))
-    grad_tokens = grad_middle + norm_back(unit_one, scale_one, gain_one, grad_first)
-    grad_tokens = both_micros(grad_tokens.astype(BF16))
-
-    grad_heads = dot_tn(normed, grad_qkv)
-    grad_other = swap_cores(grad_heads[:, 3 * columns :].astype(BF16))
-    grad_heads = grad_heads[:, : 3 * columns] + grad_other.astype(F32)
-    grad_heads = sum_blocks(
-        pick(grad_heads, 0, 0), [pick(grad_heads, k, 0) for k in range(1, groups)]
-    ).astype(BF16)
-    g_heads = lax.all_gather(grad_heads, "context", axis=0, tiled=False)
-
     head_sums = jnp.sum(grad_qkv.astype(F32), axis=0).reshape(2, pairs, 3, PAIR)
     head_sums = jnp.stack([head_sums[:, :, 0], head_sums[:, :, 2]], axis=1)
-    head_sums = own_first(head_sums.reshape(2, 2, columns)).transpose(1, 0, 2)
     head_row = lax.dynamic_update_slice_in_dim(
-        jnp.zeros((2, 2, half), F32), head_sums, plane * columns, 2
-    )
-    up_sums = own_first(
-        jnp.stack([jnp.sum(side.astype(F32), axis=0) for side in (back_own, back_other)])
-    )
-    up_row = lax.dynamic_update_slice_in_dim(
-        jnp.zeros((2, groups * hidden), F32), up_sums, group * hidden, 1
-    )
-    vectors = jnp.concatenate(
+        jnp.zeros((2, 2, half), F32), head_sums.reshape(2, 2, columns), plane * columns, 2
+    )
+    up_sums = [jnp.sum(side.astype(F32), axis=0) for side in (back_own, back_other_in)]
+    sums = jnp.concatenate(
         [
             jnp.sum(grad_normed * tree_unit, axis=0),
             jnp.sum(grad_two * unit_two, axis=0),
@@ -451,38 +500,96 @@
             jnp.sum(grad_branch.astype(F32), axis=0),
             jnp.sum(mine_cot.astype(F32), axis=0),
             head_row.reshape(-1),
-            up_row.reshape(-1),
+            *up_sums,
         ]
     )
-    vectors = lax.psum(vectors, ("fsdp", "context", "tensor")).reshape(-1, width)
-
-    def share(whole):
-        return lax.dynamic_slice_in_dim(whole, group * part, part, whole.ndim - 1)
-
-    g_gain = share(vectors[0:2])
-    g_shift = share(vectors[2:4])
-    g_out_shift = share(vectors[4])
-    g_down_shift = share(vectors[5])
-    g_qv = lax.dynamic_slice_in_dim(
-        vectors[6:8], (core * groups + group) * (part // 2), part // 2, 1
-    )
-    g_up_shift = lax.dynamic_slice_in_dim(
-        vectors[8:].reshape(-1), (core * groups + group) * hidden, hidden, 0
-    )
-    g_heads = g_heads.reshape(planes, part, pairs, 3, PAIR).transpose(3, 1, 0, 2, 4)
+    lines = -(-sums.shape[0] // (16 * width)) * 16
+    sums = jnp.pad(sums, (0, lines * width - sums.shape[0])).reshape(lines, width)
+    blocks = [
+        jnp.concatenate([grad_normed[k * rows : (k + 1) * rows], sums]) for k in range(planes)
+    ]
+    blocks = jnp.concatenate(blocks).astype(BF16)
+    blocks, grad_qkv, down_up[-1], down_down[-1], *out_blocks = gate(
+        [blocks, grad_qkv, down_up[-1], down_down[-1], *out_blocks]
+    )
+    later = zero_from(blocks)
+    grad_first = lax.psum_scatter(blocks, "context", scatter_dimension=0, tiled=True)
+    g_up = lax.all_gather(grad_up, "context", axis=0, tiled=True)
+
+    down_up, down_down = line_step(down_up, down_down)
+    grad_heads = dot_tn(normed, grad_qkv)
+    head_other = swap_cores(grad_heads[:, 3 * columns :].astype(BF16))
+    grad_heads = grad_heads[:, : 3 * columns] + head_other.astype(F32)
+    head_pieces = [pick(grad_heads, k, 0).astype(BF16) for k in range(1, groups)]
+    grad_heads = add_up(pick(grad_heads, 0, 0), send_blocks(head_pieces)).astype(BF16)
+    grad_heads = grad_heads.reshape(part, pairs, 3, PAIR).transpose(2, 0, 1, 3)
+    grad_heads = grad_heads.reshape(3 * part, columns)
+    out_blocks = send_blocks(out_blocks)
+    layer_out = dot_nn(
+        lax.dynamic_slice_in_dim(active_own, later, groups * rows, 0), down_own
+    ) + dot_nn(lax.dynamic_slice_in_dim(active_other, later, groups * rows, 0), down_other)
+    layer_out = layer_out.astype(BF16)
+    grad_first, grad_heads, down_up[-1], down_down[-1], out_own_block, *layer_blocks = gate(
+        [grad_first, grad_heads, down_up[-1], down_down[-1], out_own_block]
+        + [layer_out[k * rows : (k + 1) * rows] for k in range(groups)],
+        *out_blocks,
+        g_up,
+    )
+    while len(down_up) < planes:
+        down_up, down_down = line_step(down_up, down_down)
+    grad_out = add_up(out_own_block, out_blocks).astype(BF16)
+    grad_out = lax.psum_scatter(grad_out, "context", scatter_dimension=0, tiled=True)
+    layer_out = add_up(layer_blocks[0], send_blocks(layer_blocks[1:]))
+    layer_out = middle + (layer_out + down_shift)
+    layer_out = both_micros(layer_out.astype(BF16))
+    grad_heads, grad_out = gate([grad_heads, grad_out], down_up[-1], down_down[-1])
+
+    lines = grad_out.shape[0]
+    last = [grad_heads] + [
+        grad_out[:, i : i + columns] for i in range(0, part, columns)
+    ]
+    last = lax.all_gather(jnp.concatenate(last), "context", axis=1, tiled=True)
+    g_heads = last[: 3 * part]
+    g_out = last[3 * part :].reshape(part // columns, lines, planes, columns)
+    g_out = g_out.transpose(2, 1, 0, 3).reshape(half, part)
+    g_down = jnp.zeros((groups, planes, hidden // planes, part), F32)
+    for k, piece in enumerate(line_blocks(down_up, down_down)):
+        g_down = lax.dynamic_update_slice_in_dim(
+            g_down, piece.astype(F32)[:, None], (plane + k) % planes, 1
+        )
+
+    sums = grad_first[rows:].astype(F32).reshape(-1)
+    grad_first = grad_first[:rows].astype(F32)
+    unit_one, scale_one = normalise(mine.astype(F32))
+    grad_tokens = grad_middle + norm_back(unit_one, scale_one, gain_one, grad_first)
+    grad_tokens = both_micros(grad_tokens.astype(BF16))
+
+    spread = sums[: 6 * width].reshape(6, groups, part)
+    spread = spread.transpose(1, 0, 2).reshape(groups, 6 * part)
+    head_row = sums[6 * width : 8 * width].reshape(4, groups, part // 2)
+    head_row = head_row.transpose(1, 0, 2).reshape(groups, 2 * part)
+    up_sums = sums[8 * width : 8 * width + 2 * hidden].reshape(2, hidden)
+    sums = jnp.concatenate([spread, head_row], axis=1)
+    total = pick(sums, 0, 0)
+    for k in range(1, groups):
+        total = total + xor_send(pick(sums, k, 0), k)
+    total = total[0]
+    total_other = swap_cores(jnp.concatenate([total[: 6 * part], total[7 * part :], up_sums[1]]))
+    total = jnp.concatenate([total[: 7 * part], up_sums[0]]) + total_other
+    wide = total[: 6 * part].reshape(6, part)
     return (
         layer_out,
         grad_tokens,
-        g_gain,
-        g_shift,
-        g_heads.reshape(3, part, half).astype(F32),
-        g_qv,
+        wide[0:2],
+        wide[2:4],
+        g_heads.astype(F32).reshape(3, part, half),
+        total[6 * part : 7 * part].reshape(2, part // 2),
         g_out.astype(F32),
-        g_out_shift,
+        wide[4],
         g_up.astype(F32),
-        g_up_shift,
-        g_down.reshape(groups * hidden, part).astype(F32),
-        g_down_shift,
+        total[7 * part :],
+        g_down.reshape(groups * hidden, part),
+        wide[5],
     )
 
 

time: 1300 us -> 909 us (0.70)
  waiting for transfers between devices: 751 us -> 374 us
  local copies, waits for them, and re-layouts: 94 us -> 191 us
  blocking collectives: 80 us -> 0 us
  matrix products: 167 us -> 140 us
    psum x2 -> x0, waiting for transfers between devices: 215 us -> none  [the longest x1 161 us: per_device(): lax.psum(vectors, ('fsdp', 'context', 'tensor')).reshape(-1, width)]
    all_gather x1 -> x0, blocking collectives: 80 us -> none  [per_device(): lax.all_gather(packed, ('tensor', 'fsdp'), axis=0, tiled=False).astype(F32)]
    unnamed x167 -> x313, local copies, waits for them, and re-layouts: 22.6 us -> 102 us
    ppermute x30 -> x43, waiting for transfers between devices: 231 us -> 162 us  [xor_send(): return lax.ppermute(value, 'fsdp', [(i, i ^ step) for i in range(size)])]
    all_gather x4 -> x3, waiting for transfers between devices: 133 us -> 72.3 us  [the longest x1 28.7 us: per_device(): last = lax.all_gather(jnp.concatenate(last), 'context', axis=1, tiled=True)]
    reduce_scatter x1, waiting for transfers between devices: 60.7 us -> 0.01 us  [per_device(): lax.psum_scatter(grad_down, 'context', scatter_dimension=0, tiled=True)]
    all_gather x1, waiting for transfers between devices: 51.3 us -> 0.01 us  [per_device(): g_up = lax.all_gather(grad_up, 'context', axis=0, tiled=True)]
    reduce_scatter x0 -> x3, waiting for transfers between devices: none -> 40.5 us  [the longest x1 40.5 us: per_device(): lax.psum_scatter(blocks, 'context', scatter_dimension=0, tiled=True)]
  transfers between devices with their start and end apart: 63 -> 75, of which waited for: 29 -> 34; matrix products, arithmetic and copies ran while one was open for 19% -> 31% of each run, Pallas kernels for 4% -> 5%
where the time goes in v2:
time: 909 us; the launch traced here: 903 us
  waiting for transfers between devices  374 us (41%)
  local copies, waits for them, and re-layouts  191 us (21%)
  matrix products  140 us (15%)
  starting transfers between devices  70.8 us (8%)
  other arithmetic  64.3 us (7%)
  Pallas kernels  46.3 us (5%)
  between operations  16.4 us (2%)
    ppermute x43, waiting for transfers between devices, xor_send(): return lax.ppermute(value, 'fsdp', [(i, i ^ step) for i in range(size)])  162 us
    unnamed x313, local copies, waits for them, and re-layouts  102 us
    ppermute x43, starting transfers between devices, xor_send(): return lax.ppermute(value, 'fsdp', [(i, i ^ step) for i in range(size)])  54.8 us
    dot_general x7, matrix products, dot_nn(): lax.dot_general(left, right, (((1,), (0,)), ((), ())), preferred_element_...  51.9 us
    dot_general x7, matrix products, dot_nt(): lax.dot_general(left, right, (((1,), (1,)), ((), ())), preferred_element_...  50 us
    ppermute x6, waiting for transfers between devices, ring_send(): lax.ppermute(value, 'context', [(i, (i + step) % size) for i in range(siz...  49.2 us
    reduce_scatter x1, waiting for transfers between devices, per_device(): lax.psum_scatter(blocks, 'context', scatter_dimension=0, tiled=True)  40.5 us
    ppermute x3, waiting for transfers between devices, line_step(): lax.ppermute(downward[-1], 'context', [(i + 1, i) for i in range(0, size...  39.3 us
  transfers between devices with their start and end apart: 75, of which 34 were waited for; matrix products, arithmetic and copies ran while one was open for 31% of the time, Pallas kernels for 5%

profile of v2, /device:TPU:0, one launch (start us, length us, event | category | flops | bytes accessed | tf_op | source)
XLA Modules:
  0.0 902.8 jit_solution(14887029349262729501)
XLA Ops:
  29.6 10.1 %collective-permute-done.refs_0_ = bf16[544,768]{1,0:T(8,128)(2,1)S(1)} collective-permute-done((bf16[544,768]{1,0:T(8,128)(2,1)}, bf16[544,768]{1,0:T(8,128)(2,1)S(1)}, u32[]{:S(2)}, u32[]{:S(2)}) %collective-permute-start) | collective-permute-done | bytes 835616 | tf_op jit(solution)/shard_map/ppermute | solution.py:40
  72.4 21.5 %all-gather.12.cloned.1.call-done = bf16[1,1024,2048]{2,1,0:T(8,128)(2,1)} async-done(((bf16[1,256,2048]{2,1,0:T(8,128)(2,1)}), bf16[1,1024,2048]{2,1,0:T(8,128)(2,1)}) %all-gather.12.cloned.1.call-update) | async-done | bytes 4194320 | tf_op jit(solution)/shard_map/all_gather | solution.py:342
  111.4 9.7 %add_convert_fusion.4.refs_0_ = bf16[1024,1536]{1,0:T(8,128)(2,1)S(1)} fusion(bf16[2048,768]{1,0:T(8,128)(2,1)} %collective-permute-done.4, bf16[2048,768]{1,0:T(8,128)(2,1)} %fusion.50, f32[1536]{0:T(1024)S(1)} %add.425, bf16[1024,2048]{1,0:T(8,128)(2,1)S(1)} %copy-done.4, f32[2048]{0:T(1024)S(1)} %bitcast.292, f32[2048]{0:T(1024)S(1)} %bitcast.276, ...), kind=kOutput, calls=%fused_computation.21 | convolution fusion | flops 6470762496 | bytes 13662208 | tf_op jit(solution)/shard_map/dot_general | solution.py:23
  121.2 13.6 %collective-permute-done.10.refs_8_ = bf16[512,1024]{1,0:T(8,128)(2,1)S(1)} collective-permute-done((bf16[512,1024]{1,0:T(8,128)(2,1)S(1)}, bf16[512,1024]{1,0:T(8,128)(2,1)S(1)}, u32[]{:S(2)}, u32[]{:S(2)}) %collective-permute-start.10) | collective-permute-done | bytes 1048608 | tf_op jit(solution)/shard_map/ppermute | solution.py:40
  160.9 18.1 %attend.1 = bf16[8,128,512]{2,1,0:T(8,128)(2,1)S(1)} custom-call(s32[8]{0:T(128)S(1)} %select_reduce_fusion.order, f32[8]{0:T(128)S(1)} %fusion.65.slopes, bf16[8,128,1536]{2,1,0:T(8,128)(2,1)S(1)} %bitcast.239), custom_call_target="tpu_custom_call" | custom-call | flops 17179869184 | bytes 1 | tf_op jit(solution)/shard_map/attend/pallas_call | solution.py:216
  191.4 5.5 collective-permute-done.17.refs_2_
  198.8 7.5 collective-permute-done.18.refs_3_
  223.1 3.7 fusion.80
  238.6 13.6 %collective-permute-done.24.refs_0_ = bf16[256,2048]{1,0:T(8,128)(2,1)S(1)} collective-permute-done((bf16[256,2048]{1,0:T(8,128)(2,1)S(1)}, bf16[256,2048]{1,0:T(8,128)(2,1)S(1)}, u32[]{:S(2)}, u32[]{:S(2)}) %collective-permute-start.24) | collective-permute-done | bytes 1048608 | tf_op jit(solution)/shard_map/ppermute | solution.py:40
  258.1 5.4 collective-permute-done.26
  264.5 10.1 %multiply_convert_fusion = (bf16[1024,1024]{1,0:T(8,128)(2,1)S(1)}, f32[1024,1024]{1,0:T(8,128)}) fusion(f32[1024]{0:T(1024)S(1)} %bitcast.298, bf16[1024,2048]{1,0:T(8,128)(2,1)S(1)} %constant_dynamic-update-slice_fusion.5, bf16[2048,1024]{1,0:T(8,128)(2,1)} %collective-permute-done.28), kind=kOutput, calls=%fused_computation.36 | convolution fusion | flops 4301258752 | bytes 14684160 | tf_op jit(solution)/shard_map/dot_general | solution.py:23
  274.6 4.8 convolution_convert_fusion.2
  279.6 6.3 fusion.82
  287.9 6.6 add_convert_fusion.3.refs_1_
  294.5 22.1 %all-gather.6.cloned.1.call-done.refs_0_ = bf16[1024,2048]{1,0:T(8,128)(2,1)} async-done(((bf16[256,2048]{1,0:T(8,128)(2,1)}), bf16[1024,2048]{1,0:T(8,128)(2,1)}) %all-gather.6.cloned.1.call-update) | async-done | bytes 4194320 | tf_op jit(solution)/shard_map/all_gather | solution.py:405
  323.1 10.7 %convert_reduce_fusion.3 = (bf16[1024]{0:T(1024)(128)(2,1)S(1)}, bf16[1024,1024]{1,0:T(8,128)(2,1)S(1)}) fusion(f32[1024,1024]{1,0:T(8,128)} %copy-done.137, f32[1024]{0:T(1024)S(1)} %bitcast.296, bf16[1024,2048]{1,0:T(8,128)(2,1)} %copy-done.119, bf16[1024,2048]{1,0:T(8,128)(2,1)} %copy-done.41), kind=kOutput, calls=%fused_computation.35 | convolution fusion | flops 4308597760 | bytes 14686208 | tf_op jit(solution)/shard_map/dot_general | solution.py:31
  333.9 7.7 convert_reduce_fusion.2
  341.6 6.4 fusion.83
  348.0 7.1 add_convert_fusion.2
  358.5 5.3 convolution_convert_fusion.1
  364.4 6.8 collective-permute-done.34
  371.2 5.0 add_convert_fusion.1
  383.4 22.5 %collective-permute-done.31.refs_1_ = bf16[256,2048]{1,0:T(8,128)(2,1)S(1)} collective-permute-done((bf16[256,2048]{1,0:T(8,128)(2,1)S(1)}, bf16[256,2048]{1,0:T(8,128)(2,1)S(1)}, u32[]{:S(2)}, u32[]{:S(2)}) %collective-permute-start.31) | collective-permute-done | bytes 1048608 | tf_op jit(solution)/shard_map/ppermute | solution.py:40
  406.8 22.2 %collective-permute-done.32.refs_2_ = bf16[256,2048]{1,0:T(8,128)(2,1)S(1)} collective-permute-done((bf16[256,2048]{1,0:T(8,128)(2,1)S(1)}, bf16[256,2048]{1,0:T(8,128)(2,1)S(1)}, u32[]{:S(2)}, u32[]{:S(2)}) %collective-permute-start.32) | collective-permute-done | bytes 1048608 | tf_op jit(solution)/shard_map/ppermute | solution.py:40
  450.0 3.5 convolution_convert_fusion.3
  454.6 3.5 convolution_convert_fusion.4
  466.6 13.6 %collective-permute-done.35 = bf16[256,512]{1,0:T(8,128)(2,1)S(1)} collective-permute-done((bf16[256,512]{1,0:T(8,128)(2,1)S(1)}, bf16[256,512]{1,0:T(8,128)(2,1)S(1)}, u32[]{:S(2)}, u32[]{:S(2)}) %collective-permute-start.35) | collective-permute-done | bytes 262176 | tf_op jit(solution)/shard_map/ppermute | solution.py:45
  481.7 19.1 %collective-permute-done.36 = bf16[256,512]{1,0:T(8,128)(2,1)S(1)} collective-permute-done((bf16[256,512]{1,0:T(8,128)(2,1)S(1)}, bf16[256,512]{1,0:T(8,128)(2,1)S(1)}, u32[]{:S(2)}, u32[]{:S(2)}) %collective-permute-start.36) | collective-permute-done | bytes 262176 | tf_op jit(solution)/shard_map/ppermute | solution.py:45
  505.7 3.9 convert_add_fusion
  523.0 28.2 %attend_back.1 = bf16[8,128,1536]{2,1,0:T(8,128)(2,1)S(1)} custom-call(s32[8]{0:T(128)S(1)} %copy-done.97, f32[8]{0:T(128)S(1)} %copy-done.95, bf16[8,128,1536]{2,1,0:T(8,128)(2,1)} %bitcast.238, bf16[8,128,512]{2,1,0:T(8,128)(2,1)S(1)} %bitcast.236), custom_call_target="tpu_custom_call" | custom-call | flops 32212254720 | bytes 1 | tf_op jit(solution)/shard_map/attend_back/pallas_call | solution.py:238
  561.8 11.1 %fusion.71 = (bf16[2048]{0:T(1024)(128)(2,1)S(1)}, bf16[2048]{0:T(1024)(128)(2,1)S(1)}, bf16[1024,2048]{1,0:T(8,128)(2,1)}) fusion(f32[1024]{0:T(1024)S(1)} %copy-done.132, f32[1024]{0:T(1024)S(1)} %copy-done.127, bf16[1024,2048]{1,0:T(8,128)(2,1)} %copy-done.3, bf16[1024,1536]{1,0:T(8,128)(2,1)S(1)} %get-tuple-element.143.refs_1_, ...), kind=kOutput, calls=%fused_computation.284 | convolution fusion | flops 6469709824 | bytes 17842176 | tf_op jit(solution)/shard_map/dot_general | solution.py:31
  580.3 9.6 %fusion.68 = f32[2048,1536]{0,1:T(8,128)S(1)} fusion(bf16[1024,1536]{1,0:T(8,128)(2,1)S(1)} %get-tuple-element.150, bf16[1024,2048]{1,0:T(8,128)(2,1)} %copy-done.3, f32[2048]{0:T(1024)S(1)} %bitcast.293, f32[2048]{0:T(1024)S(1)} %bitcast.277, f32[1024]{0:T(1024)S(1)} %copy-done.132, f32[1024]{0:T(1024)S(1)} %copy-done.127), kind=kOutput, calls=%fused_computation.283 | convolution fusion | flops 6455033856 | bytes 19947520 | tf_op jit(solution)/shard_map/dot_general | solution.py:27
  589.9 4.6 copy-done.108
  595.1 10.9 %fusion.84 = f32[1024,2048]{1,0:T(8,128)} fusion(bf16[1024,1024]{1,0:T(8,128)(2,1)} %copy-done.136, bf16[1024,2048]{1,0:T(8,128)(2,1)} %collective-permute-done.30), kind=kOutput, calls=%fused_computation.297 | convolution fusion | flops 4294967296 | bytes 14680064 | tf_op jit(solution)/shard_map/dot_general | solution.py:23
  613.3 7.8 add_convert_fusion
  624.2 6.9 collective-permute-done.50
  631.7 15.4 %collective-permute-done.49 = bf16[512,768]{0,1:T(8,128)(2,1)S(1)} collective-permute-done((bf16[512,768]{0,1:T(8,128)(2,1)S(1)}, bf16[512,768]{0,1:T(8,128)(2,1)S(1)}, u32[]{:S(2)}, u32[]{:S(2)}) %collective-permute-start.49) | collective-permute-done | bytes 786464 | tf_op jit(solution)/shard_map/ppermute | solution.py:40
  659.9 11.1 %collective-permute-done.52.refs_3_ = bf16[4,256,512]{2,1,0:T(8,128)(2,1)} collective-permute-done((bf16[4,256,512]{2,1,0:T(8,128)(2,1)}, bf16[4,256,512]{2,1,0:T(8,128)(2,1)}, u32[]{:S(2)}, u32[]{:S(2)}) %collective-permute-start.52) | collective-permute-done | bytes 1048608 | tf_op jit(solution)/shard_map/ppermute | solution.py:51
  671.0 23.7 %collective-permute-done.54.refs_10_ = bf16[1024,512]{1,0:T(8,128)(2,1)} collective-permute-done((bf16[1024,512]{1,0:T(8,128)(2,1)}, bf16[1024,512]{1,0:T(8,128)(2,1)}, u32[]{:S(2)}, u32[]{:S(2)}) %collective-permute-start.54) | collective-permute-done | bytes 1048608 | tf_op jit(solution)/shard_map/ppermute | solution.py:40
  694.7 40.5 %reduce-scatter.9.cloned.1.call-done.refs_0_ = bf16[272,2048]{1,0:T(8,128)(2,1)} async-done(((bf16[1088,2048]{1,0:T(8,128)(2,1)}), bf16[272,2048]{1,0:T(8,128)(2,1)}) %reduce-scatter.9.cloned.1.call-update) | async-done | bytes 1114128 | tf_op jit(solution)/shard_map/reduce_scatter | solution.py:516
  746.0 3.5 add_convert_fusion.5
  752.6 4.5 convert_element_type.273
  769.0 28.2 %collective-permute-done.66.refs_3_ = bf16[4,256,512]{2,1,0:T(8,128)(2,1)S(1)} collective-permute-done((bf16[4,256,512]{2,1,0:T(8,128)(2,1)}, bf16[4,256,512]{2,1,0:T(8,128)(2,1)S(1)}, u32[]{:S(2)}, u32[]{:S(2)}) %collective-permute-start.66) | collective-permute-done | bytes 1048608 | tf_op jit(solution)/shard_map/ppermute | solution.py:51
  802.9 4.0 fusion.32
  807.5 3.8 collective-permute-done.62
  817.0 15.3 %collective-permute-done.56 = bf16[256,2048]{1,0:T(8,128)(2,1)} collective-permute-done((bf16[256,2048]{1,0:T(8,128)(2,1)}, bf16[256,2048]{1,0:T(8,128)(2,1)}, u32[]{:S(2)}, u32[]{:S(2)}) %collective-permute-start.56) | collective-permute-done | bytes 1048608 | tf_op jit(solution)/shard_map/ppermute | solution.py:40
  841.4 4.5 copy.226
  854.6 28.7 %all-gather.10.cloned.1.call-done = bf16[2048,1024]{1,0:T(8,128)(2,1)} async-done(((bf16[2048,256]{1,0:T(8,128)(2,1)}), bf16[2048,1024]{1,0:T(8,128)(2,1)}) %all-gather.10.cloned.1.call-update) | async-done | bytes 4194320 | tf_op jit(solution)/shard_map/all_gather | solution.py:551
  (641 shorter events, 328.5 us)
Async XLA Ops:
  7.2 86.7 %all-gather.12.cloned.1.call-start = ((), (), s32[]{:S(2)}) async-start(), calls=%async_computation.11 | async-start | bytes 5242880 | tf_op jit(solution)/shard_map/all_gather | solution.py:342
  10.3 306.3 %all-gather.6.cloned.1.call-start = ((), (), s32[]{:S(2)}) async-start(), calls=%async_computation.4 | async-start | bytes 5242880 | tf_op jit(solution)/shard_map/all_gather | solution.py:405
  17.9 21.7 %collective-permute-start = (bf16[544,768]{1,0:T(8,128)(2,1)}, bf16[544,768]{1,0:T(8,128)(2,1)S(1)}, u32[]{:S(2)}, u32[]{:S(2)}) collective-permute-start(bf16[544,768]{1,0:T(8,128)(2,1)} %maximum_maximum_fusion), channel_id=1, source_target_pairs={{0,8},{8,0},{16,24},{24,16},{1,9},{9,1},{17,25},{25,17},{2,10},{10... | collective-permute-start | bytes 2506760 | tf_op jit(solution)/shard_map/ppermute | solution.py:40
  61.2 47.7 %collective-permute-start.4 = (bf16[2048,768]{1,0:T(8,128)(2,1)}, bf16[2048,768]{1,0:T(8,128)(2,1)}, u32[]{:S(2)}, u32[]{:S(2)}) collective-permute-start(bf16[2048,768]{1,0:T(8,128)(2,1)} %fusion.50), channel_id=1, source_target_pairs={{0,1},{1,0},{2,3},{3,2},{4,5},{5,4},{6,7},{7,6},{8,9},{9,8},{10,11... | collective-permute-start | bytes 9437192 | tf_op jit(solution)/shard_map/ppermute | solution.py:35
  61.2 60.0 %collective-permute-start.6 = (bf16[1024,512]{1,0:T(8,128)(2,1)}, bf16[1024,512]{1,0:T(8,128)(2,1)}, u32[]{:S(2)}, u32[]{:S(2)}) collective-permute-start(bf16[1024,512]{1,0:T(8,128)(2,1)} %param.23), channel_id=1, source_target_pairs={{0,8},{8,0},{16,24},{24,16},{1,9},{9,1},{17,25},{25,17},{2,10},{10... | collective-permute-start | bytes 3145736 | tf_op jit(solution)/shard_map/ppermute | solution.py:40
  62.6 58.5 %collective-permute-start.7 = (bf16[1024,512]{1,0:T(8,128)(2,1)}, bf16[1024,512]{1,0:T(8,128)(2,1)}, u32[]{:S(2)}, u32[]{:S(2)}) collective-permute-start(bf16[1024,512]{1,0:T(8,128)(2,1)} %param.23), channel_id=1, source_target_pairs={{0,16},{8,24},{16,0},{24,8},{1,17},{9,25},{17,1},{25,9},{2,18},{10... | collective-permute-start | bytes 3145736 | tf_op jit(solution)/shard_map/ppermute | solution.py:40
  68.3 52.8 %collective-permute-start.8 = (bf16[512,1024]{1,0:T(8,128)(2,1)}, bf16[512,1024]{1,0:T(8,128)(2,1)}, u32[]{:S(2)}, u32[]{:S(2)}) collective-permute-start(bf16[512,1024]{1,0:T(8,128)(2,1)} %get-tuple-element.98), channel_id=1, source_target_pairs={{0,8},{8,0},{16,24},{24,16},{1,9},{9,1},{17,25},{25,17},{2,10},{10... | collective-permute-start | bytes 3145736 | tf_op jit(solution)/shard_map/ppermute | solution.py:40
  70.8 50.4 %collective-permute-start.9 = (bf16[512,1024]{1,0:T(8,128)(2,1)}, bf16[512,1024]{1,0:T(8,128)(2,1)}, u32[]{:S(2)}, u32[]{:S(2)}) collective-permute-start(bf16[512,1024]{1,0:T(8,128)(2,1)} %get-tuple-element.99), channel_id=1, source_target_pairs={{0,16},{8,24},{16,0},{24,8},{1,17},{9,25},{17,1},{25,9},{2,18},{10... | collective-permute-start | bytes 3145736 | tf_op jit(solution)/shard_map/ppermute | solution.py:40
  108.9 25.9 %collective-permute-start.10 = (bf16[512,1024]{1,0:T(8,128)(2,1)S(1)}, bf16[512,1024]{1,0:T(8,128)(2,1)S(1)}, u32[]{:S(2)}, u32[]{:S(2)}) collective-permute-start(bf16[512,1024]{1,0:T(8,128)(2,1)S(1)} %copy-done.51), channel_id=1, source_target_pairs={{0,24},{8,16},{16,8},{24,0},{1,25},{9,17},{17,9},{25,1},{2,26},{10... | collective-permute-start | bytes 3145736 | tf_op jit(solution)/shard_map/ppermute | solution.py:40
  154.7 55.0 %collective-permute-start.13 = (bf16[1024,2048]{1,0:T(8,128)(2,1)}, bf16[1024,2048]{1,0:T(8,128)(2,1)}, u32[]{:S(2)}, u32[]{:S(2)}) collective-permute-start(bf16[1024,2048]{1,0:T(8,128)(2,1)} %maximum_dynamic-update-slice_fusion), channel_id=1, source_target_pairs={{0,1},{1,0},{2,3},{3,2},{4,5},{5,4},{6,7},{7,6},{8,9},{9,8},{10,11... | collective-permute-start | bytes 12582920 | tf_op jit(solution)/shard_map/ppermute | solution.py:35
  155.4 23.5 %collective-permute-start.14 = (bf16[256,512]{1,0:T(8,128)(2,1)S(1)}, bf16[256,512]{1,0:T(8,128)(2,1)S(1)}, u32[]{:S(2)}, u32[]{:S(2)}) collective-permute-start(bf16[256,512]{1,0:T(8,128)(2,1)S(1)} %get-tuple-element.106), channel_id=1, source_target_pairs={{0,8},{8,0},{16,24},{24,16},{1,9},{9,1},{17,25},{25,17},{2,10},{10... | collective-permute-start | bytes 786440 | tf_op jit(solution)/shard_map/ppermute | solution.py:40
  156.9 22.0 %collective-permute-start.15 = (bf16[256,512]{1,0:T(8,128)(2,1)S(1)}, bf16[256,512]{1,0:T(8,128)(2,1)S(1)}, u32[]{:S(2)}, u32[]{:S(2)}) collective-permute-start(bf16[256,512]{1,0:T(8,128)(2,1)S(1)} %get-tuple-element.107), channel_id=1, source_target_pairs={{0,16},{8,24},{16,0},{24,8},{1,17},{9,25},{17,1},{25,9},{2,18},{10... | collective-permute-start | bytes 786440 | tf_op jit(solution)/shard_map/ppermute | solution.py:40
  179.0 30.6 %collective-permute-start.20 = (bf16[256,2048]{1,0:T(8,128)(2,1)S(1)}, bf16[256,2048]{1,0:T(8,128)(2,1)S(1)}, u32[]{:S(2)}, u32[]{:S(2)}) collective-permute-start(bf16[256,2048]{1,0:T(8,128)(2,1)S(1)} %get-tuple-element.110), channel_id=1, source_target_pairs={{0,8},{8,0},{16,24},{24,16},{1,9},{9,1},{17,25},{25,17},{2,10},{10... | collective-permute-start | bytes 3145736 | tf_op jit(solution)/shard_map/ppermute | solution.py:40
  180.6 29.1 %collective-permute-start.21 = (bf16[256,2048]{1,0:T(8,128)(2,1)S(1)}, bf16[256,2048]{1,0:T(8,128)(2,1)S(1)}, u32[]{:S(2)}, u32[]{:S(2)}) collective-permute-start(bf16[256,2048]{1,0:T(8,128)(2,1)S(1)} %get-tuple-element.110), channel_id=1, source_target_pairs={{0,16},{8,24},{16,0},{24,8},{1,17},{9,25},{17,1},{25,9},{2,18},{10... | collective-permute-start | bytes 3145736 | tf_op jit(solution)/shard_map/ppermute | solution.py:40
  206.2 58.2 %collective-permute-start.28 = (bf16[2048,1024]{1,0:T(8,128)(2,1)}, bf16[2048,1024]{1,0:T(8,128)(2,1)}, u32[]{:S(2)}, u32[]{:S(2)}) collective-permute-start(bf16[2048,1024]{1,0:T(8,128)(2,1)} %constant_dynamic-update-slice_fusion.16), channel_id=1, source_target_pairs={{0,1},{1,0},{2,3},{3,2},{4,5},{5,4},{6,7},{7,6},{8,9},{9,8},{10,11... | collective-permute-start | bytes 12582920 | tf_op jit(solution)/shard_map/ppermute | solution.py:35
  234.1 196.9 %reduce-scatter.5.cloned.1.call-start = ((), (), s32[]{:S(2)}) async-start(), calls=%async_computation.5 | async-start | bytes 5242880 | tf_op jit(solution)/shard_map/reduce_scatter | solution.py:442
  323.0 190.9 %reduce-scatter.7.cloned.1.call-start = ((), (), s32[]{:S(2)}) async-start(), calls=%async_computation.6 | async-start | bytes 5242880 | tf_op jit(solution)/shard_map/reduce_scatter | solution.py:449
  378.7 316.0 %all-gather.8.cloned.1.call-start = ((), (), s32[]{:S(2)}) async-start(), calls=%async_computation.8 | async-start | bytes 5242880 | tf_op jit(solution)/shard_map/all_gather | solution.py:517
  379.9 26.0 %collective-permute-start.31 = (bf16[256,2048]{1,0:T(8,128)(2,1)S(1)}, bf16[256,2048]{1,0:T(8,128)(2,1)S(1)}, u32[]{:S(2)}, u32[]{:S(2)}) collective-permute-start(bf16[256,2048]{1,0:T(8,128)(2,1)S(1)} %copy-done.62), channel_id=1, source_target_pairs={{0,8},{8,0},{16,24},{24,16},{1,9},{9,1},{17,25},{25,17},{2,10},{10... | collective-permute-start | bytes 3145736 | tf_op jit(solution)/shard_map/ppermute | solution.py:40
  381.4 47.6 %collective-permute-start.32 = (bf16[256,2048]{1,0:T(8,128)(2,1)S(1)}, bf16[256,2048]{1,0:T(8,128)(2,1)S(1)}, u32[]{:S(2)}, u32[]{:S(2)}) collective-permute-start(bf16[256,2048]{1,0:T(8,128)(2,1)S(1)} %copy-done.60), channel_id=1, source_target_pairs={{0,16},{8,24},{16,0},{24,8},{1,17},{9,25},{17,1},{25,9},{2,18},{10... | collective-permute-start | bytes 3145736 | tf_op jit(solution)/shard_map/ppermute | solution.py:40
  382.9 47.2 %collective-permute-start.33 = (bf16[256,2048]{1,0:T(8,128)(2,1)S(1)}, bf16[256,2048]{1,0:T(8,128)(2,1)S(1)}, u32[]{:S(2)}, u32[]{:S(2)}) collective-permute-start(bf16[256,2048]{1,0:T(8,128)(2,1)S(1)} %copy-done.58), channel_id=1, source_target_pairs={{0,24},{8,16},{16,8},{24,0},{1,25},{9,17},{17,9},{25,1},{2,26},{10... | collective-permute-start | bytes 3145736 | tf_op jit(solution)/shard_map/ppermute | solution.py:40
  449.9 55.7 %collective-permute-start.46 = (bf16[1024,2048]{1,0:T(8,128)(2,1)}, bf16[1024,2048]{1,0:T(8,128)(2,1)}, u32[]{:S(2)}, u32[]{:S(2)}) collective-permute-start(bf16[1024,2048]{1,0:T(8,128)(2,1)} %convolution_convert_fusion), channel_id=1, source_target_pairs={{0,1},{1,0},{2,3},{3,2},{4,5},{5,4},{6,7},{7,6},{8,9},{9,8},{10,11... | collective-permute-start | bytes 12582920 | tf_op jit(solution)/shard_map/ppermute | solution.py:35
  463.8 37.0 %collective-permute-start.36 = (bf16[256,512]{1,0:T(8,128)(2,1)S(1)}, bf16[256,512]{1,0:T(8,128)(2,1)S(1)}, u32[]{:S(2)}, u32[]{:S(2)}) collective-permute-start(bf16[256,512]{1,0:T(8,128)(2,1)S(1)} %get-tuple-element.134), channel_id=1, source_target_pairs={{0,4},{2,6},{4,0},{6,2},{1,5},{3,7},{5,1},{7,3},{8,12},{10,14},{12... | collective-permute-start | bytes 786440 | tf_op jit(solution)/shard_map/ppermute | solution.py:45
  464.1 39.1 %collective-permute-start.37 = (bf16[256,512]{1,0:T(8,128)(2,1)S(1)}, bf16[256,512]{1,0:T(8,128)(2,1)}, u32[]{:S(2)}, u32[]{:S(2)}) collective-permute-start(bf16[256,512]{1,0:T(8,128)(2,1)S(1)} %get-tuple-element.135), channel_id=1, source_target_pairs={{0,2},{2,4},{4,6},{6,0},{1,3},{3,5},{5,7},{7,1},{8,10},{10,12},{12... | collective-permute-start | bytes 786440 | tf_op jit(solution)/shard_map/ppermute | solution.py:45
  466.3 45.5 %collective-permute-start.38 = (bf16[256,512]{1,0:T(8,128)(2,1)S(1)}, bf16[256,512]{1,0:T(8,128)(2,1)S(1)}, u32[]{:S(2)}, u32[]{:S(2)}) collective-permute-start(bf16[256,512]{1,0:T(8,128)(2,1)S(1)} %get-tuple-element.219), channel_id=1, source_target_pairs={{0,8},{8,0},{16,24},{24,16},{1,9},{9,1},{17,25},{25,17},{2,10},{10... | collective-permute-start | bytes 786440 | tf_op jit(solution)/shard_map/ppermute | solution.py:40
  480.2 31.6 %collective-permute-start.39 = (bf16[256,512]{1,0:T(8,128)(2,1)S(1)}, bf16[256,512]{1,0:T(8,128)(2,1)S(1)}, u32[]{:S(2)}, u32[]{:S(2)}) collective-permute-start(bf16[256,512]{1,0:T(8,128)(2,1)S(1)} %get-tuple-element.218), channel_id=1, source_target_pairs={{0,16},{8,24},{16,0},{24,8},{1,17},{9,25},{17,1},{25,9},{2,18},{10... | collective-permute-start | bytes 786440 | tf_op jit(solution)/shard_map/ppermute | solution.py:40
  515.4 35.8 %collective-permute-start.41 = (bf16[4,256,512]{2,1,0:T(8,128)(2,1)S(1)}, bf16[4,256,512]{2,1,0:T(8,128)(2,1)S(1)}, u32[]{:S(2)}, u32[]{:S(2)}) collective-permute-start(bf16[4,256,512]{2,1,0:T(8,128)(2,1)S(1)} %bitcast_dynamic-update-slice_fusion.4), channel_id=1, source_target_pairs={{0,2},{2,4},{4,6},{1,3},{3,5},{5,7},{8,10},{10,12},{12,14},{9,11},... | collective-permute-start | bytes 3145736 | tf_op jit(solution)/shard_map/ppermute | solution.py:50
  516.8 34.4 %collective-permute-start.42 = (bf16[4,256,512]{2,1,0:T(8,128)(2,1)S(1)}, bf16[4,256,512]{2,1,0:T(8,128)(2,1)}, u32[]{:S(2)}, u32[]{:S(2)}) collective-permute-start(bf16[4,256,512]{2,1,0:T(8,128)(2,1)S(1)} %bitcast_dynamic-update-slice_fusion.4), channel_id=1, source_target_pairs={{2,0},{4,2},{6,4},{3,1},{5,3},{7,5},{10,8},{12,10},{14,12},{11,9},... | collective-permute-start | bytes 3145736 | tf_op jit(solution)/shard_map/ppermute | solution.py:51
  518.2 33.0 %collective-permute-start.43 = (bf16[1,128,1024]{2,1,0:T(8,128)(2,1)S(1)}, bf16[1,128,1024]{2,1,0:T(8,128)(2,1)S(1)}, u32[]{:S(2)}, u32[]{:S(2)}) collective-permute-start(bf16[1,128,1024]{2,1,0:T(8,128)(2,1)S(1)} %get-tuple-element.215), channel_id=1, source_target_pairs={{0,8},{8,0},{16,24},{24,16},{1,9},{9,1},{17,25},{25,17},{2,10},{10... | collective-permute-start | bytes 786440 | tf_op jit(solution)/shard_map/ppermute | solution.py:40
  518.8 32.4 %collective-permute-start.44 = (bf16[1,128,1024]{2,1,0:T(8,128)(2,1)S(1)}, bf16[1,128,1024]{2,1,0:T(8,128)(2,1)S(1)}, u32[]{:S(2)}, u32[]{:S(2)}) collective-permute-start(bf16[1,128,1024]{2,1,0:T(8,128)(2,1)S(1)} %get-tuple-element.214), channel_id=1, source_target_pairs={{0,16},{8,24},{16,0},{24,8},{1,17},{9,25},{17,1},{25,9},{2,18},{10... | collective-permute-start | bytes 786440 | tf_op jit(solution)/shard_map/ppermute | solution.py:40
  519.5 31.7 %collective-permute-start.45 = (bf16[1,128,1024]{2,1,0:T(8,128)(2,1)S(1)}, bf16[1,128,1024]{2,1,0:T(8,128)(2,1)S(1)}, u32[]{:S(2)}, u32[]{:S(2)}) collective-permute-start(bf16[1,128,1024]{2,1,0:T(8,128)(2,1)S(1)} %get-tuple-element.213), channel_id=1, source_target_pairs={{0,24},{8,16},{16,8},{24,0},{1,25},{9,17},{17,9},{25,1},{2,26},{10... | collective-permute-start | bytes 786440 | tf_op jit(solution)/shard_map/ppermute | solution.py:40
  561.7 173.5 %reduce-scatter.9.cloned.1.call-start = ((), (), s32[]{:S(2)}) async-start(), calls=%async_computation.7 | async-start | bytes 5570560 | tf_op jit(solution)/shard_map/reduce_scatter | solution.py:516
  579.6 220.0 %reduce-scatter.11.cloned.1.call-start = ((), (), s32[]{:S(2)}) async-start(), calls=%async_computation.9 | async-start | bytes 1310720 | tf_op jit(solution)/shard_map/reduce_scatter | solution.py:541
  610.6 36.4 %collective-permute-start.49 = (bf16[512,768]{0,1:T(8,128)(2,1)S(1)}, bf16[512,768]{0,1:T(8,128)(2,1)S(1)}, u32[]{:S(2)}, u32[]{:S(2)}) collective-permute-start(bf16[512,768]{0,1:T(8,128)(2,1)S(1)} %get-tuple-element.191), channel_id=1, source_target_pairs={{0,16},{8,24},{16,0},{24,8},{1,17},{9,25},{17,1},{25,9},{2,18},{10... | collective-permute-start | bytes 2359304 | tf_op jit(solution)/shard_map/ppermute | solution.py:40
  611.9 36.2 %collective-permute-start.48 = (bf16[512,768]{0,1:T(8,128)(2,1)S(1)}, bf16[512,768]{0,1:T(8,128)(2,1)S(1)}, u32[]{:S(2)}, u32[]{:S(2)}) collective-permute-start(bf16[512,768]{0,1:T(8,128)(2,1)S(1)} %get-tuple-element.189), channel_id=1, source_target_pairs={{0,8},{8,0},{16,24},{24,16},{1,9},{9,1},{17,25},{25,17},{2,10},{10... | collective-permute-start | bytes 2359304 | tf_op jit(solution)/shard_map/ppermute | solution.py:40
  621.1 38.8 %collective-permute-start.51 = (bf16[4,256,512]{2,1,0:T(8,128)(2,1)S(1)}, bf16[4,256,512]{2,1,0:T(8,128)(2,1)}, u32[]{:S(2)}, u32[]{:S(2)}) collective-permute-start(bf16[4,256,512]{2,1,0:T(8,128)(2,1)S(1)} %copy-done.23), channel_id=1, source_target_pairs={{2,4},{4,6},{3,5},{5,7},{10,12},{12,14},{11,13},{13,15},{18,20},{2... | collective-permute-start | bytes 3145736 | tf_op jit(solution)/shard_map/ppermute | solution.py:50
  622.8 48.2 %collective-permute-start.52 = (bf16[4,256,512]{2,1,0:T(8,128)(2,1)}, bf16[4,256,512]{2,1,0:T(8,128)(2,1)}, u32[]{:S(2)}, u32[]{:S(2)}) collective-permute-start(bf16[4,256,512]{2,1,0:T(8,128)(2,1)} %get-tuple-element.152), channel_id=1, source_target_pairs={{2,0},{4,2},{3,1},{5,3},{10,8},{12,10},{11,9},{13,11},{18,16},{20,... | collective-permute-start | bytes 3145736 | tf_op jit(solution)/shard_map/ppermute | solution.py:51
  631.1 39.9 %collective-permute-start.53 = (bf16[1024,512]{1,0:T(8,128)(2,1)}, bf16[1024,512]{1,0:T(8,128)(2,1)}, u32[]{:S(2)}, u32[]{:S(2)}) collective-permute-start(bf16[1024,512]{1,0:T(8,128)(2,1)} %get-tuple-element.153), channel_id=1, source_target_pairs={{0,8},{8,0},{16,24},{24,16},{1,9},{9,1},{17,25},{25,17},{2,10},{10... | collective-permute-start | bytes 3145736 | tf_op jit(solution)/shard_map/ppermute | solution.py:40
  647.1 47.6 %collective-permute-start.54 = (bf16[1024,512]{1,0:T(8,128)(2,1)}, bf16[1024,512]{1,0:T(8,128)(2,1)}, u32[]{:S(2)}, u32[]{:S(2)}) collective-permute-start(bf16[1024,512]{1,0:T(8,128)(2,1)} %get-tuple-element.154), channel_id=1, source_target_pairs={{0,16},{8,24},{16,0},{24,8},{1,17},{9,25},{17,1},{25,9},{2,18},{10... | collective-permute-start | bytes 3145736 | tf_op jit(solution)/shard_map/ppermute | solution.py:40
  648.0 46.7 %collective-permute-start.55 = (bf16[1024,512]{1,0:T(8,128)(2,1)}, bf16[1024,512]{1,0:T(8,128)(2,1)}, u32[]{:S(2)}, u32[]{:S(2)}) collective-permute-start(bf16[1024,512]{1,0:T(8,128)(2,1)} %get-tuple-element.155), channel_id=1, source_target_pairs={{0,24},{8,16},{16,8},{24,0},{1,25},{9,17},{17,9},{25,1},{2,26},{10... | collective-permute-start | bytes 3145736 | tf_op jit(solution)/shard_map/ppermute | solution.py:40
  749.6 133.8 %all-gather.10.cloned.1.call-start = ((), (), s32[]{:S(2)}) async-start(), calls=%async_computation.10 | async-start | bytes 5242880 | tf_op jit(solution)/shard_map/all_gather | solution.py:551
  760.5 36.7 %collective-permute-start.66 = (bf16[4,256,512]{2,1,0:T(8,128)(2,1)}, bf16[4,256,512]{2,1,0:T(8,128)(2,1)S(1)}, u32[]{:S(2)}, u32[]{:S(2)}) collective-permute-start(bf16[4,256,512]{2,1,0:T(8,128)(2,1)} %get-tuple-element.168), channel_id=1, source_target_pairs={{2,0},{3,1},{10,8},{11,9},{18,16},{19,17},{26,24},{27,25}} | collective-permute-start | bytes 3145736 | tf_op jit(solution)/shard_map/ppermute | solution.py:51
  761.8 55.2 %collective-permute-start.58 = (bf16[256,2048]{1,0:T(8,128)(2,1)}, bf16[256,2048]{1,0:T(8,128)(2,1)}, u32[]{:S(2)}, u32[]{:S(2)}) collective-permute-start(bf16[256,2048]{1,0:T(8,128)(2,1)} %get-tuple-element.163), channel_id=1, source_target_pairs={{0,24},{8,16},{16,8},{24,0},{1,25},{9,17},{17,9},{25,1},{2,26},{10... | collective-permute-start | bytes 3145736 | tf_op jit(solution)/shard_map/ppermute | solution.py:40
  764.3 52.7 %collective-permute-start.57 = (bf16[256,2048]{1,0:T(8,128)(2,1)}, bf16[256,2048]{1,0:T(8,128)(2,1)}, u32[]{:S(2)}, u32[]{:S(2)}) collective-permute-start(bf16[256,2048]{1,0:T(8,128)(2,1)} %get-tuple-element.162), channel_id=1, source_target_pairs={{0,16},{8,24},{16,0},{24,8},{1,17},{9,25},{17,1},{25,9},{2,18},{10... | collective-permute-start | bytes 3145736 | tf_op jit(solution)/shard_map/ppermute | solution.py:40
  764.9 42.0 %collective-permute-start.63 = (f32[1,4096]{1,0:T(1,128)S(1)}, f32[1,4096]{1,0:T(1,128)S(1)}, u32[]{:S(2)}, u32[]{:S(2)}) collective-permute-start(f32[1,4096]{1,0:T(1,128)S(1)} %get-tuple-element.237), channel_id=1, source_target_pairs={{0,24},{8,16},{16,8},{24,0},{1,25},{9,17},{17,9},{25,1},{2,26},{10... | collective-permute-start | bytes 49160 | tf_op jit(solution)/shard_map/ppermute | solution.py:40
  768.4 43.0 %collective-permute-start.62 = (f32[1,4096]{1,0:T(1,128)S(1)}, f32[1,4096]{1,0:T(1,128)S(1)}, u32[]{:S(2)}, u32[]{:S(2)}) collective-permute-start(f32[1,4096]{1,0:T(1,128)S(1)} %get-tuple-element.236), channel_id=1, source_target_pairs={{0,16},{8,24},{16,0},{24,8},{1,17},{9,25},{17,1},{25,9},{2,18},{10... | collective-permute-start | bytes 49160 | tf_op jit(solution)/shard_map/ppermute | solution.py:40
  807.0 25.3 %collective-permute-start.56 = (bf16[256,2048]{1,0:T(8,128)(2,1)}, bf16[256,2048]{1,0:T(8,128)(2,1)}, u32[]{:S(2)}, u32[]{:S(2)}) collective-permute-start(bf16[256,2048]{1,0:T(8,128)(2,1)} %copy-done.53), channel_id=1, source_target_pairs={{0,8},{8,0},{16,24},{24,16},{1,9},{9,1},{17,25},{25,17},{2,10},{10... | collective-permute-start | bytes 3145736 | tf_op jit(solution)/shard_map/ppermute | solution.py:40
  811.3 34.6 %collective-permute-start.60 = (bf16[256,2048]{1,0:T(8,128)(2,1)}, bf16[256,2048]{1,0:T(8,128)(2,1)}, u32[]{:S(2)}, u32[]{:S(2)}) collective-permute-start(bf16[256,2048]{1,0:T(8,128)(2,1)} %fusion.32), channel_id=1, source_target_pairs={{0,1},{1,0},{2,3},{3,2},{4,5},{5,4},{6,7},{7,6},{8,9},{9,8},{10,11... | collective-permute-start | bytes 3145736 | tf_op jit(solution)/shard_map/ppermute | solution.py:35
  (167 other events, 1431.9 us)
Sparse Core Ops, SparseCore 0:
  10.4 83.4 all-gather.11
  234.3 82.2 all-gather.5
  323.1 75.4 reduce-scatter.4
  401.5 87.2 reduce-scatter.6
  561.8 85.6 all-gather.7
  650.3 84.8 reduce-scatter.8
  749.7 30.5 reduce-scatter.10
  803.0 80.2 all-gather.9

commit v3 on v2

--- a/solution.py
+++ b/solution.py
@@ -334,10 +334,7 @@
         axis=0,
     )
     up_pieces = [pick(w_up, k, 1) for k in range(groups)]
-    down_rows = lax.dynamic_index_in_dim(
-        w_down.reshape(groups, planes, hidden // planes, part), plane, 1, keepdims=False
-    )
-    down_pieces = [pick(down_rows, k, 0)[0] for k in range(groups)]
+    down_pieces = [pick(w_down, k, 0) for k in range(groups)]
 
     tree = lax.all_gather(mine, "context", axis=0, tiled=True)
     head_first = gather_first(chosen)
@@ -385,14 +382,16 @@
     tree_unit, _ = normalise(tree.astype(F32))
     normed = (tree_unit * gain_one + shift_one).astype(BF16)
     qkv = (dot_nn(normed, w_heads) + head_shift).astype(BF16)
-    qkv, *rest = gate([qkv, *out_first, *down_pieces[1:]], *up_blocks[1:])
-    out_first, down_pieces[1:] = rest[: len(out_first)], rest[len(out_first) :]
+    qkv, *out_first = gate([qkv, *out_first])
     out_second = gather_second(out_first)
-    down_blocks = down_pieces[:1] + send_blocks(down_pieces[1:])
     mixed = attend(order, slopes, qkv)
-    mixed, mine_cot, *down_blocks = gate([mixed, mine_cot, *down_blocks], *out_second)
+    mixed, mine_cot, *rest = gate(
+        [mixed, mine_cot, *down_pieces, *out_first, *out_second, *up_blocks]
+    )
+    down_pieces, rest = rest[:groups], rest[groups:]
+    out_first, rest = rest[: len(out_first)], rest[len(out_first) :]
+    out_second, up_blocks = rest[: len(out_second)], rest[len(out_second) :]
     out_own = place(gather_blocks(mine_out, out_first, out_second), 1)
-    down_rows = place(down_blocks, 1)
     up_own = place(up_blocks, 0)
     up_other, out_other = swap_cores(up_own), swap_cores(out_own)
 
@@ -400,9 +399,11 @@
     for k in range(1, planes):
         arrived.append(ring_send(rows_of(mixed, k), k))
     cot_first = gather_first(mine_cot)
+    down_pieces = list(gate(down_pieces, arrived[1]))
+    early = range(1, 3) if groups == 4 else range(1, groups)
+    down_blocks = down_pieces[:1] + [xor_send(down_pieces[k], k) for k in early]
     out_other, *rest = gate([out_other, *arrived, *cot_first])
     arrived, cot_first = rest[:planes], rest[planes:]
-    down_own = lax.all_gather(down_rows, "context", axis=0, tiled=True)
     cot_second = gather_second(cot_first)
     attended = jnp.stack(arrived[::-1], axis=0)
     attended = jnp.roll(attended, plane + 1, axis=0)
@@ -413,9 +414,12 @@
     )
     unit_two, scale_two = normalise(middle)
     normed_two = (unit_two * gain_two + shift_two).astype(BF16)
-    (normed_two,) = gate([normed_two], *cot_second)
-    two_first = gate(gather_first(normed_two))
+    (normed_two,) = gate([normed_two], *cot_second, *down_blocks[1:])
+    two_first = gather_first(normed_two)
+    rest = gate([*two_first, *down_pieces])
+    two_first, down_pieces = rest[: len(two_first)], rest[len(two_first) :]
     two_second = gather_second(two_first)
+    down_blocks += [xor_send(down_pieces[k], k) for k in range(len(down_blocks), groups)]
     all_two = jnp.concatenate(gather_blocks(normed_two, two_first, two_second), axis=0)
     all_cot = jnp.concatenate(gather_blocks(mine_cot, cot_first, cot_second), axis=0)
 
@@ -429,10 +433,11 @@
     def slope_of(pre):
         return normal_cdf(pre) + pre * normal_pdf(pre)
 
-    (down_own,) = gate([down_own], grad_down)
+    (down_blocks[-1],) = gate(down_blocks[-1:], grad_down)
+    down_own = place(down_blocks, 1)
     down_other = swap_cores(down_own)
+    back_own = (dot_nt(all_cot, down_own) * slope_of(pre_own)).astype(BF16)
     back_other = (dot_nt(all_cot, down_other) * slope_of(pre_other)).astype(BF16)
-    back_own = (dot_nt(all_cot, down_own) * slope_of(pre_own)).astype(BF16)
 
     grad_two = (dot_nt(back_own, up_own) + dot_nt(back_other, up_other)).astype(BF16)
     back_other_in = back_other
@@ -442,6 +447,7 @@
     grad_down = lax.psum_scatter(grad_down, "context", scatter_dimension=0, tiled=True)
     grad_two = send_blocks(sent)
     grad_up = swap_cores(dot_tn(all_two, back_other).astype(BF16))
+    (grad_up,) = gate([grad_up], grad_two[0])
     grad_up = (dot_tn(all_two, back_own) + grad_up.astype(F32)).astype(BF16)
     grad_up = grad_up.reshape(groups, planes, part // planes, hidden).transpose(1, 0, 2, 3)
     grad_up = grad_up.reshape(width, hidden)
@@ -460,30 +466,40 @@
     )
     grad_mixed = grad_mixed.transpose(2, 0, 1, 3).reshape(planes, rows, 2 * columns)
     grad_mixed = jnp.roll(grad_mixed, -plane, axis=0)
-    grad_down = exchange(grad_down, 1)
-    grad_mixed = gate([grad_mixed[k] for k in range(planes)])
+    grad_out = swap_cores(dot_tn(attended[1], grad_branch).astype(BF16))
+    grad_out = dot_tn(attended[0], grad_branch) + grad_out.astype(F32)
+    out_own_block, *rest = gate(
+        [pick(grad_out, 0, 1)]
+        + [pick(grad_out, k, 1).astype(BF16) for k in range(1, groups)]
+        + [grad_mixed[k] for k in range(planes)]
+    )
+    out_blocks, grad_mixed = rest[: groups - 1], rest[groups - 1 :]
 
     back_rows = [grad_mixed[0]]
     for k in range(1, planes):
         back_rows.append(ring_send(grad_mixed[k], k))
-    grad_out = swap_cores(dot_tn(attended[1], grad_branch).astype(BF16))
-    grad_out = dot_tn(attended[0], grad_branch) + grad_out.astype(F32)
+    grad_out = add_up(out_own_block, send_blocks(out_blocks)).astype(BF16)
     grad_tree = jnp.roll(jnp.stack(back_rows[:1] + back_rows[:0:-1]), plane, axis=0)
     grad_tree = grad_tree.reshape(planes * rows, 2 * columns)
-    out_blocks = [pick(grad_out, k, 1) for k in range(groups)]
-    out_own_block, out_blocks = out_blocks[0], [piece.astype(BF16) for piece in out_blocks[1:]]
-    grad_tree, grad_up, *grad_down = gate([grad_tree, grad_up, *grad_down])
-    grad_down = place([piece[None] for piece in grad_down], 0)
-
+    grad_tree, grad_up, grad_down, grad_out = gate([grad_tree, grad_up, grad_down, grad_out])
+    grad_out = lax.psum_scatter(grad_out, "context", scatter_dimension=0, tiled=True)
+
+    lines = grad_down.shape[0]
+    grad_up = grad_up.reshape(groups, lines // (hidden // part), hidden)
+    both = []
+    for k in range(groups):
+        piece = pick(grad_up, k, 0)[0]
+        piece = [piece[:, i : i + part] for i in range(0, hidden, part)]
+        both.append(jnp.concatenate([pick(grad_down, k, 1), *piece]))
+    both = both[:1] + send_blocks(both[1:])
+    grad_qkv = attend_back(order, slopes, qkv, grad_tree)
+    grad_qkv, grad_out, *both = gate([grad_qkv, grad_out, *both])
+    g_out = lax.all_gather(grad_out, "context", axis=0, tiled=True)
+    grad_down = place([piece[None, :lines] for piece in both], 0)
+    g_up = jnp.concatenate([piece[lines:] for piece in both])
+    g_up = lax.all_gather(g_up, "context", axis=0, tiled=True)
     down_up, down_down = line_step([grad_down], [grad_down])
-    grad_up = exchange(grad_up.reshape(groups, part // planes, hidden), 0)
-    grad_qkv = attend_back(order, slopes, qkv, grad_tree)
-    grad_qkv, down_up[-1], down_down[-1], *rest = gate(
-        [grad_qkv, down_up[-1], down_down[-1], *grad_up, *out_blocks]
-    )
-    grad_up, out_blocks = rest[:groups], rest[groups:]
-
-    grad_up = place([piece[0] for piece in grad_up], 1)
+
     grad_normed = dot_nt(grad_qkv, w_heads)
     head_sums = jnp.sum(grad_qkv.astype(F32), axis=0).reshape(2, pairs, 3, PAIR)
     head_sums = jnp.stack([head_sums[:, :, 0], head_sums[:, :, 2]], axis=1)
@@ -509,12 +525,11 @@
         jnp.concatenate([grad_normed[k * rows : (k + 1) * rows], sums]) for k in range(planes)
     ]
     blocks = jnp.concatenate(blocks).astype(BF16)
-    blocks, grad_qkv, down_up[-1], down_down[-1], *out_blocks = gate(
-        [blocks, grad_qkv, down_up[-1], down_down[-1], *out_blocks]
+    blocks, grad_qkv, down_up[-1], down_down[-1] = gate(
+        [blocks, grad_qkv, down_up[-1], down_down[-1]], g_out
     )
     later = zero_from(blocks)
     grad_first = lax.psum_scatter(blocks, "context", scatter_dimension=0, tiled=True)
-    g_up = lax.all_gather(grad_up, "context", axis=0, tiled=True)
 
     down_up, down_down = line_step(down_up, down_down)
     grad_heads = dot_tn(normed, grad_qkv)
@@ -524,34 +539,38 @@
     grad_heads = add_up(pick(grad_heads, 0, 0), send_blocks(head_pieces)).astype(BF16)
     grad_heads = grad_heads.reshape(part, pairs, 3, PAIR).transpose(2, 0, 1, 3)
     grad_heads = grad_heads.reshape(3 * part, columns)
-    out_blocks = send_blocks(out_blocks)
     layer_out = dot_nn(
         lax.dynamic_slice_in_dim(active_own, later, groups * rows, 0), down_own
     ) + dot_nn(lax.dynamic_slice_in_dim(active_other, later, groups * rows, 0), down_other)
     layer_out = layer_out.astype(BF16)
-    grad_first, grad_heads, down_up[-1], down_down[-1], out_own_block, *layer_blocks = gate(
-        [grad_first, grad_heads, down_up[-1], down_down[-1], out_own_block]
-        + [layer_out[k * rows : (k + 1) * rows] for k in range(groups)],
-        *out_blocks,
-        g_up,
+    grad_heads, down_up[-1], down_down[-1], *layer_blocks = gate(
+        [grad_heads, down_up[-1], down_down[-1]]
+        + [layer_out[k * rows : (k + 1) * rows] for k in range(groups)]
     )
     while len(down_up) < planes:
         down_up, down_down = line_step(down_up, down_down)
-    grad_out = add_up(out_own_block, out_blocks).astype(BF16)
-    grad_out = lax.psum_scatter(grad_out, "context", scatter_dimension=0, tiled=True)
-    layer_out = add_up(layer_blocks[0], send_blocks(layer_blocks[1:]))
-    layer_out = middle + (layer_out + down_shift)
+    layer_blocks[1:] = send_blocks(layer_blocks[1:])
+    grad_first, grad_heads, g_up, g_out = gate(
+        [grad_first, grad_heads, g_up, g_out],
+        down_up[-1],
+        down_down[-1],
+        *layer_blocks[1:],
+    )
+    layer_out = middle + (add_up(layer_blocks[0], layer_blocks[1:]) + down_shift)
     layer_out = both_micros(layer_out.astype(BF16))
-    grad_heads, grad_out = gate([grad_heads, grad_out], down_up[-1], down_down[-1])
-
-    lines = grad_out.shape[0]
-    last = [grad_heads] + [
-        grad_out[:, i : i + columns] for i in range(0, part, columns)
-    ]
-    last = lax.all_gather(jnp.concatenate(last), "context", axis=1, tiled=True)
-    g_heads = last[: 3 * part]
-    g_out = last[3 * part :].reshape(part // columns, lines, planes, columns)
-    g_out = g_out.transpose(2, 1, 0, 3).reshape(half, part)
+
+    g_heads = lax.all_gather(grad_heads, "context", axis=1, tiled=True)
+    ordered = jnp.zeros((part, groups * hidden), F32)
+    g_up = g_up.reshape(planes, groups, hidden // part, -1, part)
+    for k in range(groups):
+        for i in range(hidden // part):
+            ordered = lax.dynamic_update_slice_in_dim(
+                ordered,
+                g_up[:, k, i].reshape(part, part).astype(F32),
+                (group ^ k) * hidden + i * part,
+                1,
+            )
+    g_up = ordered
     g_down = jnp.zeros((groups, planes, hidden // planes, part), F32)
     for k, piece in enumerate(line_blocks(down_up, down_down)):
         g_down = lax.dynamic_update_slice_in_dim(
@@ -586,7 +605,7 @@
         total[6 * part : 7 * part].reshape(2, part // 2),
         g_out.astype(F32),
         wide[4],
-        g_up.astype(F32),
+        g_up,
         total[7 * part :],
         g_down.reshape(groups * hidden, part),
         wide[5],

time: 909 us -> 902 us (level)
  waiting for transfers between devices: 374 us -> 354 us
    ppermute x43 -> x40, waiting for transfers between devices: 162 us -> 195 us  [xor_send(): return lax.ppermute(value, 'fsdp', [(i, i ^ step) for i in range(size)])]
    reduce_scatter x1, waiting for transfers between devices: 40.5 us -> 11.1 us  [per_device(): lax.psum_scatter(blocks, 'context', scatter_dimension=0, tiled=True)]
    ppermute x3, waiting for transfers between devices: 39.3 us -> 57.5 us  [line_step(): lax.ppermute(downward[-1], 'context', [(i + 1, i) for i in range(0, size...]
    all_gather x1, waiting for transfers between devices: 21.5 us -> 7.01 us  [per_device(): tree = lax.all_gather(mine, 'context', axis=0, tiled=True)]
    ppermute x6, starting transfers between devices: 5.18 us -> 18.5 us  [ring_send(): lax.ppermute(value, 'context', [(i, (i + step) % size) for i in range(siz...]
    all_gather x3, waiting for transfers between devices: 50.8 us -> 39.3 us  [the longest x1 38.8 us: per_device(): g_heads = lax.all_gather(grad_heads, 'context', axis=1, tiled=True)]
    ppermute x43 -> x40, starting transfers between devices: 54.8 us -> 44.8 us  [xor_send(): return lax.ppermute(value, 'fsdp', [(i, i ^ step) for i in range(size)])]
    dynamic_update_slice x26 -> x22, local copies, waits for them, and re-layouts: 28.7 us -> 32.3 us  [place(): lax.dynamic_update_slice_in_dim(whole, piece, (index ^ k) * width, axis)]
  transfers between devices with their start and end apart: 75 -> 72, of which waited for: 34 -> 35; matrix products, arithmetic and copies ran while one was open for 31% -> 31% of each run, Pallas kernels for 5% -> 5%
where the time goes in v3:
time: 902 us; the launch traced here: 894 us
  waiting for transfers between devices  354 us (39%)
  local copies, waits for them, and re-layouts  197 us (22%)
  matrix products  133 us (15%)
  starting transfers between devices  76.6 us (8%)
  other arithmetic  71.3 us (8%)
  Pallas kernels  46.2 us (5%)
  between operations  16.6 us (2%)
    ppermute x40, waiting for transfers between devices, xor_send(): return lax.ppermute(value, 'fsdp', [(i, i ^ step) for i in range(size)])  195 us
    unnamed x306, local copies, waits for them, and re-layouts  104 us
    ppermute x3, waiting for transfers between devices, line_step(): lax.ppermute(downward[-1], 'context', [(i + 1, i) for i in range(0, size...  57.5 us
    dot_general x7, matrix products, dot_nt(): lax.dot_general(left, right, (((1,), (1,)), ((), ())), preferred_element_...  49.1 us
    dot_general x7, matrix products, dot_nn(): lax.dot_general(left, right, (((1,), (0,)), ((), ())), preferred_element_...  47 us
    ppermute x40, starting transfers between devices, xor_send(): return lax.ppermute(value, 'fsdp', [(i, i ^ step) for i in range(size)])  44.8 us
    ppermute x6, waiting for transfers between devices, ring_send(): lax.ppermute(value, 'context', [(i, (i + step) % size) for i in range(siz...  42.6 us
    all_gather x1, waiting for transfers between devices, per_device(): g_heads = lax.all_gather(grad_heads, 'context', axis=1, tiled=True)  38.8 us
  transfers between devices with their start and end apart: 72, of which 35 were waited for; matrix products, arithmetic and copies ran while one was open for 31% of the time, Pallas kernels for 5%

profile of v3, /device:TPU:0, one launch (start us, length us, event | category | flops | bytes accessed | tf_op | source)
XLA Modules:
  0.0 894.4 jit_solution(1639605880110353473)
XLA Ops:
  28.6 11.9 %collective-permute-done.1.refs_1_ = bf16[544,768]{1,0:T(8,128)(2,1)S(1)} collective-permute-done((bf16[544,768]{1,0:T(8,128)(2,1)}, bf16[544,768]{1,0:T(8,128)(2,1)S(1)}, u32[]{:S(2)}, u32[]{:S(2)}) %collective-permute-start.1) | collective-permute-done | bytes 835616 | tf_op jit(solution)/shard_map/ppermute | solution.py:40
  56.6 14.6 %collective-permute-done.3.refs_7_ = bf16[272,768]{1,0:T(8,128)(2,1)S(1)} collective-permute-done((bf16[272,768]{1,0:T(8,128)(2,1)S(1)}, bf16[272,768]{1,0:T(8,128)(2,1)S(1)}, u32[]{:S(2)}, u32[]{:S(2)}) %collective-permute-start.3) | collective-permute-done | bytes 417824 | tf_op jit(solution)/shard_map/ppermute | solution.py:40
  87.0 7.0 all-gather.12.cloned.1.call-done
  109.9 9.6 %add_convert_fusion.4.refs_0_ = bf16[1024,1536]{1,0:T(8,128)(2,1)S(1)} fusion(bf16[2048,768]{1,0:T(8,128)(2,1)} %collective-permute-done.4, bf16[2048,768]{1,0:T(8,128)(2,1)} %fusion.50, f32[1536]{0:T(1024)S(1)} %add.444, bf16[1024,2048]{1,0:T(8,128)(2,1)S(1)} %copy-done.4, f32[2048]{0:T(1024)S(1)} %bitcast.299, f32[2048]{0:T(1024)S(1)} %bitcast.283, ...), kind=kOutput, calls=%fused_computation.21 | convolution fusion | flops 6470762496 | bytes 13662208 | tf_op jit(solution)/shard_map/dot_general | solution.py:23
  123.4 17.9 %attend.1 = bf16[8,128,512]{2,1,0:T(8,128)(2,1)S(1)} custom-call(s32[8]{0:T(128)S(1)} %select_reduce_fusion.order, f32[8]{0:T(128)S(1)} %fusion.65.slopes, bf16[8,128,1536]{2,1,0:T(8,128)(2,1)S(1)} %bitcast.242), custom_call_target="tpu_custom_call" | custom-call | flops 17179869184 | bytes 1 | tf_op jit(solution)/shard_map/attend/pallas_call | solution.py:216
  179.7 7.2 collective-permute-done.15.refs_3_
  200.4 3.7 fusion.84
  205.9 7.4 collective-permute-done.21.refs_3_
  214.9 7.4 collective-permute-done.19.refs_1_
  229.5 16.7 %collective-permute-done.24.refs_1_ = bf16[256,2048]{1,0:T(8,128)(2,1)S(1)} collective-permute-done((bf16[256,2048]{1,0:T(8,128)(2,1)S(1)}, bf16[256,2048]{1,0:T(8,128)(2,1)S(1)}, u32[]{:S(2)}, u32[]{:S(2)}) %collective-permute-start.24) | collective-permute-done | bytes 1048608 | tf_op jit(solution)/shard_map/ppermute | solution.py:40
  249.7 8.9 collective-permute-done.26
  258.8 10.0 %multiply_convert_fusion = (bf16[1024,1024]{1,0:T(8,128)(2,1)S(1)}, f32[1024,1024]{1,0:T(8,128)}) fusion(f32[1024]{0:T(1024)S(1)} %bitcast.305, bf16[1024,2048]{1,0:T(8,128)(2,1)S(1)} %constant_dynamic-update-slice_fusion.5, bf16[2048,1024]{1,0:T(8,128)(2,1)} %collective-permute-done.28), kind=kOutput, calls=%fused_computation.36 | convolution fusion | flops 4301258752 | bytes 14684160 | tf_op jit(solution)/shard_map/dot_general | solution.py:23
  268.8 4.8 convolution_convert_fusion.2
  279.4 6.3 fusion.86
  287.6 6.7 add_convert_fusion.3.refs_1_
  294.4 10.5 %collective-permute-done.25.refs_0_ = bf16[1024,512]{1,0:T(8,128)(2,1)S(1)} collective-permute-done((bf16[1024,512]{1,0:T(8,128)(2,1)S(1)}, bf16[1024,512]{1,0:T(8,128)(2,1)S(1)}, u32[]{:S(2)}, u32[]{:S(2)}) %collective-permute-start.25) | collective-permute-done | bytes 1048608 | tf_op jit(solution)/shard_map/ppermute | solution.py:40
  308.2 9.7 %convert_reduce_fusion.3 = (bf16[1024]{0:T(1024)(128)(2,1)S(1)}, bf16[1024,1024]{1,0:T(8,128)(2,1)S(1)}) fusion(f32[1024,1024]{1,0:T(8,128)} %copy-done.134, f32[1024]{0:T(1024)S(1)} %bitcast.303, bf16[1024,2048]{1,0:T(8,128)(2,1)} %copy-done.115, bf16[1024,2048]{1,0:T(8,128)(2,1)} %constant_dynamic-update-slice_fusion.16), kind=kOutput, calls=%fused_computation.35 | convolution fusion | flops 4308597760 | bytes 14686208 | tf_op jit(solution)/shard_map/dot_general | solution.py:31
  318.0 7.7 convert_reduce_fusion.2
  325.7 6.4 fusion.87
  332.1 7.1 add_convert_fusion.2
  343.4 5.1 convolution_convert_fusion.1
  352.6 22.5 %collective-permute-done.31.refs_1_ = bf16[256,2048]{1,0:T(8,128)(2,1)S(1)} collective-permute-done((bf16[256,2048]{1,0:T(8,128)(2,1)S(1)}, bf16[256,2048]{1,0:T(8,128)(2,1)S(1)}, u32[]{:S(2)}, u32[]{:S(2)}) %collective-permute-start.31) | collective-permute-done | bytes 1048608 | tf_op jit(solution)/shard_map/ppermute | solution.py:40
  376.1 5.0 add_convert_fusion.1
  383.6 14.0 %collective-permute-done.32.refs_2_ = bf16[256,2048]{1,0:T(8,128)(2,1)S(1)} collective-permute-done((bf16[256,2048]{1,0:T(8,128)(2,1)}, bf16[256,2048]{1,0:T(8,128)(2,1)S(1)}, u32[]{:S(2)}, u32[]{:S(2)}) %collective-permute-start.32) | collective-permute-done | bytes 1048608 | tf_op jit(solution)/shard_map/ppermute | solution.py:40
  408.2 3.9 convert_reduce_fusion.6
  442.4 5.4 collective-permute-start.36
  447.8 14.6 %collective-permute-done.36 = bf16[256,512]{1,0:T(8,128)(2,1)S(1)} collective-permute-done((bf16[256,512]{1,0:T(8,128)(2,1)S(1)}, bf16[256,512]{1,0:T(8,128)(2,1)S(1)}, u32[]{:S(2)}, u32[]{:S(2)}) %collective-permute-start.36) | collective-permute-done | bytes 262176 | tf_op jit(solution)/shard_map/ppermute | solution.py:45
  463.1 8.8 collective-permute-start.38
  471.9 17.3 %collective-permute-done.37 = bf16[256,512]{1,0:T(8,128)(2,1)} collective-permute-done((bf16[256,512]{1,0:T(8,128)(2,1)}, bf16[256,512]{1,0:T(8,128)(2,1)}, u32[]{:S(2)}, u32[]{:S(2)}) %collective-permute-start.37) | collective-permute-done | bytes 262176 | tf_op jit(solution)/shard_map/ppermute | solution.py:45
  507.4 28.3 %attend_back.1 = bf16[8,128,1536]{2,1,0:T(8,128)(2,1)S(1)} custom-call(s32[8]{0:T(128)S(1)} %copy-done.97, f32[8]{0:T(128)S(1)} %copy-done.95, bf16[8,128,1536]{2,1,0:T(8,128)(2,1)} %bitcast.243, bf16[8,128,512]{2,1,0:T(8,128)(2,1)S(1)} %bitcast.240), custom_call_target="tpu_custom_call" | custom-call | flops 32212254720 | bytes 1 | tf_op jit(solution)/shard_map/attend_back/pallas_call | solution.py:238
  558.1 5.5 collective-permute-start.45
  563.7 11.2 %fusion.71 = (bf16[2048]{0:T(1024)(128)(2,1)S(1)}, bf16[2048]{0:T(1024)(128)(2,1)S(1)}, bf16[1024,2048]{1,0:T(8,128)(2,1)}) fusion(f32[1024]{0:T(1024)S(1)} %copy-done.128, f32[1024]{0:T(1024)S(1)} %copy-done.123, bf16[1024,2048]{1,0:T(8,128)(2,1)} %copy-done.3, bf16[1024,1536]{1,0:T(8,128)(2,1)S(1)} %get-tuple-element.160.refs_1_, ...), kind=kOutput, calls=%fused_computation.292 | convolution fusion | flops 6469709824 | bytes 17842176 | tf_op jit(solution)/shard_map/dot_general | solution.py:31
  592.0 8.3 collective-permute-done.46.refs_3_
  608.8 8.0 fusion.68
  616.8 4.5 copy-done.106
  623.7 6.3 fusion.88
  632.3 4.7 slice_add_fusion
  640.9 7.6 add_convert_fusion
  650.2 7.5 collective-permute-done.48
  657.7 17.3 %collective-permute-done.50 = bf16[512,768]{0,1:T(8,128)(2,1)S(1)} collective-permute-done((bf16[512,768]{0,1:T(8,128)(2,1)S(1)}, bf16[512,768]{0,1:T(8,128)(2,1)S(1)}, u32[]{:S(2)}, u32[]{:S(2)}) %collective-permute-start.50) | collective-permute-done | bytes 786464 | tf_op jit(solution)/shard_map/ppermute | solution.py:40
  683.1 19.7 %collective-permute-done.52.refs_2_ = bf16[4,256,512]{2,1,0:T(8,128)(2,1)S(1)} collective-permute-done((bf16[4,256,512]{2,1,0:T(8,128)(2,1)}, bf16[4,256,512]{2,1,0:T(8,128)(2,1)S(1)}, u32[]{:S(2)}, u32[]{:S(2)}) %collective-permute-start.52) | collective-permute-done | bytes 1048608 | tf_op jit(solution)/shard_map/ppermute | solution.py:51
  712.0 20.3 %collective-permute-done.53.refs_6_ = bf16[256,2048]{1,0:T(8,128)(2,1)} collective-permute-done((bf16[256,2048]{1,0:T(8,128)(2,1)}, bf16[256,2048]{1,0:T(8,128)(2,1)}, u32[]{:S(2)}, u32[]{:S(2)}) %collective-permute-start.53) | collective-permute-done | bytes 1048608 | tf_op jit(solution)/shard_map/ppermute | solution.py:40
  732.3 22.8 %collective-permute-done.54.refs_7_ = bf16[256,2048]{1,0:T(8,128)(2,1)} collective-permute-done((bf16[256,2048]{1,0:T(8,128)(2,1)}, bf16[256,2048]{1,0:T(8,128)(2,1)}, u32[]{:S(2)}, u32[]{:S(2)}) %collective-permute-start.54) | collective-permute-done | bytes 1048608 | tf_op jit(solution)/shard_map/ppermute | solution.py:40
  765.0 29.5 %collective-permute-done.58.refs_5_ = bf16[4,256,512]{2,1,0:T(8,128)(2,1)S(1)} collective-permute-done((bf16[4,256,512]{2,1,0:T(8,128)(2,1)}, bf16[4,256,512]{2,1,0:T(8,128)(2,1)S(1)}, u32[]{:S(2)}, u32[]{:S(2)}) %collective-permute-start.58) | collective-permute-done | bytes 1048608 | tf_op jit(solution)/shard_map/ppermute | solution.py:51
  799.9 11.1 %reduce-scatter.11.cloned.1.call-done.refs_0_ = bf16[272,2048]{1,0:T(8,128)(2,1)} async-done(((bf16[1088,2048]{1,0:T(8,128)(2,1)}), bf16[272,2048]{1,0:T(8,128)(2,1)}) %reduce-scatter.11.cloned.1.call-update) | async-done | bytes 1114128 | tf_op jit(solution)/shard_map/reduce_scatter | solution.py:532
  824.6 4.0 fusion.32
  842.8 38.8 %all-gather.10.cloned.1.call-done = bf16[1536,1024]{1,0:T(8,128)(2,1)} async-done(((bf16[1536,256]{1,0:T(8,128)(2,1)}), bf16[1536,1024]{1,0:T(8,128)(2,1)}) %all-gather.10.cloned.1.call-update) | async-done | bytes 3145744 | tf_op jit(solution)/shard_map/all_gather | solution.py:562
  881.6 5.5 convert.42
  (642 shorter events, 338.7 us)
Async XLA Ops:
  7.2 86.8 %all-gather.12.cloned.1.call-start = ((), (), s32[]{:S(2)}) async-start(), calls=%async_computation.11 | async-start | bytes 5242880 | tf_op jit(solution)/shard_map/all_gather | solution.py:339
  10.3 388.3 %reduce-scatter.5.cloned.1.call-start = ((), (), s32[]{:S(2)}) async-start(), calls=%async_computation.4 | async-start | bytes 5242880 | tf_op jit(solution)/shard_map/reduce_scatter | solution.py:447
  22.4 97.2 %collective-permute-start.7 = (bf16[1024,512]{1,0:T(8,128)(2,1)}, bf16[1024,512]{1,0:T(8,128)(2,1)}, u32[]{:S(2)}, u32[]{:S(2)}) collective-permute-start(bf16[1024,512]{1,0:T(8,128)(2,1)} %param.23), channel_id=1, source_target_pairs={{0,16},{8,24},{16,0},{24,8},{1,17},{9,25},{17,1},{25,9},{2,18},{10... | collective-permute-start | bytes 3145736 | tf_op jit(solution)/shard_map/ppermute | solution.py:40
  22.9 96.7 %collective-permute-start.6 = (bf16[1024,512]{1,0:T(8,128)(2,1)}, bf16[1024,512]{1,0:T(8,128)(2,1)}, u32[]{:S(2)}, u32[]{:S(2)}) collective-permute-start(bf16[1024,512]{1,0:T(8,128)(2,1)} %param.23), channel_id=1, source_target_pairs={{0,8},{8,0},{16,24},{24,16},{1,9},{9,1},{17,25},{25,17},{2,10},{10... | collective-permute-start | bytes 3145736 | tf_op jit(solution)/shard_map/ppermute | solution.py:40
  73.6 33.9 %collective-permute-start.4 = (bf16[2048,768]{1,0:T(8,128)(2,1)}, bf16[2048,768]{1,0:T(8,128)(2,1)}, u32[]{:S(2)}, u32[]{:S(2)}) collective-permute-start(bf16[2048,768]{1,0:T(8,128)(2,1)} %fusion.50), channel_id=1, source_target_pairs={{0,1},{1,0},{2,3},{3,2},{4,5},{5,4},{6,7},{7,6},{8,9},{9,8},{10,11... | collective-permute-start | bytes 9437192 | tf_op jit(solution)/shard_map/ppermute | solution.py:35
  82.8 58.4 %collective-permute-start.10 = (bf16[512,1024]{1,0:T(8,128)(2,1)}, bf16[512,1024]{1,0:T(8,128)(2,1)}, u32[]{:S(2)}, u32[]{:S(2)}) collective-permute-start(bf16[512,1024]{1,0:T(8,128)(2,1)} %get-tuple-element.108), channel_id=1, source_target_pairs={{0,8},{8,0},{16,24},{24,16},{1,9},{9,1},{17,25},{25,17},{2,10},{10... | collective-permute-start | bytes 3145736 | tf_op jit(solution)/shard_map/ppermute | solution.py:40
  86.2 55.1 %collective-permute-start.11 = (bf16[512,1024]{1,0:T(8,128)(2,1)}, bf16[512,1024]{1,0:T(8,128)(2,1)}, u32[]{:S(2)}, u32[]{:S(2)}) collective-permute-start(bf16[512,1024]{1,0:T(8,128)(2,1)} %get-tuple-element.109), channel_id=1, source_target_pairs={{0,16},{8,24},{16,0},{24,8},{1,17},{9,25},{17,1},{25,9},{2,18},{10... | collective-permute-start | bytes 3145736 | tf_op jit(solution)/shard_map/ppermute | solution.py:40
  107.5 33.8 %collective-permute-start.12 = (bf16[512,1024]{1,0:T(8,128)(2,1)S(1)}, bf16[512,1024]{1,0:T(8,128)(2,1)S(1)}, u32[]{:S(2)}, u32[]{:S(2)}) collective-permute-start(bf16[512,1024]{1,0:T(8,128)(2,1)S(1)} %copy-done.64), channel_id=1, source_target_pairs={{0,24},{8,16},{16,8},{24,0},{1,25},{9,17},{17,9},{25,1},{2,26},{10... | collective-permute-start | bytes 3145736 | tf_op jit(solution)/shard_map/ppermute | solution.py:40
  154.7 35.2 %collective-permute-start.13 = (bf16[1024,2048]{1,0:T(8,128)(2,1)}, bf16[1024,2048]{1,0:T(8,128)(2,1)}, u32[]{:S(2)}, u32[]{:S(2)}) collective-permute-start(bf16[1024,2048]{1,0:T(8,128)(2,1)} %maximum_dynamic-update-slice_fusion), channel_id=1, source_target_pairs={{0,1},{1,0},{2,3},{3,2},{4,5},{5,4},{6,7},{7,6},{8,9},{9,8},{10,11... | collective-permute-start | bytes 12582920 | tf_op jit(solution)/shard_map/ppermute | solution.py:35
  154.8 33.6 %collective-permute-start.18 = (bf16[256,2048]{1,0:T(8,128)(2,1)}, bf16[256,2048]{1,0:T(8,128)(2,1)S(1)}, u32[]{:S(2)}, u32[]{:S(2)}) collective-permute-start(bf16[256,2048]{1,0:T(8,128)(2,1)} %get-tuple-element.116), channel_id=1, source_target_pairs={{0,16},{8,24},{16,0},{24,8},{1,17},{9,25},{17,1},{25,9},{2,18},{10... | collective-permute-start | bytes 3145736 | tf_op jit(solution)/shard_map/ppermute | solution.py:40
  155.5 34.4 %collective-permute-start.17 = (bf16[256,2048]{1,0:T(8,128)(2,1)}, bf16[256,2048]{1,0:T(8,128)(2,1)S(1)}, u32[]{:S(2)}, u32[]{:S(2)}) collective-permute-start(bf16[256,2048]{1,0:T(8,128)(2,1)} %get-tuple-element.116), channel_id=1, source_target_pairs={{0,8},{8,0},{16,24},{24,16},{1,9},{9,1},{17,25},{25,17},{2,10},{10... | collective-permute-start | bytes 3145736 | tf_op jit(solution)/shard_map/ppermute | solution.py:40
  179.7 79.1 %collective-permute-start.28 = (bf16[2048,1024]{1,0:T(8,128)(2,1)}, bf16[2048,1024]{1,0:T(8,128)(2,1)}, u32[]{:S(2)}, u32[]{:S(2)}) collective-permute-start(bf16[2048,1024]{1,0:T(8,128)(2,1)} %constant_dynamic-update-slice_fusion.17), channel_id=1, source_target_pairs={{0,1},{1,0},{2,3},{3,2},{4,5},{5,4},{6,7},{7,6},{8,9},{9,8},{10,11... | collective-permute-start | bytes 12582920 | tf_op jit(solution)/shard_map/ppermute | solution.py:35
  186.9 26.4 %collective-permute-start.21 = (bf16[1024,512]{1,0:T(8,128)(2,1)}, bf16[1024,512]{1,0:T(8,128)(2,1)}, u32[]{:S(2)}, u32[]{:S(2)}) collective-permute-start(bf16[1024,512]{1,0:T(8,128)(2,1)} %get-tuple-element.129.refs_3_), channel_id=1, source_target_pairs={{0,8},{8,0},{16,24},{24,16},{1,9},{9,1},{17,25},{25,17},{2,10},{10... | collective-permute-start | bytes 3145736 | tf_op jit(solution)/shard_map/ppermute | solution.py:40
  188.4 26.4 %collective-permute-start.22 = (bf16[1024,512]{1,0:T(8,128)(2,1)}, bf16[1024,512]{1,0:T(8,128)(2,1)}, u32[]{:S(2)}, u32[]{:S(2)}) collective-permute-start(bf16[1024,512]{1,0:T(8,128)(2,1)} %get-tuple-element.130.refs_4_), channel_id=1, source_target_pairs={{0,16},{8,24},{16,0},{24,8},{1,17},{9,25},{17,1},{25,9},{2,18},{10... | collective-permute-start | bytes 3145736 | tf_op jit(solution)/shard_map/ppermute | solution.py:40
  195.8 26.4 %collective-permute-start.19 = (bf16[128,2048]{1,0:T(8,128)(2,1)S(1)}, bf16[128,2048]{1,0:T(8,128)(2,1)S(1)}, u32[]{:S(2)}, u32[]{:S(2)}) collective-permute-start(bf16[128,2048]{1,0:T(8,128)(2,1)S(1)} %slice.366), channel_id=1, source_target_pairs={{0,8},{8,0},{16,24},{24,16},{1,9},{9,1},{17,25},{25,17},{2,10},{10... | collective-permute-start | bytes 1572872 | tf_op jit(solution)/shard_map/ppermute | solution.py:40
  196.4 27.1 %collective-permute-start.20 = (bf16[128,2048]{1,0:T(8,128)(2,1)S(1)}, bf16[128,2048]{1,0:T(8,128)(2,1)S(1)}, u32[]{:S(2)}, u32[]{:S(2)}) collective-permute-start(bf16[128,2048]{1,0:T(8,128)(2,1)S(1)} %slice.367), channel_id=1, source_target_pairs={{0,16},{8,24},{16,0},{24,8},{1,17},{9,25},{17,1},{25,9},{2,18},{10... | collective-permute-start | bytes 1572872 | tf_op jit(solution)/shard_map/ppermute | solution.py:40
  225.0 23.2 %collective-permute-start.23 = (bf16[256,2048]{1,0:T(8,128)(2,1)S(1)}, bf16[256,2048]{1,0:T(8,128)(2,1)S(1)}, u32[]{:S(2)}, u32[]{:S(2)}) collective-permute-start(bf16[256,2048]{1,0:T(8,128)(2,1)S(1)} %gate.24), channel_id=1, source_target_pairs={{0,8},{8,0},{16,24},{24,16},{1,9},{9,1},{17,25},{25,17},{2,10},{10... | collective-permute-start | bytes 3145736 | tf_op jit(solution)/shard_map/ppermute | solution.py:40
  278.4 26.5 %collective-permute-start.25 = (bf16[1024,512]{1,0:T(8,128)(2,1)S(1)}, bf16[1024,512]{1,0:T(8,128)(2,1)S(1)}, u32[]{:S(2)}, u32[]{:S(2)}) collective-permute-start(bf16[1024,512]{1,0:T(8,128)(2,1)S(1)} %get-tuple-element.132), channel_id=1, source_target_pairs={{0,24},{8,16},{16,8},{24,0},{1,25},{9,17},{17,9},{25,1},{2,26},{10... | collective-permute-start | bytes 3145736 | tf_op jit(solution)/shard_map/ppermute | solution.py:40
  308.2 188.0 %reduce-scatter.7.cloned.1.call-start = ((), (), s32[]{:S(2)}) async-start(), calls=%async_computation.5 | async-start | bytes 5242880 | tf_op jit(solution)/shard_map/reduce_scatter | solution.py:455
  348.5 26.6 %collective-permute-start.34 = (bf16[2048,1024]{1,0:T(8,128)(2,1)S(1)}, bf16[2048,1024]{1,0:T(8,128)(2,1)S(1)}, u32[]{:S(2)}, u32[]{:S(2)}) collective-permute-start(bf16[2048,1024]{1,0:T(8,128)(2,1)S(1)} %convolution_convert_fusion.1), channel_id=1, source_target_pairs={{0,1},{1,0},{2,3},{3,2},{4,5},{5,4},{6,7},{7,6},{8,9},{9,8},{10,11... | collective-permute-start | bytes 12582920 | tf_op jit(solution)/shard_map/ppermute | solution.py:35
  349.1 26.0 %collective-permute-start.31 = (bf16[256,2048]{1,0:T(8,128)(2,1)S(1)}, bf16[256,2048]{1,0:T(8,128)(2,1)S(1)}, u32[]{:S(2)}, u32[]{:S(2)}) collective-permute-start(bf16[256,2048]{1,0:T(8,128)(2,1)S(1)} %get-tuple-element.140), channel_id=1, source_target_pairs={{0,8},{8,0},{16,24},{24,16},{1,9},{9,1},{17,25},{25,17},{2,10},{10... | collective-permute-start | bytes 3145736 | tf_op jit(solution)/shard_map/ppermute | solution.py:40
  350.1 47.5 %collective-permute-start.32 = (bf16[256,2048]{1,0:T(8,128)(2,1)}, bf16[256,2048]{1,0:T(8,128)(2,1)S(1)}, u32[]{:S(2)}, u32[]{:S(2)}) collective-permute-start(bf16[256,2048]{1,0:T(8,128)(2,1)} %get-tuple-element.141), channel_id=1, source_target_pairs={{0,16},{8,24},{16,0},{24,8},{1,17},{9,25},{17,1},{25,9},{2,18},{10... | collective-permute-start | bytes 3145736 | tf_op jit(solution)/shard_map/ppermute | solution.py:40
  350.7 47.9 %collective-permute-start.33 = (bf16[256,2048]{1,0:T(8,128)(2,1)}, bf16[256,2048]{1,0:T(8,128)(2,1)}, u32[]{:S(2)}, u32[]{:S(2)}) collective-permute-start(bf16[256,2048]{1,0:T(8,128)(2,1)} %get-tuple-element.142), channel_id=1, source_target_pairs={{0,24},{8,16},{16,8},{24,0},{1,25},{9,17},{17,9},{25,1},{2,26},{10... | collective-permute-start | bytes 3145736 | tf_op jit(solution)/shard_map/ppermute | solution.py:40
  383.6 155.4 %reduce-scatter.9.cloned.1.call-start = ((), (), s32[]{:S(2)}) async-start(), calls=%async_computation.6 | async-start | bytes 1310720 | tf_op jit(solution)/shard_map/reduce_scatter | solution.py:485
  438.9 53.8 %collective-permute-start.39 = (bf16[1024,512]{1,0:T(8,128)(2,1)S(1)}, bf16[1024,512]{1,0:T(8,128)(2,1)}, u32[]{:S(2)}, u32[]{:S(2)}) collective-permute-start(bf16[1024,512]{1,0:T(8,128)(2,1)S(1)} %get-tuple-element.153), channel_id=1, source_target_pairs={{0,8},{8,0},{16,24},{24,16},{1,9},{9,1},{17,25},{25,17},{2,10},{10... | collective-permute-start | bytes 3145736 | tf_op jit(solution)/shard_map/ppermute | solution.py:40
  439.9 52.8 %collective-permute-start.40 = (bf16[1024,512]{1,0:T(8,128)(2,1)}, bf16[1024,512]{1,0:T(8,128)(2,1)}, u32[]{:S(2)}, u32[]{:S(2)}) collective-permute-start(bf16[1024,512]{1,0:T(8,128)(2,1)} %get-tuple-element.154), channel_id=1, source_target_pairs={{0,16},{8,24},{16,0},{24,8},{1,17},{9,25},{17,1},{25,9},{2,18},{10... | collective-permute-start | bytes 3145736 | tf_op jit(solution)/shard_map/ppermute | solution.py:40
  439.9 52.8 %collective-permute-start.41 = (bf16[1024,512]{1,0:T(8,128)(2,1)}, bf16[1024,512]{1,0:T(8,128)(2,1)}, u32[]{:S(2)}, u32[]{:S(2)}) collective-permute-start(bf16[1024,512]{1,0:T(8,128)(2,1)} %get-tuple-element.155), channel_id=1, source_target_pairs={{0,24},{8,16},{16,8},{24,0},{1,25},{9,17},{17,9},{25,1},{2,26},{10... | collective-permute-start | bytes 3145736 | tf_op jit(solution)/shard_map/ppermute | solution.py:40
  447.8 41.4 %collective-permute-start.37 = (bf16[256,512]{1,0:T(8,128)(2,1)}, bf16[256,512]{1,0:T(8,128)(2,1)}, u32[]{:S(2)}, u32[]{:S(2)}) collective-permute-start(bf16[256,512]{1,0:T(8,128)(2,1)} %get-tuple-element.149), channel_id=1, source_target_pairs={{0,4},{2,6},{4,0},{6,2},{1,5},{3,7},{5,1},{7,3},{8,12},{10,14},{12... | collective-permute-start | bytes 786440 | tf_op jit(solution)/shard_map/ppermute | solution.py:45
  463.1 26.1 %collective-permute-start.38 = (bf16[256,512]{1,0:T(8,128)(2,1)}, bf16[256,512]{1,0:T(8,128)(2,1)}, u32[]{:S(2)}, u32[]{:S(2)}) collective-permute-start(bf16[256,512]{1,0:T(8,128)(2,1)} %get-tuple-element.150), channel_id=1, source_target_pairs={{0,2},{2,4},{4,6},{6,0},{1,3},{3,5},{5,7},{7,1},{8,10},{10,12},{12... | collective-permute-start | bytes 786440 | tf_op jit(solution)/shard_map/ppermute | solution.py:45
  502.0 99.5 %all-gather.6.cloned.1.call-start = ((), (), s32[]{:S(2)}) async-start(), calls=%async_computation.7 | async-start | bytes 1310720 | tf_op jit(solution)/shard_map/all_gather | solution.py:497
  502.4 34.2 %collective-permute-start.42 = (bf16[512,512]{1,0:T(8,128)(2,1)S(1)}, bf16[512,512]{1,0:T(8,128)(2,1)S(1)}, u32[]{:S(2)}, u32[]{:S(2)}) collective-permute-start(bf16[512,512]{1,0:T(8,128)(2,1)S(1)} %pad_maximum_fusion.8), channel_id=1, source_target_pairs={{0,8},{8,0},{16,24},{24,16},{1,9},{9,1},{17,25},{25,17},{2,10},{10... | collective-permute-start | bytes 1572872 | tf_op jit(solution)/shard_map/ppermute | solution.py:40
  504.0 33.4 %collective-permute-start.43 = (bf16[512,512]{1,0:T(8,128)(2,1)S(1)}, bf16[512,512]{1,0:T(8,128)(2,1)S(1)}, u32[]{:S(2)}, u32[]{:S(2)}) collective-permute-start(bf16[512,512]{1,0:T(8,128)(2,1)S(1)} %pad_maximum_fusion.9), channel_id=1, source_target_pairs={{0,16},{8,24},{16,0},{24,8},{1,17},{9,25},{17,1},{25,9},{2,18},{10... | collective-permute-start | bytes 1572872 | tf_op jit(solution)/shard_map/ppermute | solution.py:40
  505.6 32.6 %collective-permute-start.44 = (bf16[512,512]{1,0:T(8,128)(2,1)S(1)}, bf16[512,512]{1,0:T(8,128)(2,1)S(1)}, u32[]{:S(2)}, u32[]{:S(2)}) collective-permute-start(bf16[512,512]{1,0:T(8,128)(2,1)S(1)} %pad_maximum_fusion.10), channel_id=1, source_target_pairs={{0,24},{8,16},{16,8},{24,0},{1,25},{9,17},{17,9},{25,1},{2,26},{10... | collective-permute-start | bytes 1572872 | tf_op jit(solution)/shard_map/ppermute | solution.py:40
  556.8 43.5 %collective-permute-start.46 = (bf16[4,256,512]{2,1,0:T(8,128)(2,1)}, bf16[4,256,512]{2,1,0:T(8,128)(2,1)}, u32[]{:S(2)}, u32[]{:S(2)}) collective-permute-start(bf16[4,256,512]{2,1,0:T(8,128)(2,1)} %bitcast_dynamic-update-slice_fusion), channel_id=1, source_target_pairs={{2,0},{4,2},{6,4},{3,1},{5,3},{7,5},{10,8},{12,10},{14,12},{11,9},... | collective-permute-start | bytes 3145736 | tf_op jit(solution)/shard_map/ppermute | solution.py:51
  558.1 42.9 %collective-permute-start.45 = (bf16[4,256,512]{2,1,0:T(8,128)(2,1)}, bf16[4,256,512]{2,1,0:T(8,128)(2,1)}, u32[]{:S(2)}, u32[]{:S(2)}) collective-permute-start(bf16[4,256,512]{2,1,0:T(8,128)(2,1)} %bitcast_dynamic-update-slice_fusion), channel_id=1, source_target_pairs={{0,2},{2,4},{4,6},{1,3},{3,5},{5,7},{8,10},{10,12},{12,14},{9,11},... | collective-permute-start | bytes 3145736 | tf_op jit(solution)/shard_map/ppermute | solution.py:50
  563.6 236.3 %all-gather.8.cloned.1.call-start = ((), (), s32[]{:S(2)}) async-start(), calls=%async_computation.9 | async-start | bytes 5242880 | tf_op jit(solution)/shard_map/all_gather | solution.py:500
  582.1 228.9 %reduce-scatter.11.cloned.1.call-start = ((), (), s32[]{:S(2)}) async-start(), calls=%async_computation.8 | async-start | bytes 5570560 | tf_op jit(solution)/shard_map/reduce_scatter | solution.py:532
  623.6 258.0 %all-gather.10.cloned.1.call-start = ((), (), s32[]{:S(2)}) async-start(), calls=%async_computation.10 | async-start | bytes 3932160 | tf_op jit(solution)/shard_map/all_gather | solution.py:562
  630.0 53.1 %collective-permute-start.51 = (bf16[4,256,512]{2,1,0:T(8,128)(2,1)}, bf16[4,256,512]{2,1,0:T(8,128)(2,1)S(1)}, u32[]{:S(2)}, u32[]{:S(2)}) collective-permute-start(bf16[4,256,512]{2,1,0:T(8,128)(2,1)} %get-tuple-element.167), channel_id=1, source_target_pairs={{2,4},{4,6},{3,5},{5,7},{10,12},{12,14},{11,13},{13,15},{18,20},{2... | collective-permute-start | bytes 3145736 | tf_op jit(solution)/shard_map/ppermute | solution.py:50
  630.7 72.0 %collective-permute-start.52 = (bf16[4,256,512]{2,1,0:T(8,128)(2,1)}, bf16[4,256,512]{2,1,0:T(8,128)(2,1)S(1)}, u32[]{:S(2)}, u32[]{:S(2)}) collective-permute-start(bf16[4,256,512]{2,1,0:T(8,128)(2,1)} %get-tuple-element.168), channel_id=1, source_target_pairs={{2,0},{4,2},{3,1},{5,3},{10,8},{12,10},{11,9},{13,11},{18,16},{20,... | collective-permute-start | bytes 3145736 | tf_op jit(solution)/shard_map/ppermute | solution.py:51
  638.7 36.3 %collective-permute-start.50 = (bf16[512,768]{0,1:T(8,128)(2,1)S(1)}, bf16[512,768]{0,1:T(8,128)(2,1)S(1)}, u32[]{:S(2)}, u32[]{:S(2)}) collective-permute-start(bf16[512,768]{0,1:T(8,128)(2,1)S(1)} %get-tuple-element.200), channel_id=1, source_target_pairs={{0,24},{8,16},{16,8},{24,0},{1,25},{9,17},{17,9},{25,1},{2,26},{10... | collective-permute-start | bytes 2359304 | tf_op jit(solution)/shard_map/ppermute | solution.py:40
  640.2 36.2 %collective-permute-start.49 = (bf16[512,768]{0,1:T(8,128)(2,1)S(1)}, bf16[512,768]{0,1:T(8,128)(2,1)S(1)}, u32[]{:S(2)}, u32[]{:S(2)}) collective-permute-start(bf16[512,768]{0,1:T(8,128)(2,1)S(1)} %get-tuple-element.201), channel_id=1, source_target_pairs={{0,16},{8,24},{16,0},{24,8},{1,17},{9,25},{17,1},{25,9},{2,18},{10... | collective-permute-start | bytes 2359304 | tf_op jit(solution)/shard_map/ppermute | solution.py:40
  705.9 26.3 %collective-permute-start.53 = (bf16[256,2048]{1,0:T(8,128)(2,1)}, bf16[256,2048]{1,0:T(8,128)(2,1)}, u32[]{:S(2)}, u32[]{:S(2)}) collective-permute-start(bf16[256,2048]{1,0:T(8,128)(2,1)} %copy-done.70), channel_id=1, source_target_pairs={{0,8},{8,0},{16,24},{24,16},{1,9},{9,1},{17,25},{25,17},{2,10},{10... | collective-permute-start | bytes 3145736 | tf_op jit(solution)/shard_map/ppermute | solution.py:40
  707.4 47.7 %collective-permute-start.54 = (bf16[256,2048]{1,0:T(8,128)(2,1)}, bf16[256,2048]{1,0:T(8,128)(2,1)}, u32[]{:S(2)}, u32[]{:S(2)}) collective-permute-start(bf16[256,2048]{1,0:T(8,128)(2,1)} %get-tuple-element.171), channel_id=1, source_target_pairs={{0,16},{8,24},{16,0},{24,8},{1,17},{9,25},{17,1},{25,9},{2,18},{10... | collective-permute-start | bytes 3145736 | tf_op jit(solution)/shard_map/ppermute | solution.py:40
  708.9 46.2 %collective-permute-start.55 = (bf16[256,2048]{1,0:T(8,128)(2,1)}, bf16[256,2048]{1,0:T(8,128)(2,1)}, u32[]{:S(2)}, u32[]{:S(2)}) collective-permute-start(bf16[256,2048]{1,0:T(8,128)(2,1)} %get-tuple-element.172), channel_id=1, source_target_pairs={{0,24},{8,16},{16,8},{24,0},{1,25},{9,17},{17,9},{25,1},{2,26},{10... | collective-permute-start | bytes 3145736 | tf_op jit(solution)/shard_map/ppermute | solution.py:40
  709.9 51.4 %collective-permute-start.57 = (bf16[4,256,512]{2,1,0:T(8,128)(2,1)}, bf16[4,256,512]{2,1,0:T(8,128)(2,1)S(1)}, u32[]{:S(2)}, u32[]{:S(2)}) collective-permute-start(bf16[4,256,512]{2,1,0:T(8,128)(2,1)} %copy-done.59), channel_id=1, source_target_pairs={{4,6},{5,7},{12,14},{13,15},{20,22},{21,23},{28,30},{29,31}} | collective-permute-start | bytes 3145736 | tf_op jit(solution)/shard_map/ppermute | solution.py:50
  710.7 83.8 %collective-permute-start.58 = (bf16[4,256,512]{2,1,0:T(8,128)(2,1)}, bf16[4,256,512]{2,1,0:T(8,128)(2,1)S(1)}, u32[]{:S(2)}, u32[]{:S(2)}) collective-permute-start(bf16[4,256,512]{2,1,0:T(8,128)(2,1)} %copy-done.61), channel_id=1, source_target_pairs={{2,0},{3,1},{10,8},{11,9},{18,16},{19,17},{26,24},{27,25}} | collective-permute-start | bytes 3145736 | tf_op jit(solution)/shard_map/ppermute | solution.py:51
  758.4 36.5 %collective-permute-start.56 = (bf16[256,2048]{1,0:T(8,128)(2,1)S(1)}, bf16[256,2048]{1,0:T(8,128)(2,1)}, u32[]{:S(2)}, u32[]{:S(2)}) collective-permute-start(bf16[256,2048]{1,0:T(8,128)(2,1)S(1)} %add_convert_fusion.5), channel_id=1, source_target_pairs={{0,1},{1,0},{2,3},{3,2},{4,5},{5,4},{6,7},{7,6},{8,9},{9,8},{10,11... | collective-permute-start | bytes 3145736 | tf_op jit(solution)/shard_map/ppermute | solution.py:35
  (160 other events, 1487.0 us)
Sparse Core Ops, SparseCore 0:
  10.4 83.5 all-gather.11
  308.3 78.4 reduce-scatter.4
  389.8 93.4 reduce-scatter.6
  502.1 25.2 reduce-scatter.8
  563.7 37.7 all-gather.5
  603.0 102.9 all-gather.7
  708.9 102.0 reduce-scatter.10
  819.1 62.4 all-gather.9

commit v4 on v3

--- a/solution.py
+++ b/solution.py
@@ -64,7 +64,14 @@
     pass
 
 
+def corner(value):
+    limits = [1] * (value.ndim - 2) + [8, 128]
+    return lax.slice(value, [0] * value.ndim, limits).reshape(8, 128).astype(F32)
+
+
 def gate(values, *earlier):
+    if earlier:
+        earlier = (sum([corner(value) for value in earlier[1:]], corner(earlier[0])),)
     anywhere = pl.BlockSpec(memory_space=pl.ANY)
     return pl.pallas_call(
         pass_on,
@@ -99,14 +106,14 @@
     return [value, *first] + ([jnp.concatenate(second, axis=0)] if second else [])
 
 
-def place(pieces, axis):
+def place(pieces, axis, offset=0):
     index = lax.axis_index("fsdp")
     width = pieces[0].shape[axis]
     shape = list(pieces[0].shape)
     shape[axis] = width * len(pieces)
     whole = jnp.zeros(shape, pieces[0].dtype)
     for k, piece in enumerate(pieces):
-        whole = lax.dynamic_update_slice_in_dim(whole, piece, (index ^ k) * width, axis)
+        whole = lax.dynamic_update_slice_in_dim(whole, piece, (index ^ k) * width + offset, axis)
     return whole
 
 
@@ -493,10 +500,10 @@
         both.append(jnp.concatenate([pick(grad_down, k, 1), *piece]))
     both = both[:1] + send_blocks(both[1:])
     grad_qkv = attend_back(order, slopes, qkv, grad_tree)
-    grad_qkv, grad_out, *both = gate([grad_qkv, grad_out, *both])
+    grad_qkv, grad_out = gate([grad_qkv, grad_out], *both[1:])
     g_out = lax.all_gather(grad_out, "context", axis=0, tiled=True)
-    grad_down = place([piece[None, :lines] for piece in both], 0)
     g_up = jnp.concatenate([piece[lines:] for piece in both])
+    grad_down = place([piece[None, :lines] for piece in both], 0, zero_from(g_up))
     g_up = lax.all_gather(g_up, "context", axis=0, tiled=True)
     down_up, down_down = line_step([grad_down], [grad_down])
 

time: 902 us -> 873 us (0.968)
  local copies, waits for them, and re-layouts: 197 us -> 174 us
    unnamed x306 -> x264, local copies, waits for them, and re-layouts: 104 us -> 83 us
    ppermute x3, waiting for transfers between devices: 57.5 us -> 45.5 us  [line_step(): lax.ppermute(downward[-1], 'context', [(i + 1, i) for i in range(0, size...]
  transfers between devices with their start and end apart: 72 -> 72, of which waited for: 35 -> 32; matrix products, arithmetic and copies ran while one was open for 31% -> 33% of each run, Pallas kernels for 5% -> 5%
where the time goes in v4:
time: 873 us; the launch traced here: 866 us
  waiting for transfers between devices  348 us (40%)
  local copies, waits for them, and re-layouts  174 us (20%)
  matrix products  134 us (15%)
  starting transfers between devices  77.4 us (9%)
  other arithmetic  70.2 us (8%)
  Pallas kernels  46.2 us (5%)
  between operations  17.2 us (2%)
    ppermute x40, waiting for transfers between devices, xor_send(): return lax.ppermute(value, 'fsdp', [(i, i ^ step) for i in range(size)])  196 us
    unnamed x264, local copies, waits for them, and re-layouts  83 us
    dot_general x7, matrix products, dot_nn(): lax.dot_general(left, right, (((1,), (0,)), ((), ())), preferred_element_...  49.5 us
    ppermute x6, waiting for transfers between devices, ring_send(): lax.ppermute(value, 'context', [(i, (i + step) % size) for i in range(siz...  48.5 us
    dot_general x7, matrix products, dot_nt(): lax.dot_general(left, right, (((1,), (1,)), ((), ())), preferred_element_...  47.9 us
    ppermute x3, waiting for transfers between devices, line_step(): lax.ppermute(downward[-1], 'context', [(i + 1, i) for i in range(0, size...  45.5 us
    ppermute x40, starting transfers between devices, xor_send(): return lax.ppermute(value, 'fsdp', [(i, i ^ step) for i in range(size)])  43.7 us
    all_gather x1, waiting for transfers between devices, per_device(): g_heads = lax.all_gather(grad_heads, 'context', axis=1, tiled=True)  39.8 us
  transfers between devices with their start and end apart: 72, of which 32 were waited for; matrix products, arithmetic and copies ran while one was open for 33% of the time, Pallas kernels for 5%

profile of v4, /device:TPU:0, one launch (start us, length us, event | category | flops | bytes accessed | tf_op | source)
XLA Modules:
  0.0 866.0 jit_solution(5167077943293006107)
XLA Ops:
  28.7 11.9 %collective-permute-done.1.refs_1_ = bf16[544,768]{1,0:T(8,128)(2,1)S(1)} collective-permute-done((bf16[544,768]{1,0:T(8,128)(2,1)}, bf16[544,768]{1,0:T(8,128)(2,1)S(1)}, u32[]{:S(2)}, u32[]{:S(2)}) %collective-permute-start.1) | collective-permute-done | bytes 835616 | tf_op jit(solution)/shard_map/ppermute | solution.py:40
  56.6 14.5 %collective-permute-done.3 = bf16[272,768]{1,0:T(8,128)(2,1)S(1)} collective-permute-done((bf16[272,768]{1,0:T(8,128)(2,1)S(1)}, bf16[272,768]{1,0:T(8,128)(2,1)S(1)}, u32[]{:S(2)}, u32[]{:S(2)}) %collective-permute-start.3) | collective-permute-done | bytes 417824 | tf_op jit(solution)/shard_map/ppermute | solution.py:40
  87.3 6.7 all-gather.12.cloned.1.call-done
  107.9 9.6 %add_convert_fusion.4.refs_0_ = bf16[1024,1536]{1,0:T(8,128)(2,1)S(1)} fusion(bf16[2048,768]{1,0:T(8,128)(2,1)} %collective-permute-done.4, bf16[2048,768]{1,0:T(8,128)(2,1)} %fusion.50, f32[1536]{0:T(1024)S(1)} %add.498, bf16[1024,2048]{1,0:T(8,128)(2,1)S(1)} %copy-done.4, f32[2048]{0:T(1024)S(1)} %bitcast.311, f32[2048]{0:T(1024)S(1)} %bitcast.295, ...), kind=kOutput, calls=%fused_computation.21 | convolution fusion | flops 6470762496 | bytes 13662208 | tf_op jit(solution)/shard_map/dot_general | solution.py:23
  121.3 17.9 %attend.1 = bf16[8,128,512]{2,1,0:T(8,128)(2,1)S(1)} custom-call(s32[8]{0:T(128)S(1)} %select_reduce_fusion.order, f32[8]{0:T(128)S(1)} %fusion.70.slopes, bf16[8,128,1536]{2,1,0:T(8,128)(2,1)S(1)} %bitcast.253), custom_call_target="tpu_custom_call" | custom-call | flops 17179869184 | bytes 1 | tf_op jit(solution)/shard_map/attend/pallas_call | solution.py:223
  177.7 9.6 %collective-permute-done.15.refs_3_ = bf16[256,512]{1,0:T(8,128)(2,1)S(1)} collective-permute-done((bf16[256,512]{1,0:T(8,128)(2,1)S(1)}, bf16[256,512]{1,0:T(8,128)(2,1)S(1)}, u32[]{:S(2)}, u32[]{:S(2)}) %collective-permute-start.15) | collective-permute-done | bytes 262176 | tf_op jit(solution)/shard_map/ppermute | solution.py:45
  205.4 8.3 collective-permute-done.21
  215.2 7.5 collective-permute-done.19
  229.6 19.2 %collective-permute-done.24.refs_1_ = bf16[256,2048]{1,0:T(8,128)(2,1)S(1)} collective-permute-done((bf16[256,2048]{1,0:T(8,128)(2,1)S(1)}, bf16[256,2048]{1,0:T(8,128)(2,1)S(1)}, u32[]{:S(2)}, u32[]{:S(2)}) %collective-permute-start.24) | collective-permute-done | bytes 1048608 | tf_op jit(solution)/shard_map/ppermute | solution.py:40
  252.3 9.0 %collective-permute-done.26 = bf16[128,2048]{1,0:T(8,128)(2,1)S(1)} collective-permute-done((bf16[128,2048]{1,0:T(8,128)(2,1)S(1)}, bf16[128,2048]{1,0:T(8,128)(2,1)S(1)}, u32[]{:S(2)}, u32[]{:S(2)}) %collective-permute-start.26) | collective-permute-done | bytes 524320 | tf_op jit(solution)/shard_map/ppermute | solution.py:40
  261.4 10.0 %multiply_convert_fusion = (bf16[1024,1024]{1,0:T(8,128)(2,1)S(1)}, f32[1024,1024]{1,0:T(8,128)}) fusion(f32[1024]{0:T(1024)S(1)} %bitcast.317, bf16[1024,2048]{1,0:T(8,128)(2,1)S(1)} %constant_dynamic-update-slice_fusion.5, bf16[2048,1024]{1,0:T(8,128)(2,1)} %collective-permute-done.28), kind=kOutput, calls=%fused_computation.36 | convolution fusion | flops 4301258752 | bytes 14684160 | tf_op jit(solution)/shard_map/dot_general | solution.py:23
  271.4 4.8 convolution_convert_fusion.2
  280.1 6.6 fusion.90
  288.8 6.4 add_convert_fusion.3
  295.9 9.7 %collective-permute-done.25.refs_0_ = bf16[1024,512]{1,0:T(8,128)(2,1)S(1)} collective-permute-done((bf16[1024,512]{1,0:T(8,128)(2,1)S(1)}, bf16[1024,512]{1,0:T(8,128)(2,1)S(1)}, u32[]{:S(2)}, u32[]{:S(2)}) %collective-permute-start.25) | collective-permute-done | bytes 1048608 | tf_op jit(solution)/shard_map/ppermute | solution.py:40
  306.8 9.7 %convert_reduce_fusion.3 = (bf16[1024]{0:T(1024)(128)(2,1)S(1)}, bf16[1024,1024]{1,0:T(8,128)(2,1)S(1)}) fusion(f32[1024,1024]{1,0:T(8,128)} %copy-done.110, f32[1024]{0:T(1024)S(1)} %bitcast.315, bf16[1024,2048]{1,0:T(8,128)(2,1)} %copy-done.93, bf16[1024,2048]{1,0:T(8,128)(2,1)} %constant_dynamic-update-slice_fusion.16), kind=kOutput, calls=%fused_computation.35 | convolution fusion | flops 4308597760 | bytes 14686208 | tf_op jit(solution)/shard_map/dot_general | solution.py:31
  316.5 7.7 convert_reduce_fusion.2
  324.3 6.4 fusion.91
  330.6 7.1 add_convert_fusion.2
  342.0 5.1 convolution_convert_fusion.1
  351.1 22.5 %collective-permute-done.31.refs_1_ = bf16[256,2048]{1,0:T(8,128)(2,1)S(1)} collective-permute-done((bf16[256,2048]{1,0:T(8,128)(2,1)S(1)}, bf16[256,2048]{1,0:T(8,128)(2,1)S(1)}, u32[]{:S(2)}, u32[]{:S(2)}) %collective-permute-start.31) | collective-permute-done | bytes 1048608 | tf_op jit(solution)/shard_map/ppermute | solution.py:40
  374.7 5.0 add_convert_fusion.1
  383.0 13.2 %collective-permute-done.32.refs_2_ = bf16[256,2048]{1,0:T(8,128)(2,1)S(1)} collective-permute-done((bf16[256,2048]{1,0:T(8,128)(2,1)}, bf16[256,2048]{1,0:T(8,128)(2,1)S(1)}, u32[]{:S(2)}, u32[]{:S(2)}) %collective-permute-start.32) | collective-permute-done | bytes 1048608 | tf_op jit(solution)/shard_map/ppermute | solution.py:40
  402.0 3.9 convert_reduce_fusion.6
  436.3 5.5 collective-permute-start.36
  441.7 13.7 %collective-permute-done.36 = bf16[256,512]{1,0:T(8,128)(2,1)S(1)} collective-permute-done((bf16[256,512]{1,0:T(8,128)(2,1)S(1)}, bf16[256,512]{1,0:T(8,128)(2,1)S(1)}, u32[]{:S(2)}, u32[]{:S(2)}) %collective-permute-start.36) | collective-permute-done | bytes 262176 | tf_op jit(solution)/shard_map/ppermute | solution.py:45
  456.2 8.8 %collective-permute-start.38 = (bf16[256,512]{1,0:T(8,128)(2,1)}, bf16[256,512]{1,0:T(8,128)(2,1)}, u32[]{:S(2)}, u32[]{:S(2)}) collective-permute-start(bf16[256,512]{1,0:T(8,128)(2,1)} %get-tuple-element.146), channel_id=1, source_target_pairs={{0,2},{2,4},{4,6},{6,0},{1,3},{3,5},{5,7},{7,1},{8,10},{10,12},{12... | collective-permute-start | bytes 786440 | tf_op jit(solution)/shard_map/ppermute | solution.py:45
  464.9 21.8 %collective-permute-done.37 = bf16[256,512]{1,0:T(8,128)(2,1)} collective-permute-done((bf16[256,512]{1,0:T(8,128)(2,1)}, bf16[256,512]{1,0:T(8,128)(2,1)}, u32[]{:S(2)}, u32[]{:S(2)}) %collective-permute-start.37) | collective-permute-done | bytes 262176 | tf_op jit(solution)/shard_map/ppermute | solution.py:45
  505.2 28.3 %attend_back.1 = bf16[8,128,1536]{2,1,0:T(8,128)(2,1)S(1)} custom-call(s32[8]{0:T(128)S(1)} %copy-done.65, f32[8]{0:T(128)S(1)} %copy-done.63, bf16[8,128,1536]{2,1,0:T(8,128)(2,1)} %bitcast.254, bf16[8,128,512]{2,1,0:T(8,128)(2,1)S(1)} %bitcast.251), custom_call_target="tpu_custom_call" | custom-call | flops 32212254720 | bytes 1 | tf_op jit(solution)/shard_map/attend_back/pallas_call | solution.py:245
  548.6 5.5 collective-permute-start.45
  558.9 10.0 %fusion.76 = (bf16[2048]{0:T(1024)(128)(2,1)S(1)}, bf16[2048]{0:T(1024)(128)(2,1)S(1)}, bf16[1024,2048]{1,0:T(8,128)(2,1)S(1)}) fusion(f32[1024]{0:T(1024)S(1)} %copy-done.104, f32[1024]{0:T(1024)S(1)} %copy-done.99, bf16[1024,2048]{1,0:T(8,128)(2,1)} %copy-done.3, bf16[1024,1536]{1,0:T(8,128)(2,1)S(1)} %get-tuple-element.156.refs_1_, ...), kind=kOutput, calls=%fused_computation.308 | convolution fusion | flops 6469709824 | bytes 17842176 | tf_op jit(solution)/shard_map/dot_general | solution.py:31
  582.3 4.4 collective-permute-done.46.refs_3_
  591.3 8.0 fusion.73
  599.4 4.6 copy-done.74
  606.2 9.2 %fusion.92 = f32[1024,2048]{1,0:T(8,128)} fusion(bf16[1024,1024]{1,0:T(8,128)(2,1)S(1)} %copy-done.109, bf16[1024,2048]{1,0:T(8,128)(2,1)} %collective-permute-done.30), kind=kOutput, calls=%fused_computation.324 | convolution fusion | flops 4294967296 | bytes 14680064 | tf_op jit(solution)/shard_map/dot_general | solution.py:23
  617.4 4.8 slice_add_fusion
  626.1 6.9 add_convert_fusion
  634.8 8.2 collective-permute-done.48
  643.0 17.5 %collective-permute-done.50 = bf16[512,768]{0,1:T(8,128)(2,1)S(1)} collective-permute-done((bf16[512,768]{0,1:T(8,128)(2,1)S(1)}, bf16[512,768]{0,1:T(8,128)(2,1)S(1)}, u32[]{:S(2)}, u32[]{:S(2)}) %collective-permute-start.50) | collective-permute-done | bytes 786464 | tf_op jit(solution)/shard_map/ppermute | solution.py:40
  668.5 11.7 %collective-permute-done.52.refs_2_ = bf16[4,256,512]{2,1,0:T(8,128)(2,1)S(1)} collective-permute-done((bf16[4,256,512]{2,1,0:T(8,128)(2,1)}, bf16[4,256,512]{2,1,0:T(8,128)(2,1)S(1)}, u32[]{:S(2)}, u32[]{:S(2)}) %collective-permute-start.52) | collective-permute-done | bytes 1048608 | tf_op jit(solution)/shard_map/ppermute | solution.py:51
  692.2 16.5 %collective-permute-done.53 = bf16[256,2048]{1,0:T(8,128)(2,1)} collective-permute-done((bf16[256,2048]{1,0:T(8,128)(2,1)}, bf16[256,2048]{1,0:T(8,128)(2,1)}, u32[]{:S(2)}, u32[]{:S(2)}) %collective-permute-start.53) | collective-permute-done | bytes 1048608 | tf_op jit(solution)/shard_map/ppermute | solution.py:40
  708.7 22.8 %collective-permute-done.54 = bf16[256,2048]{1,0:T(8,128)(2,1)} collective-permute-done((bf16[256,2048]{1,0:T(8,128)(2,1)}, bf16[256,2048]{1,0:T(8,128)(2,1)}, u32[]{:S(2)}, u32[]{:S(2)}) %collective-permute-start.54) | collective-permute-done | bytes 1048608 | tf_op jit(solution)/shard_map/ppermute | solution.py:40
  736.3 4.4 copy.224
  740.7 29.4 %collective-permute-done.58 = bf16[4,256,512]{2,1,0:T(8,128)(2,1)S(1)} collective-permute-done((bf16[4,256,512]{2,1,0:T(8,128)(2,1)S(1)}, bf16[4,256,512]{2,1,0:T(8,128)(2,1)S(1)}, u32[]{:S(2)}, u32[]{:S(2)}) %collective-permute-start.58) | collective-permute-done | bytes 1048608 | tf_op jit(solution)/shard_map/ppermute | solution.py:51
  774.2 9.9 %reduce-scatter.11.cloned.1.call-done.refs_0_ = bf16[272,2048]{1,0:T(8,128)(2,1)} async-done(((bf16[1088,2048]{1,0:T(8,128)(2,1)}), bf16[272,2048]{1,0:T(8,128)(2,1)}) %reduce-scatter.11.cloned.1.call-update) | async-done | bytes 1114128 | tf_op jit(solution)/shard_map/reduce_scatter | solution.py:539
  795.2 3.9 fusion.32
  813.4 39.8 %all-gather.10.cloned.1.call-done = bf16[1536,1024]{1,0:T(8,128)(2,1)} async-done(((bf16[1536,256]{1,0:T(8,128)(2,1)}), bf16[1536,1024]{1,0:T(8,128)(2,1)}) %all-gather.10.cloned.1.call-update) | async-done | bytes 3145744 | tf_op jit(solution)/shard_map/all_gather | solution.py:569
  853.2 5.5 convert.42
  (605 shorter events, 315.1 us)
Async XLA Ops:
  7.2 86.7 %all-gather.12.cloned.1.call-start = ((), (), s32[]{:S(2)}) async-start(), calls=%async_computation.11 | async-start | bytes 5242880 | tf_op jit(solution)/shard_map/all_gather | solution.py:346
  10.3 385.9 %reduce-scatter.5.cloned.1.call-start = ((), (), s32[]{:S(2)}) async-start(), calls=%async_computation.4 | async-start | bytes 5242880 | tf_op jit(solution)/shard_map/reduce_scatter | solution.py:454
  22.4 95.2 %collective-permute-start.7 = (bf16[1024,512]{1,0:T(8,128)(2,1)}, bf16[1024,512]{1,0:T(8,128)(2,1)}, u32[]{:S(2)}, u32[]{:S(2)}) collective-permute-start(bf16[1024,512]{1,0:T(8,128)(2,1)} %param.23), channel_id=1, source_target_pairs={{0,16},{8,24},{16,0},{24,8},{1,17},{9,25},{17,1},{25,9},{2,18},{10... | collective-permute-start | bytes 3145736 | tf_op jit(solution)/shard_map/ppermute | solution.py:40
  22.9 94.7 %collective-permute-start.6 = (bf16[1024,512]{1,0:T(8,128)(2,1)}, bf16[1024,512]{1,0:T(8,128)(2,1)}, u32[]{:S(2)}, u32[]{:S(2)}) collective-permute-start(bf16[1024,512]{1,0:T(8,128)(2,1)} %param.23), channel_id=1, source_target_pairs={{0,8},{8,0},{16,24},{24,16},{1,9},{9,1},{17,25},{25,17},{2,10},{10... | collective-permute-start | bytes 3145736 | tf_op jit(solution)/shard_map/ppermute | solution.py:40
  73.6 31.8 %collective-permute-start.4 = (bf16[2048,768]{1,0:T(8,128)(2,1)}, bf16[2048,768]{1,0:T(8,128)(2,1)}, u32[]{:S(2)}, u32[]{:S(2)}) collective-permute-start(bf16[2048,768]{1,0:T(8,128)(2,1)} %fusion.50), channel_id=1, source_target_pairs={{0,1},{1,0},{2,3},{3,2},{4,5},{5,4},{6,7},{7,6},{8,9},{9,8},{10,11... | collective-permute-start | bytes 9437192 | tf_op jit(solution)/shard_map/ppermute | solution.py:35
  82.8 56.4 %collective-permute-start.10 = (bf16[512,1024]{1,0:T(8,128)(2,1)}, bf16[512,1024]{1,0:T(8,128)(2,1)}, u32[]{:S(2)}, u32[]{:S(2)}) collective-permute-start(bf16[512,1024]{1,0:T(8,128)(2,1)} %get-tuple-element.104), channel_id=1, source_target_pairs={{0,8},{8,0},{16,24},{24,16},{1,9},{9,1},{17,25},{25,17},{2,10},{10... | collective-permute-start | bytes 3145736 | tf_op jit(solution)/shard_map/ppermute | solution.py:40
  86.5 52.7 %collective-permute-start.11 = (bf16[512,1024]{1,0:T(8,128)(2,1)}, bf16[512,1024]{1,0:T(8,128)(2,1)}, u32[]{:S(2)}, u32[]{:S(2)}) collective-permute-start(bf16[512,1024]{1,0:T(8,128)(2,1)} %get-tuple-element.105), channel_id=1, source_target_pairs={{0,16},{8,24},{16,0},{24,8},{1,17},{9,25},{17,1},{25,9},{2,18},{10... | collective-permute-start | bytes 3145736 | tf_op jit(solution)/shard_map/ppermute | solution.py:40
  105.5 33.8 %collective-permute-start.12 = (bf16[512,1024]{1,0:T(8,128)(2,1)S(1)}, bf16[512,1024]{1,0:T(8,128)(2,1)S(1)}, u32[]{:S(2)}, u32[]{:S(2)}) collective-permute-start(bf16[512,1024]{1,0:T(8,128)(2,1)S(1)} %copy-done.49), channel_id=1, source_target_pairs={{0,24},{8,16},{16,8},{24,0},{1,25},{9,17},{17,9},{25,1},{2,26},{10... | collective-permute-start | bytes 3145736 | tf_op jit(solution)/shard_map/ppermute | solution.py:40
  120.8 25.0 %collective-permute-start.9 = (bf16[512,512]{1,0:T(8,128)(2,1)S(1)}, bf16[512,512]{1,0:T(8,128)(2,1)S(1)}, u32[]{:S(2)}, u32[]{:S(2)}) collective-permute-start(bf16[512,512]{1,0:T(8,128)(2,1)S(1)} %slice.419), channel_id=1, source_target_pairs={{0,16},{8,24},{16,0},{24,8},{1,17},{9,25},{17,1},{25,9},{2,18},{10... | collective-permute-start | bytes 1572872 | tf_op jit(solution)/shard_map/ppermute | solution.py:40
  155.1 35.2 %collective-permute-start.13 = (bf16[1024,2048]{1,0:T(8,128)(2,1)}, bf16[1024,2048]{1,0:T(8,128)(2,1)}, u32[]{:S(2)}, u32[]{:S(2)}) collective-permute-start(bf16[1024,2048]{1,0:T(8,128)(2,1)} %maximum_dynamic-update-slice_fusion), channel_id=1, source_target_pairs={{0,1},{1,0},{2,3},{3,2},{4,5},{5,4},{6,7},{7,6},{8,9},{9,8},{10,11... | collective-permute-start | bytes 12582920 | tf_op jit(solution)/shard_map/ppermute | solution.py:35
  155.3 33.5 %collective-permute-start.18 = (bf16[256,2048]{1,0:T(8,128)(2,1)}, bf16[256,2048]{1,0:T(8,128)(2,1)S(1)}, u32[]{:S(2)}, u32[]{:S(2)}) collective-permute-start(bf16[256,2048]{1,0:T(8,128)(2,1)} %get-tuple-element.112), channel_id=1, source_target_pairs={{0,16},{8,24},{16,0},{24,8},{1,17},{9,25},{17,1},{25,9},{2,18},{10... | collective-permute-start | bytes 3145736 | tf_op jit(solution)/shard_map/ppermute | solution.py:40
  155.8 34.5 %collective-permute-start.17 = (bf16[256,2048]{1,0:T(8,128)(2,1)}, bf16[256,2048]{1,0:T(8,128)(2,1)S(1)}, u32[]{:S(2)}, u32[]{:S(2)}) collective-permute-start(bf16[256,2048]{1,0:T(8,128)(2,1)} %get-tuple-element.112), channel_id=1, source_target_pairs={{0,8},{8,0},{16,24},{24,16},{1,9},{9,1},{17,25},{25,17},{2,10},{10... | collective-permute-start | bytes 3145736 | tf_op jit(solution)/shard_map/ppermute | solution.py:40
  177.7 83.6 %collective-permute-start.28 = (bf16[2048,1024]{1,0:T(8,128)(2,1)}, bf16[2048,1024]{1,0:T(8,128)(2,1)}, u32[]{:S(2)}, u32[]{:S(2)}) collective-permute-start(bf16[2048,1024]{1,0:T(8,128)(2,1)} %constant_dynamic-update-slice_fusion.17), channel_id=1, source_target_pairs={{0,1},{1,0},{2,3},{3,2},{4,5},{5,4},{6,7},{7,6},{8,9},{9,8},{10,11... | collective-permute-start | bytes 12582920 | tf_op jit(solution)/shard_map/ppermute | solution.py:35
  187.3 26.4 %collective-permute-start.21 = (bf16[1024,512]{1,0:T(8,128)(2,1)}, bf16[1024,512]{1,0:T(8,128)(2,1)}, u32[]{:S(2)}, u32[]{:S(2)}) collective-permute-start(bf16[1024,512]{1,0:T(8,128)(2,1)} %get-tuple-element.125.refs_3_), channel_id=1, source_target_pairs={{0,8},{8,0},{16,24},{24,16},{1,9},{9,1},{17,25},{25,17},{2,10},{10... | collective-permute-start | bytes 3145736 | tf_op jit(solution)/shard_map/ppermute | solution.py:40
  188.8 26.4 %collective-permute-start.22 = (bf16[1024,512]{1,0:T(8,128)(2,1)}, bf16[1024,512]{1,0:T(8,128)(2,1)}, u32[]{:S(2)}, u32[]{:S(2)}) collective-permute-start(bf16[1024,512]{1,0:T(8,128)(2,1)} %get-tuple-element.126.refs_4_), channel_id=1, source_target_pairs={{0,16},{8,24},{16,0},{24,8},{1,17},{9,25},{17,1},{25,9},{2,18},{10... | collective-permute-start | bytes 3145736 | tf_op jit(solution)/shard_map/ppermute | solution.py:40
  196.3 26.4 %collective-permute-start.19 = (bf16[128,2048]{1,0:T(8,128)(2,1)S(1)}, bf16[128,2048]{1,0:T(8,128)(2,1)S(1)}, u32[]{:S(2)}, u32[]{:S(2)}) collective-permute-start(bf16[128,2048]{1,0:T(8,128)(2,1)S(1)} %slice.423), channel_id=1, source_target_pairs={{0,8},{8,0},{16,24},{24,16},{1,9},{9,1},{17,25},{25,17},{2,10},{10... | collective-permute-start | bytes 1572872 | tf_op jit(solution)/shard_map/ppermute | solution.py:40
  196.9 27.0 %collective-permute-start.20 = (bf16[128,2048]{1,0:T(8,128)(2,1)S(1)}, bf16[128,2048]{1,0:T(8,128)(2,1)S(1)}, u32[]{:S(2)}, u32[]{:S(2)}) collective-permute-start(bf16[128,2048]{1,0:T(8,128)(2,1)S(1)} %slice.424), channel_id=1, source_target_pairs={{0,16},{8,24},{16,0},{24,8},{1,17},{9,25},{17,1},{25,9},{2,18},{10... | collective-permute-start | bytes 1572872 | tf_op jit(solution)/shard_map/ppermute | solution.py:40
  279.1 26.5 %collective-permute-start.25 = (bf16[1024,512]{1,0:T(8,128)(2,1)S(1)}, bf16[1024,512]{1,0:T(8,128)(2,1)S(1)}, u32[]{:S(2)}, u32[]{:S(2)}) collective-permute-start(bf16[1024,512]{1,0:T(8,128)(2,1)S(1)} %get-tuple-element.128), channel_id=1, source_target_pairs={{0,24},{8,16},{16,8},{24,0},{1,25},{9,17},{17,9},{25,1},{2,26},{10... | collective-permute-start | bytes 3145736 | tf_op jit(solution)/shard_map/ppermute | solution.py:40
  306.7 187.0 %reduce-scatter.7.cloned.1.call-start = ((), (), s32[]{:S(2)}) async-start(), calls=%async_computation.5 | async-start | bytes 5242880 | tf_op jit(solution)/shard_map/reduce_scatter | solution.py:462
  347.1 27.6 %collective-permute-start.34 = (bf16[2048,1024]{1,0:T(8,128)(2,1)S(1)}, bf16[2048,1024]{1,0:T(8,128)(2,1)S(1)}, u32[]{:S(2)}, u32[]{:S(2)}) collective-permute-start(bf16[2048,1024]{1,0:T(8,128)(2,1)S(1)} %convolution_convert_fusion.1), channel_id=1, source_target_pairs={{0,1},{1,0},{2,3},{3,2},{4,5},{5,4},{6,7},{7,6},{8,9},{9,8},{10,11... | collective-permute-start | bytes 12582920 | tf_op jit(solution)/shard_map/ppermute | solution.py:35
  347.7 26.0 %collective-permute-start.31 = (bf16[256,2048]{1,0:T(8,128)(2,1)S(1)}, bf16[256,2048]{1,0:T(8,128)(2,1)S(1)}, u32[]{:S(2)}, u32[]{:S(2)}) collective-permute-start(bf16[256,2048]{1,0:T(8,128)(2,1)S(1)} %get-tuple-element.136), channel_id=1, source_target_pairs={{0,8},{8,0},{16,24},{24,16},{1,9},{9,1},{17,25},{25,17},{2,10},{10... | collective-permute-start | bytes 3145736 | tf_op jit(solution)/shard_map/ppermute | solution.py:40
  348.7 47.5 %collective-permute-start.32 = (bf16[256,2048]{1,0:T(8,128)(2,1)}, bf16[256,2048]{1,0:T(8,128)(2,1)S(1)}, u32[]{:S(2)}, u32[]{:S(2)}) collective-permute-start(bf16[256,2048]{1,0:T(8,128)(2,1)} %get-tuple-element.137), channel_id=1, source_target_pairs={{0,16},{8,24},{16,0},{24,8},{1,17},{9,25},{17,1},{25,9},{2,18},{10... | collective-permute-start | bytes 3145736 | tf_op jit(solution)/shard_map/ppermute | solution.py:40
  349.3 46.9 %collective-permute-start.33 = (bf16[256,2048]{1,0:T(8,128)(2,1)}, bf16[256,2048]{1,0:T(8,128)(2,1)S(1)}, u32[]{:S(2)}, u32[]{:S(2)}) collective-permute-start(bf16[256,2048]{1,0:T(8,128)(2,1)} %get-tuple-element.138), channel_id=1, source_target_pairs={{0,24},{8,16},{16,8},{24,0},{1,25},{9,17},{17,9},{25,1},{2,26},{10... | collective-permute-start | bytes 3145736 | tf_op jit(solution)/shard_map/ppermute | solution.py:40
  382.2 153.8 %reduce-scatter.9.cloned.1.call-start = ((), (), s32[]{:S(2)}) async-start(), calls=%async_computation.6 | async-start | bytes 1310720 | tf_op jit(solution)/shard_map/reduce_scatter | solution.py:492
  432.8 57.5 %collective-permute-start.39 = (bf16[1024,512]{1,0:T(8,128)(2,1)S(1)}, bf16[1024,512]{1,0:T(8,128)(2,1)}, u32[]{:S(2)}, u32[]{:S(2)}) collective-permute-start(bf16[1024,512]{1,0:T(8,128)(2,1)S(1)} %get-tuple-element.149), channel_id=1, source_target_pairs={{0,8},{8,0},{16,24},{24,16},{1,9},{9,1},{17,25},{25,17},{2,10},{10... | collective-permute-start | bytes 3145736 | tf_op jit(solution)/shard_map/ppermute | solution.py:40
  433.8 56.4 %collective-permute-start.40 = (bf16[1024,512]{1,0:T(8,128)(2,1)}, bf16[1024,512]{1,0:T(8,128)(2,1)}, u32[]{:S(2)}, u32[]{:S(2)}) collective-permute-start(bf16[1024,512]{1,0:T(8,128)(2,1)} %get-tuple-element.150), channel_id=1, source_target_pairs={{0,16},{8,24},{16,0},{24,8},{1,17},{9,25},{17,1},{25,9},{2,18},{10... | collective-permute-start | bytes 3145736 | tf_op jit(solution)/shard_map/ppermute | solution.py:40
  434.6 55.6 %collective-permute-start.41 = (bf16[1024,512]{1,0:T(8,128)(2,1)}, bf16[1024,512]{1,0:T(8,128)(2,1)}, u32[]{:S(2)}, u32[]{:S(2)}) collective-permute-start(bf16[1024,512]{1,0:T(8,128)(2,1)} %get-tuple-element.151), channel_id=1, source_target_pairs={{0,24},{8,16},{16,8},{24,0},{1,25},{9,17},{17,9},{25,1},{2,26},{10... | collective-permute-start | bytes 3145736 | tf_op jit(solution)/shard_map/ppermute | solution.py:40
  441.7 45.1 %collective-permute-start.37 = (bf16[256,512]{1,0:T(8,128)(2,1)}, bf16[256,512]{1,0:T(8,128)(2,1)}, u32[]{:S(2)}, u32[]{:S(2)}) collective-permute-start(bf16[256,512]{1,0:T(8,128)(2,1)} %get-tuple-element.145), channel_id=1, source_target_pairs={{0,4},{2,6},{4,0},{6,2},{1,5},{3,7},{5,1},{7,3},{8,12},{10,14},{12... | collective-permute-start | bytes 786440 | tf_op jit(solution)/shard_map/ppermute | solution.py:45
  456.2 30.6 %collective-permute-start.38 = (bf16[256,512]{1,0:T(8,128)(2,1)}, bf16[256,512]{1,0:T(8,128)(2,1)}, u32[]{:S(2)}, u32[]{:S(2)}) collective-permute-start(bf16[256,512]{1,0:T(8,128)(2,1)} %get-tuple-element.146), channel_id=1, source_target_pairs={{0,2},{2,4},{4,6},{6,0},{1,3},{3,5},{5,7},{7,1},{8,10},{10,12},{12... | collective-permute-start | bytes 786440 | tf_op jit(solution)/shard_map/ppermute | solution.py:45
  498.3 83.2 %all-gather.6.cloned.1.call-start = ((), (), s32[]{:S(2)}) async-start(), calls=%async_computation.7 | async-start | bytes 1310720 | tf_op jit(solution)/shard_map/all_gather | solution.py:504
  500.2 34.0 %collective-permute-start.42 = (bf16[512,512]{1,0:T(8,128)(2,1)S(1)}, bf16[512,512]{1,0:T(8,128)(2,1)S(1)}, u32[]{:S(2)}, u32[]{:S(2)}) collective-permute-start(bf16[512,512]{1,0:T(8,128)(2,1)S(1)} %pad_maximum_fusion.6), channel_id=1, source_target_pairs={{0,8},{8,0},{16,24},{24,16},{1,9},{9,1},{17,25},{25,17},{2,10},{10... | collective-permute-start | bytes 1572872 | tf_op jit(solution)/shard_map/ppermute | solution.py:40
  501.3 32.8 %collective-permute-start.43 = (bf16[512,512]{1,0:T(8,128)(2,1)S(1)}, bf16[512,512]{1,0:T(8,128)(2,1)S(1)}, u32[]{:S(2)}, u32[]{:S(2)}) collective-permute-start(bf16[512,512]{1,0:T(8,128)(2,1)S(1)} %pad_maximum_fusion.7), channel_id=1, source_target_pairs={{0,16},{8,24},{16,0},{24,8},{1,17},{9,25},{17,1},{25,9},{2,18},{10... | collective-permute-start | bytes 1572872 | tf_op jit(solution)/shard_map/ppermute | solution.py:40
  502.9 31.3 %collective-permute-start.44 = (bf16[512,512]{1,0:T(8,128)(2,1)S(1)}, bf16[512,512]{1,0:T(8,128)(2,1)S(1)}, u32[]{:S(2)}, u32[]{:S(2)}) collective-permute-start(bf16[512,512]{1,0:T(8,128)(2,1)S(1)} %pad_maximum_fusion.8), channel_id=1, source_target_pairs={{0,24},{8,16},{16,8},{24,0},{1,25},{9,17},{17,9},{25,1},{2,26},{10... | collective-permute-start | bytes 1572872 | tf_op jit(solution)/shard_map/ppermute | solution.py:40
  537.6 236.5 %all-gather.8.cloned.1.call-start = ((), (), s32[]{:S(2)}) async-start(), calls=%async_computation.9 | async-start | bytes 5242880 | tf_op jit(solution)/shard_map/all_gather | solution.py:507
  547.4 39.3 %collective-permute-start.46 = (bf16[4,256,512]{2,1,0:T(8,128)(2,1)}, bf16[4,256,512]{2,1,0:T(8,128)(2,1)}, u32[]{:S(2)}, u32[]{:S(2)}) collective-permute-start(bf16[4,256,512]{2,1,0:T(8,128)(2,1)} %fusion.51), channel_id=1, source_target_pairs={{2,0},{4,2},{6,4},{3,1},{5,3},{7,5},{10,8},{12,10},{14,12},{11,9},... | collective-permute-start | bytes 3145736 | tf_op jit(solution)/shard_map/ppermute | solution.py:51
  548.6 38.0 %collective-permute-start.45 = (bf16[4,256,512]{2,1,0:T(8,128)(2,1)}, bf16[4,256,512]{2,1,0:T(8,128)(2,1)}, u32[]{:S(2)}, u32[]{:S(2)}) collective-permute-start(bf16[4,256,512]{2,1,0:T(8,128)(2,1)} %fusion.51), channel_id=1, source_target_pairs={{0,2},{2,4},{4,6},{1,3},{3,5},{5,7},{8,10},{10,12},{12,14},{9,11},... | collective-permute-start | bytes 3145736 | tf_op jit(solution)/shard_map/ppermute | solution.py:50
  558.3 225.8 %reduce-scatter.11.cloned.1.call-start = ((), (), s32[]{:S(2)}) async-start(), calls=%async_computation.8 | async-start | bytes 5570560 | tf_op jit(solution)/shard_map/reduce_scatter | solution.py:539
  606.1 247.0 %all-gather.10.cloned.1.call-start = ((), (), s32[]{:S(2)}) async-start(), calls=%async_computation.10 | async-start | bytes 3932160 | tf_op jit(solution)/shard_map/all_gather | solution.py:569
  615.3 53.2 %collective-permute-start.51 = (bf16[4,256,512]{2,1,0:T(8,128)(2,1)}, bf16[4,256,512]{2,1,0:T(8,128)(2,1)S(1)}, u32[]{:S(2)}, u32[]{:S(2)}) collective-permute-start(bf16[4,256,512]{2,1,0:T(8,128)(2,1)} %get-tuple-element.159), channel_id=1, source_target_pairs={{2,4},{4,6},{3,5},{5,7},{10,12},{12,14},{11,13},{13,15},{18,20},{2... | collective-permute-start | bytes 3145736 | tf_op jit(solution)/shard_map/ppermute | solution.py:50
  616.1 64.1 %collective-permute-start.52 = (bf16[4,256,512]{2,1,0:T(8,128)(2,1)}, bf16[4,256,512]{2,1,0:T(8,128)(2,1)S(1)}, u32[]{:S(2)}, u32[]{:S(2)}) collective-permute-start(bf16[4,256,512]{2,1,0:T(8,128)(2,1)} %get-tuple-element.160), channel_id=1, source_target_pairs={{2,0},{4,2},{3,1},{5,3},{10,8},{12,10},{11,9},{13,11},{18,16},{20,... | collective-permute-start | bytes 3145736 | tf_op jit(solution)/shard_map/ppermute | solution.py:51
  624.1 36.3 %collective-permute-start.50 = (bf16[512,768]{0,1:T(8,128)(2,1)S(1)}, bf16[512,768]{0,1:T(8,128)(2,1)S(1)}, u32[]{:S(2)}, u32[]{:S(2)}) collective-permute-start(bf16[512,768]{0,1:T(8,128)(2,1)S(1)} %get-tuple-element.192), channel_id=1, source_target_pairs={{0,24},{8,16},{16,8},{24,0},{1,25},{9,17},{17,9},{25,1},{2,26},{10... | collective-permute-start | bytes 2359304 | tf_op jit(solution)/shard_map/ppermute | solution.py:40
  625.6 36.2 %collective-permute-start.49 = (bf16[512,768]{0,1:T(8,128)(2,1)S(1)}, bf16[512,768]{0,1:T(8,128)(2,1)S(1)}, u32[]{:S(2)}, u32[]{:S(2)}) collective-permute-start(bf16[512,768]{0,1:T(8,128)(2,1)S(1)} %get-tuple-element.193), channel_id=1, source_target_pairs={{0,16},{8,24},{16,0},{24,8},{1,17},{9,25},{17,1},{25,9},{2,18},{10... | collective-permute-start | bytes 2359304 | tf_op jit(solution)/shard_map/ppermute | solution.py:40
  682.4 26.3 %collective-permute-start.53 = (bf16[256,2048]{1,0:T(8,128)(2,1)}, bf16[256,2048]{1,0:T(8,128)(2,1)}, u32[]{:S(2)}, u32[]{:S(2)}) collective-permute-start(bf16[256,2048]{1,0:T(8,128)(2,1)} %copy-done.55), channel_id=1, source_target_pairs={{0,8},{8,0},{16,24},{24,16},{1,9},{9,1},{17,25},{25,17},{2,10},{10... | collective-permute-start | bytes 3145736 | tf_op jit(solution)/shard_map/ppermute | solution.py:40
  683.8 47.7 %collective-permute-start.54 = (bf16[256,2048]{1,0:T(8,128)(2,1)}, bf16[256,2048]{1,0:T(8,128)(2,1)}, u32[]{:S(2)}, u32[]{:S(2)}) collective-permute-start(bf16[256,2048]{1,0:T(8,128)(2,1)} %get-tuple-element.163), channel_id=1, source_target_pairs={{0,16},{8,24},{16,0},{24,8},{1,17},{9,25},{17,1},{25,9},{2,18},{10... | collective-permute-start | bytes 3145736 | tf_op jit(solution)/shard_map/ppermute | solution.py:40
  685.3 46.2 %collective-permute-start.55 = (bf16[256,2048]{1,0:T(8,128)(2,1)}, bf16[256,2048]{1,0:T(8,128)(2,1)}, u32[]{:S(2)}, u32[]{:S(2)}) collective-permute-start(bf16[256,2048]{1,0:T(8,128)(2,1)} %get-tuple-element.164), channel_id=1, source_target_pairs={{0,24},{8,16},{16,8},{24,0},{1,25},{9,17},{17,9},{25,1},{2,26},{10... | collective-permute-start | bytes 3145736 | tf_op jit(solution)/shard_map/ppermute | solution.py:40
  686.3 48.0 %collective-permute-start.57 = (bf16[4,256,512]{2,1,0:T(8,128)(2,1)S(1)}, bf16[4,256,512]{2,1,0:T(8,128)(2,1)}, u32[]{:S(2)}, u32[]{:S(2)}) collective-permute-start(bf16[4,256,512]{2,1,0:T(8,128)(2,1)S(1)} %get-tuple-element.167), channel_id=1, source_target_pairs={{4,6},{5,7},{12,14},{13,15},{20,22},{21,23},{28,30},{29,31}} | collective-permute-start | bytes 3145736 | tf_op jit(solution)/shard_map/ppermute | solution.py:50
  690.6 79.6 %collective-permute-start.58 = (bf16[4,256,512]{2,1,0:T(8,128)(2,1)S(1)}, bf16[4,256,512]{2,1,0:T(8,128)(2,1)S(1)}, u32[]{:S(2)}, u32[]{:S(2)}) collective-permute-start(bf16[4,256,512]{2,1,0:T(8,128)(2,1)S(1)} %get-tuple-element.168), channel_id=1, source_target_pairs={{2,0},{3,1},{10,8},{11,9},{18,16},{19,17},{26,24},{27,25}} | collective-permute-start | bytes 3145736 | tf_op jit(solution)/shard_map/ppermute | solution.py:51
  734.2 38.3 %collective-permute-start.56 = (bf16[256,2048]{1,0:T(8,128)(2,1)S(1)}, bf16[256,2048]{1,0:T(8,128)(2,1)S(1)}, u32[]{:S(2)}, u32[]{:S(2)}) collective-permute-start(bf16[256,2048]{1,0:T(8,128)(2,1)S(1)} %add_convert_fusion.5), channel_id=1, source_target_pairs={{0,1},{1,0},{2,3},{3,2},{4,5},{5,4},{6,7},{7,6},{8,9},{9,8},{10,11... | collective-permute-start | bytes 3145736 | tf_op jit(solution)/shard_map/ppermute | solution.py:35
  (138 other events, 1519.5 us)
Sparse Core Ops, SparseCore 0:
  10.4 83.4 all-gather.11
  306.8 78.4 reduce-scatter.4
  388.3 93.7 reduce-scatter.6
  498.5 26.2 reduce-scatter.8
  537.8 35.1 all-gather.5
  574.4 103.3 all-gather.7
  680.8 103.2 reduce-scatter.10
  789.7 63.3 all-gather.9

commit v5 on v4

--- a/solution.py
+++ b/solution.py
@@ -502,9 +502,8 @@
     grad_qkv = attend_back(order, slopes, qkv, grad_tree)
     grad_qkv, grad_out = gate([grad_qkv, grad_out], *both[1:])
     g_out = lax.all_gather(grad_out, "context", axis=0, tiled=True)
-    g_up = jnp.concatenate([piece[lines:] for piece in both])
-    grad_down = place([piece[None, :lines] for piece in both], 0, zero_from(g_up))
-    g_up = lax.all_gather(g_up, "context", axis=0, tiled=True)
+    grad_down = place([piece[None, :lines] for piece in both], 0, zero_from(grad_qkv))
+    up_blocks = [piece[lines:] for piece in both]
     down_up, down_down = line_step([grad_down], [grad_down])
 
     grad_normed = dot_nt(grad_qkv, w_heads)
@@ -537,6 +536,9 @@
     )
     later = zero_from(blocks)
     grad_first = lax.psum_scatter(blocks, "context", scatter_dimension=0, tiled=True)
+    upper = up_blocks[0].shape[0]
+    up_blocks[0] = lax.dynamic_slice_in_dim(both[0], upper + later, upper, 0)
+    g_up = lax.all_gather(jnp.concatenate(up_blocks), "context", axis=0, tiled=True)
 
     down_up, down_down = line_step(down_up, down_down)
     grad_heads = dot_tn(normed, grad_qkv)
@@ -550,15 +552,15 @@
         lax.dynamic_slice_in_dim(active_own, later, groups * rows, 0), down_own
     ) + dot_nn(lax.dynamic_slice_in_dim(active_other, later, groups * rows, 0), down_other)
     layer_out = layer_out.astype(BF16)
-    grad_heads, down_up[-1], down_down[-1], *layer_blocks = gate(
-        [grad_heads, down_up[-1], down_down[-1]]
+    grad_first, grad_heads, down_up[-1], down_down[-1], *layer_blocks = gate(
+        [grad_first, grad_heads, down_up[-1], down_down[-1]]
         + [layer_out[k * rows : (k + 1) * rows] for k in range(groups)]
     )
     while len(down_up) < planes:
         down_up, down_down = line_step(down_up, down_down)
     layer_blocks[1:] = send_blocks(layer_blocks[1:])
-    grad_first, grad_heads, g_up, g_out = gate(
-        [grad_first, grad_heads, g_up, g_out],
+    grad_heads, g_up, g_out = gate(
+        [grad_heads, g_up, g_out],
         down_up[-1],
         down_down[-1],
         *layer_blocks[1:],

time: 873 us -> 888 us (1.017)
  other arithmetic: 70.2 us -> 80.4 us
  waiting for transfers between devices: 348 us -> 357 us
    all_gather x1, waiting for transfers between devices: 0.01 us -> 20.5 us  [per_device(): g_out = lax.all_gather(grad_out, 'context', axis=0, tiled=True)]
    ppermute x3, waiting for transfers between devices: 45.5 us -> 56.8 us  [line_step(): lax.ppermute(downward[-1], 'context', [(i + 1, i) for i in range(0, size...]
    unnamed x264 -> x268, local copies, waits for them, and re-layouts: 83 us -> 72.2 us
    reduce_scatter x1, waiting for transfers between devices: 9.91 us -> 0.01 us  [per_device(): lax.psum_scatter(blocks, 'context', scatter_dimension=0, tiled=True)]
  transfers between devices with their start and end apart: 72 -> 72, of which waited for: 32 -> 32; matrix products, arithmetic and copies ran while one was open for 33% -> 32% of each run, Pallas kernels for 5% -> 5%
where the time goes in v5:
time: 888 us; the launch traced here: 881 us
  waiting for transfers between devices  357 us (40%)
  local copies, waits for them, and re-layouts  168 us (19%)
  matrix products  133 us (15%)
  other arithmetic  80.4 us (9%)
  starting transfers between devices  78.1 us (9%)
  Pallas kernels  46.2 us (5%)
  between operations  18.1 us (2%)
    ppermute x40, waiting for transfers between devices, xor_send(): return lax.ppermute(value, 'fsdp', [(i, i ^ step) for i in range(size)])  188 us
    unnamed x268, local copies, waits for them, and re-layouts  72.2 us
    ppermute x3, waiting for transfers between devices, line_step(): lax.ppermute(downward[-1], 'context', [(i + 1, i) for i in range(0, size...  56.8 us
    dot_general x7, matrix products, dot_nt(): lax.dot_general(left, right, (((1,), (1,)), ((), ())), preferred_element_...  49 us
    ppermute x6, waiting for transfers between devices, ring_send(): lax.ppermute(value, 'context', [(i, (i + step) % size) for i in range(siz...  48.5 us
    dot_general x7, matrix products, dot_nn(): lax.dot_general(left, right, (((1,), (0,)), ((), ())), preferred_element_...  45.9 us
    ppermute x40, starting transfers between devices, xor_send(): return lax.ppermute(value, 'fsdp', [(i, i ^ step) for i in range(size)])  43.8 us
    dot_general x7, matrix products, dot_tn(): lax.dot_general(left, right, (((0,), (0,)), ((), ())), preferred_element_...  37.9 us
  transfers between devices with their start and end apart: 72, of which 32 were waited for; matrix products, arithmetic and copies ran while one was open for 32% of the time, Pallas kernels for 5%

profile of v5, /device:TPU:0, one launch (start us, length us, event | category | flops | bytes accessed | tf_op | source)
XLA Modules:
  0.0 881.1 jit_solution(7449976879379411626)
XLA Ops:
  28.7 11.9 %collective-permute-done.1.refs_1_ = bf16[544,768]{1,0:T(8,128)(2,1)S(1)} collective-permute-done((bf16[544,768]{1,0:T(8,128)(2,1)}, bf16[544,768]{1,0:T(8,128)(2,1)S(1)}, u32[]{:S(2)}, u32[]{:S(2)}) %collective-permute-start.1) | collective-permute-done | bytes 835616 | tf_op jit(solution)/shard_map/ppermute | solution.py:40
  56.6 14.5 %collective-permute-done.3 = bf16[272,768]{1,0:T(8,128)(2,1)S(1)} collective-permute-done((bf16[272,768]{1,0:T(8,128)(2,1)S(1)}, bf16[272,768]{1,0:T(8,128)(2,1)S(1)}, u32[]{:S(2)}, u32[]{:S(2)}) %collective-permute-start.3) | collective-permute-done | bytes 417824 | tf_op jit(solution)/shard_map/ppermute | solution.py:40
  87.3 6.6 all-gather.12.cloned.1.call-done
  107.9 9.6 %add_convert_fusion.4.refs_0_ = bf16[1024,1536]{1,0:T(8,128)(2,1)S(1)} fusion(bf16[2048,768]{1,0:T(8,128)(2,1)} %collective-permute-done.4, bf16[2048,768]{1,0:T(8,128)(2,1)} %fusion.50, f32[1536]{0:T(1024)S(1)} %add.506, bf16[1024,2048]{1,0:T(8,128)(2,1)S(1)} %copy-done.4, f32[2048]{0:T(1024)S(1)} %bitcast.313, f32[2048]{0:T(1024)S(1)} %bitcast.297, ...), kind=kOutput, calls=%fused_computation.21 | convolution fusion | flops 6470762496 | bytes 13662208 | tf_op jit(solution)/shard_map/dot_general | solution.py:23
  121.3 17.9 %attend.1 = bf16[8,128,512]{2,1,0:T(8,128)(2,1)S(1)} custom-call(s32[8]{0:T(128)S(1)} %select_reduce_fusion.order, f32[8]{0:T(128)S(1)} %fusion.72.slopes, bf16[8,128,1536]{2,1,0:T(8,128)(2,1)S(1)} %bitcast.255), custom_call_target="tpu_custom_call" | custom-call | flops 17179869184 | bytes 1 | tf_op jit(solution)/shard_map/attend/pallas_call | solution.py:223
  177.7 9.6 %collective-permute-done.15.refs_3_ = bf16[256,512]{1,0:T(8,128)(2,1)S(1)} collective-permute-done((bf16[256,512]{1,0:T(8,128)(2,1)S(1)}, bf16[256,512]{1,0:T(8,128)(2,1)S(1)}, u32[]{:S(2)}, u32[]{:S(2)}) %collective-permute-start.15) | collective-permute-done | bytes 262176 | tf_op jit(solution)/shard_map/ppermute | solution.py:45
  205.4 8.3 collective-permute-done.21
  215.2 7.4 collective-permute-done.19
  229.6 19.2 %collective-permute-done.24.refs_1_ = bf16[256,2048]{1,0:T(8,128)(2,1)S(1)} collective-permute-done((bf16[256,2048]{1,0:T(8,128)(2,1)S(1)}, bf16[256,2048]{1,0:T(8,128)(2,1)S(1)}, u32[]{:S(2)}, u32[]{:S(2)}) %collective-permute-start.24) | collective-permute-done | bytes 1048608 | tf_op jit(solution)/shard_map/ppermute | solution.py:40
  252.3 9.0 %collective-permute-done.26 = bf16[128,2048]{1,0:T(8,128)(2,1)S(1)} collective-permute-done((bf16[128,2048]{1,0:T(8,128)(2,1)S(1)}, bf16[128,2048]{1,0:T(8,128)(2,1)S(1)}, u32[]{:S(2)}, u32[]{:S(2)}) %collective-permute-start.26) | collective-permute-done | bytes 524320 | tf_op jit(solution)/shard_map/ppermute | solution.py:40
  261.4 10.0 %multiply_convert_fusion = (bf16[1024,1024]{1,0:T(8,128)(2,1)S(1)}, f32[1024,1024]{1,0:T(8,128)}) fusion(f32[1024]{0:T(1024)S(1)} %bitcast.319, bf16[1024,2048]{1,0:T(8,128)(2,1)S(1)} %constant_dynamic-update-slice_fusion.5, bf16[2048,1024]{1,0:T(8,128)(2,1)} %collective-permute-done.28), kind=kOutput, calls=%fused_computation.36 | convolution fusion | flops 4301258752 | bytes 14684160 | tf_op jit(solution)/shard_map/dot_general | solution.py:23
  271.4 4.8 convolution_convert_fusion.2
  280.1 6.6 fusion.93
  288.8 6.4 add_convert_fusion.3
  295.8 9.7 %collective-permute-done.25.refs_0_ = bf16[1024,512]{1,0:T(8,128)(2,1)S(1)} collective-permute-done((bf16[1024,512]{1,0:T(8,128)(2,1)S(1)}, bf16[1024,512]{1,0:T(8,128)(2,1)S(1)}, u32[]{:S(2)}, u32[]{:S(2)}) %collective-permute-start.25) | collective-permute-done | bytes 1048608 | tf_op jit(solution)/shard_map/ppermute | solution.py:40
  306.8 9.7 %convert_reduce_fusion.3 = (bf16[1024]{0:T(1024)(128)(2,1)S(1)}, bf16[1024,1024]{1,0:T(8,128)(2,1)S(1)}) fusion(f32[1024,1024]{1,0:T(8,128)} %copy-done.114, f32[1024]{0:T(1024)S(1)} %bitcast.317, bf16[1024,2048]{1,0:T(8,128)(2,1)} %copy-done.97, bf16[1024,2048]{1,0:T(8,128)(2,1)} %constant_dynamic-update-slice_fusion.16), kind=kOutput, calls=%fused_computation.35 | convolution fusion | flops 4308597760 | bytes 14686208 | tf_op jit(solution)/shard_map/dot_general | solution.py:31
  316.5 7.7 convert_reduce_fusion.2
  324.3 6.4 fusion.94
  330.6 7.1 add_convert_fusion.2
  342.0 5.1 convolution_convert_fusion.1
  351.2 22.5 %collective-permute-done.31.refs_1_ = bf16[256,2048]{1,0:T(8,128)(2,1)S(1)} collective-permute-done((bf16[256,2048]{1,0:T(8,128)(2,1)S(1)}, bf16[256,2048]{1,0:T(8,128)(2,1)S(1)}, u32[]{:S(2)}, u32[]{:S(2)}) %collective-permute-start.31) | collective-permute-done | bytes 1048608 | tf_op jit(solution)/shard_map/ppermute | solution.py:40
  374.7 5.0 add_convert_fusion.1
  383.0 13.3 %collective-permute-done.32.refs_2_ = bf16[256,2048]{1,0:T(8,128)(2,1)S(1)} collective-permute-done((bf16[256,2048]{1,0:T(8,128)(2,1)}, bf16[256,2048]{1,0:T(8,128)(2,1)S(1)}, u32[]{:S(2)}, u32[]{:S(2)}) %collective-permute-start.32) | collective-permute-done | bytes 1048608 | tf_op jit(solution)/shard_map/ppermute | solution.py:40
  402.0 3.9 convert_reduce_fusion.6
  436.3 5.5 collective-permute-start.36
  441.8 13.7 %collective-permute-done.36 = bf16[256,512]{1,0:T(8,128)(2,1)S(1)} collective-permute-done((bf16[256,512]{1,0:T(8,128)(2,1)S(1)}, bf16[256,512]{1,0:T(8,128)(2,1)S(1)}, u32[]{:S(2)}, u32[]{:S(2)}) %collective-permute-start.36) | collective-permute-done | bytes 262176 | tf_op jit(solution)/shard_map/ppermute | solution.py:45
  456.2 8.8 collective-permute-start.38
  465.0 21.9 %collective-permute-done.37 = bf16[256,512]{1,0:T(8,128)(2,1)} collective-permute-done((bf16[256,512]{1,0:T(8,128)(2,1)}, bf16[256,512]{1,0:T(8,128)(2,1)}, u32[]{:S(2)}, u32[]{:S(2)}) %collective-permute-start.37) | collective-permute-done | bytes 262176 | tf_op jit(solution)/shard_map/ppermute | solution.py:45
  505.2 28.3 %attend_back.1 = bf16[8,128,1536]{2,1,0:T(8,128)(2,1)S(1)} custom-call(s32[8]{0:T(128)S(1)} %copy-done.68, f32[8]{0:T(128)S(1)} %copy-done.66, bf16[8,128,1536]{2,1,0:T(8,128)(2,1)} %bitcast.256, bf16[8,128,512]{2,1,0:T(8,128)(2,1)S(1)} %bitcast.253), custom_call_target="tpu_custom_call" | custom-call | flops 32212254720 | bytes 1 | tf_op jit(solution)/shard_map/attend_back/pallas_call | solution.py:245
  546.3 5.5 collective-permute-start.45
  552.0 11.1 %fusion.78 = (bf16[2048]{0:T(1024)(128)(2,1)S(1)}, bf16[2048]{0:T(1024)(128)(2,1)S(1)}, bf16[1024,2048]{1,0:T(8,128)(2,1)}) fusion(f32[1024]{0:T(1024)S(1)} %copy-done.108, f32[1024]{0:T(1024)S(1)} %copy-done.103, bf16[1024,2048]{1,0:T(8,128)(2,1)} %copy-done.3, bf16[1024,1536]{1,0:T(8,128)(2,1)S(1)} %get-tuple-element.156.refs_1_, ...), kind=kOutput, calls=%fused_computation.310 | convolution fusion | flops 6469709824 | bytes 17842176 | tf_op jit(solution)/shard_map/dot_general | solution.py:31
  568.5 20.5 %all-gather.6.cloned.1.call-done.refs_2_ = bf16[1024,512]{1,0:T(8,128)(2,1)} async-done(((bf16[256,512]{1,0:T(8,128)(2,1)}), bf16[1024,512]{1,0:T(8,128)(2,1)}) %all-gather.6.cloned.1.call-update) | async-done | bytes 1048592 | tf_op jit(solution)/shard_map/all_gather | solution.py:504
  594.8 9.8 %fusion.75 = f32[2048,1536]{0,1:T(8,128)S(1)} fusion(bf16[1024,1536]{1,0:T(8,128)(2,1)S(1)} %get-tuple-element.159, bf16[1024,2048]{1,0:T(8,128)(2,1)} %copy-done.3, f32[2048]{0:T(1024)S(1)} %bitcast.314, f32[2048]{0:T(1024)S(1)} %bitcast.298, f32[1024]{0:T(1024)S(1)} %copy-done.108, f32[1024]{0:T(1024)S(1)} %copy-done.103), kind=kOutput, calls=%fused_computation.309 | convolution fusion | flops 6455033856 | bytes 19947520 | tf_op jit(solution)/shard_map/dot_general | solution.py:27
  604.6 4.6 copy-done.76
  612.2 6.4 fusion.95
  618.7 6.1 add_convert_fusion
  631.7 4.7 slice_add_fusion
  642.6 4.5 broadcast_in_dim.109
  649.9 7.4 collective-permute-done.48
  657.3 17.2 %collective-permute-done.50 = bf16[512,768]{0,1:T(8,128)(2,1)S(1)} collective-permute-done((bf16[512,768]{0,1:T(8,128)(2,1)S(1)}, bf16[512,768]{0,1:T(8,128)(2,1)S(1)}, u32[]{:S(2)}, u32[]{:S(2)}) %collective-permute-start.50) | collective-permute-done | bytes 786464 | tf_op jit(solution)/shard_map/ppermute | solution.py:40
  677.9 20.2 %collective-permute-done.52.refs_3_ = bf16[4,256,512]{2,1,0:T(8,128)(2,1)} collective-permute-done((bf16[4,256,512]{2,1,0:T(8,128)(2,1)}, bf16[4,256,512]{2,1,0:T(8,128)(2,1)}, u32[]{:S(2)}, u32[]{:S(2)}) %collective-permute-start.52) | collective-permute-done | bytes 1048608 | tf_op jit(solution)/shard_map/ppermute | solution.py:51
  726.4 9.7 %collective-permute-done.53 = bf16[256,2048]{1,0:T(8,128)(2,1)} collective-permute-done((bf16[256,2048]{1,0:T(8,128)(2,1)}, bf16[256,2048]{1,0:T(8,128)(2,1)}, u32[]{:S(2)}, u32[]{:S(2)}) %collective-permute-start.53) | collective-permute-done | bytes 1048608 | tf_op jit(solution)/shard_map/ppermute | solution.py:40
  736.1 22.1 %collective-permute-done.54 = bf16[256,2048]{1,0:T(8,128)(2,1)} collective-permute-done((bf16[256,2048]{1,0:T(8,128)(2,1)}, bf16[256,2048]{1,0:T(8,128)(2,1)}, u32[]{:S(2)}, u32[]{:S(2)}) %collective-permute-start.54) | collective-permute-done | bytes 1048608 | tf_op jit(solution)/shard_map/ppermute | solution.py:40
  758.2 4.3 add_convert_fusion.5
  762.6 36.6 %collective-permute-done.63 = bf16[4,256,512]{2,1,0:T(8,128)(2,1)} collective-permute-done((bf16[4,256,512]{2,1,0:T(8,128)(2,1)}, bf16[4,256,512]{2,1,0:T(8,128)(2,1)}, u32[]{:S(2)}, u32[]{:S(2)}) %collective-permute-start.63) | collective-permute-done | bytes 1048608 | tf_op jit(solution)/shard_map/ppermute | solution.py:51
  812.1 8.5 copy.224
  833.2 35.1 %all-gather.10.cloned.1.call-done = bf16[1536,1024]{1,0:T(8,128)(2,1)} async-done(((bf16[1536,256]{1,0:T(8,128)(2,1)}), bf16[1536,1024]{1,0:T(8,128)(2,1)}) %all-gather.10.cloned.1.call-update) | async-done | bytes 3145744 | tf_op jit(solution)/shard_map/all_gather | solution.py:571
  868.3 5.5 convert.42
  (618 shorter events, 312.9 us)
Async XLA Ops:
  7.2 86.7 %all-gather.12.cloned.1.call-start = ((), (), s32[]{:S(2)}) async-start(), calls=%async_computation.11 | async-start | bytes 5242880 | tf_op jit(solution)/shard_map/all_gather | solution.py:346
  10.3 385.9 %reduce-scatter.5.cloned.1.call-start = ((), (), s32[]{:S(2)}) async-start(), calls=%async_computation.4 | async-start | bytes 5242880 | tf_op jit(solution)/shard_map/reduce_scatter | solution.py:454
  22.4 95.2 %collective-permute-start.7 = (bf16[1024,512]{1,0:T(8,128)(2,1)}, bf16[1024,512]{1,0:T(8,128)(2,1)}, u32[]{:S(2)}, u32[]{:S(2)}) collective-permute-start(bf16[1024,512]{1,0:T(8,128)(2,1)} %param.23), channel_id=1, source_target_pairs={{0,16},{8,24},{16,0},{24,8},{1,17},{9,25},{17,1},{25,9},{2,18},{10... | collective-permute-start | bytes 3145736 | tf_op jit(solution)/shard_map/ppermute | solution.py:40
  22.9 94.7 %collective-permute-start.6 = (bf16[1024,512]{1,0:T(8,128)(2,1)}, bf16[1024,512]{1,0:T(8,128)(2,1)}, u32[]{:S(2)}, u32[]{:S(2)}) collective-permute-start(bf16[1024,512]{1,0:T(8,128)(2,1)} %param.23), channel_id=1, source_target_pairs={{0,8},{8,0},{16,24},{24,16},{1,9},{9,1},{17,25},{25,17},{2,10},{10... | collective-permute-start | bytes 3145736 | tf_op jit(solution)/shard_map/ppermute | solution.py:40
  73.6 31.8 %collective-permute-start.4 = (bf16[2048,768]{1,0:T(8,128)(2,1)}, bf16[2048,768]{1,0:T(8,128)(2,1)}, u32[]{:S(2)}, u32[]{:S(2)}) collective-permute-start(bf16[2048,768]{1,0:T(8,128)(2,1)} %fusion.50), channel_id=1, source_target_pairs={{0,1},{1,0},{2,3},{3,2},{4,5},{5,4},{6,7},{7,6},{8,9},{9,8},{10,11... | collective-permute-start | bytes 9437192 | tf_op jit(solution)/shard_map/ppermute | solution.py:35
  82.8 56.4 %collective-permute-start.10 = (bf16[512,1024]{1,0:T(8,128)(2,1)}, bf16[512,1024]{1,0:T(8,128)(2,1)}, u32[]{:S(2)}, u32[]{:S(2)}) collective-permute-start(bf16[512,1024]{1,0:T(8,128)(2,1)} %get-tuple-element.104), channel_id=1, source_target_pairs={{0,8},{8,0},{16,24},{24,16},{1,9},{9,1},{17,25},{25,17},{2,10},{10... | collective-permute-start | bytes 3145736 | tf_op jit(solution)/shard_map/ppermute | solution.py:40
  86.6 52.7 %collective-permute-start.11 = (bf16[512,1024]{1,0:T(8,128)(2,1)}, bf16[512,1024]{1,0:T(8,128)(2,1)}, u32[]{:S(2)}, u32[]{:S(2)}) collective-permute-start(bf16[512,1024]{1,0:T(8,128)(2,1)} %get-tuple-element.105), channel_id=1, source_target_pairs={{0,16},{8,24},{16,0},{24,8},{1,17},{9,25},{17,1},{25,9},{2,18},{10... | collective-permute-start | bytes 3145736 | tf_op jit(solution)/shard_map/ppermute | solution.py:40
  105.4 33.8 %collective-permute-start.12 = (bf16[512,1024]{1,0:T(8,128)(2,1)S(1)}, bf16[512,1024]{1,0:T(8,128)(2,1)S(1)}, u32[]{:S(2)}, u32[]{:S(2)}) collective-permute-start(bf16[512,1024]{1,0:T(8,128)(2,1)S(1)} %copy-done.52), channel_id=1, source_target_pairs={{0,24},{8,16},{16,8},{24,0},{1,25},{9,17},{17,9},{25,1},{2,26},{10... | collective-permute-start | bytes 3145736 | tf_op jit(solution)/shard_map/ppermute | solution.py:40
  155.1 35.2 %collective-permute-start.13 = (bf16[1024,2048]{1,0:T(8,128)(2,1)}, bf16[1024,2048]{1,0:T(8,128)(2,1)}, u32[]{:S(2)}, u32[]{:S(2)}) collective-permute-start(bf16[1024,2048]{1,0:T(8,128)(2,1)} %maximum_dynamic-update-slice_fusion), channel_id=1, source_target_pairs={{0,1},{1,0},{2,3},{3,2},{4,5},{5,4},{6,7},{7,6},{8,9},{9,8},{10,11... | collective-permute-start | bytes 12582920 | tf_op jit(solution)/shard_map/ppermute | solution.py:35
  155.3 33.6 %collective-permute-start.18 = (bf16[256,2048]{1,0:T(8,128)(2,1)}, bf16[256,2048]{1,0:T(8,128)(2,1)S(1)}, u32[]{:S(2)}, u32[]{:S(2)}) collective-permute-start(bf16[256,2048]{1,0:T(8,128)(2,1)} %get-tuple-element.112), channel_id=1, source_target_pairs={{0,16},{8,24},{16,0},{24,8},{1,17},{9,25},{17,1},{25,9},{2,18},{10... | collective-permute-start | bytes 3145736 | tf_op jit(solution)/shard_map/ppermute | solution.py:40
  155.9 34.5 %collective-permute-start.17 = (bf16[256,2048]{1,0:T(8,128)(2,1)}, bf16[256,2048]{1,0:T(8,128)(2,1)S(1)}, u32[]{:S(2)}, u32[]{:S(2)}) collective-permute-start(bf16[256,2048]{1,0:T(8,128)(2,1)} %get-tuple-element.112), channel_id=1, source_target_pairs={{0,8},{8,0},{16,24},{24,16},{1,9},{9,1},{17,25},{25,17},{2,10},{10... | collective-permute-start | bytes 3145736 | tf_op jit(solution)/shard_map/ppermute | solution.py:40
  177.7 83.6 %collective-permute-start.28 = (bf16[2048,1024]{1,0:T(8,128)(2,1)}, bf16[2048,1024]{1,0:T(8,128)(2,1)}, u32[]{:S(2)}, u32[]{:S(2)}) collective-permute-start(bf16[2048,1024]{1,0:T(8,128)(2,1)} %constant_dynamic-update-slice_fusion.17), channel_id=1, source_target_pairs={{0,1},{1,0},{2,3},{3,2},{4,5},{5,4},{6,7},{7,6},{8,9},{9,8},{10,11... | collective-permute-start | bytes 12582920 | tf_op jit(solution)/shard_map/ppermute | solution.py:35
  187.3 26.4 %collective-permute-start.21 = (bf16[1024,512]{1,0:T(8,128)(2,1)}, bf16[1024,512]{1,0:T(8,128)(2,1)}, u32[]{:S(2)}, u32[]{:S(2)}) collective-permute-start(bf16[1024,512]{1,0:T(8,128)(2,1)} %get-tuple-element.125.refs_3_), channel_id=1, source_target_pairs={{0,8},{8,0},{16,24},{24,16},{1,9},{9,1},{17,25},{25,17},{2,10},{10... | collective-permute-start | bytes 3145736 | tf_op jit(solution)/shard_map/ppermute | solution.py:40
  188.8 26.4 %collective-permute-start.22 = (bf16[1024,512]{1,0:T(8,128)(2,1)}, bf16[1024,512]{1,0:T(8,128)(2,1)}, u32[]{:S(2)}, u32[]{:S(2)}) collective-permute-start(bf16[1024,512]{1,0:T(8,128)(2,1)} %get-tuple-element.126.refs_4_), channel_id=1, source_target_pairs={{0,16},{8,24},{16,0},{24,8},{1,17},{9,25},{17,1},{25,9},{2,18},{10... | collective-permute-start | bytes 3145736 | tf_op jit(solution)/shard_map/ppermute | solution.py:40
  196.3 26.4 %collective-permute-start.19 = (bf16[128,2048]{1,0:T(8,128)(2,1)S(1)}, bf16[128,2048]{1,0:T(8,128)(2,1)S(1)}, u32[]{:S(2)}, u32[]{:S(2)}) collective-permute-start(bf16[128,2048]{1,0:T(8,128)(2,1)S(1)} %slice.424), channel_id=1, source_target_pairs={{0,8},{8,0},{16,24},{24,16},{1,9},{9,1},{17,25},{25,17},{2,10},{10... | collective-permute-start | bytes 1572872 | tf_op jit(solution)/shard_map/ppermute | solution.py:40
  196.9 27.1 %collective-permute-start.20 = (bf16[128,2048]{1,0:T(8,128)(2,1)S(1)}, bf16[128,2048]{1,0:T(8,128)(2,1)S(1)}, u32[]{:S(2)}, u32[]{:S(2)}) collective-permute-start(bf16[128,2048]{1,0:T(8,128)(2,1)S(1)} %slice.425), channel_id=1, source_target_pairs={{0,16},{8,24},{16,0},{24,8},{1,17},{9,25},{17,1},{25,9},{2,18},{10... | collective-permute-start | bytes 1572872 | tf_op jit(solution)/shard_map/ppermute | solution.py:40
  279.1 26.5 %collective-permute-start.25 = (bf16[1024,512]{1,0:T(8,128)(2,1)S(1)}, bf16[1024,512]{1,0:T(8,128)(2,1)S(1)}, u32[]{:S(2)}, u32[]{:S(2)}) collective-permute-start(bf16[1024,512]{1,0:T(8,128)(2,1)S(1)} %get-tuple-element.128), channel_id=1, source_target_pairs={{0,24},{8,16},{16,8},{24,0},{1,25},{9,17},{17,9},{25,1},{2,26},{10... | collective-permute-start | bytes 3145736 | tf_op jit(solution)/shard_map/ppermute | solution.py:40
  306.7 187.0 %reduce-scatter.7.cloned.1.call-start = ((), (), s32[]{:S(2)}) async-start(), calls=%async_computation.5 | async-start | bytes 5242880 | tf_op jit(solution)/shard_map/reduce_scatter | solution.py:462
  347.1 27.6 %collective-permute-start.34 = (bf16[2048,1024]{1,0:T(8,128)(2,1)S(1)}, bf16[2048,1024]{1,0:T(8,128)(2,1)S(1)}, u32[]{:S(2)}, u32[]{:S(2)}) collective-permute-start(bf16[2048,1024]{1,0:T(8,128)(2,1)S(1)} %convolution_convert_fusion.1), channel_id=1, source_target_pairs={{0,1},{1,0},{2,3},{3,2},{4,5},{5,4},{6,7},{7,6},{8,9},{9,8},{10,11... | collective-permute-start | bytes 12582920 | tf_op jit(solution)/shard_map/ppermute | solution.py:35
  347.7 26.0 %collective-permute-start.31 = (bf16[256,2048]{1,0:T(8,128)(2,1)S(1)}, bf16[256,2048]{1,0:T(8,128)(2,1)S(1)}, u32[]{:S(2)}, u32[]{:S(2)}) collective-permute-start(bf16[256,2048]{1,0:T(8,128)(2,1)S(1)} %get-tuple-element.136), channel_id=1, source_target_pairs={{0,8},{8,0},{16,24},{24,16},{1,9},{9,1},{17,25},{25,17},{2,10},{10... | collective-permute-start | bytes 3145736 | tf_op jit(solution)/shard_map/ppermute | solution.py:40
  348.7 47.5 %collective-permute-start.32 = (bf16[256,2048]{1,0:T(8,128)(2,1)}, bf16[256,2048]{1,0:T(8,128)(2,1)S(1)}, u32[]{:S(2)}, u32[]{:S(2)}) collective-permute-start(bf16[256,2048]{1,0:T(8,128)(2,1)} %get-tuple-element.137), channel_id=1, source_target_pairs={{0,16},{8,24},{16,0},{24,8},{1,17},{9,25},{17,1},{25,9},{2,18},{10... | collective-permute-start | bytes 3145736 | tf_op jit(solution)/shard_map/ppermute | solution.py:40
  349.3 46.9 %collective-permute-start.33 = (bf16[256,2048]{1,0:T(8,128)(2,1)}, bf16[256,2048]{1,0:T(8,128)(2,1)S(1)}, u32[]{:S(2)}, u32[]{:S(2)}) collective-permute-start(bf16[256,2048]{1,0:T(8,128)(2,1)} %get-tuple-element.138), channel_id=1, source_target_pairs={{0,24},{8,16},{16,8},{24,0},{1,25},{9,17},{17,9},{25,1},{2,26},{10... | collective-permute-start | bytes 3145736 | tf_op jit(solution)/shard_map/ppermute | solution.py:40
  382.2 153.2 %reduce-scatter.9.cloned.1.call-start = ((), (), s32[]{:S(2)}) async-start(), calls=%async_computation.6 | async-start | bytes 1310720 | tf_op jit(solution)/shard_map/reduce_scatter | solution.py:492
  432.8 57.4 %collective-permute-start.39 = (bf16[1024,512]{1,0:T(8,128)(2,1)S(1)}, bf16[1024,512]{1,0:T(8,128)(2,1)}, u32[]{:S(2)}, u32[]{:S(2)}) collective-permute-start(bf16[1024,512]{1,0:T(8,128)(2,1)S(1)} %get-tuple-element.149), channel_id=1, source_target_pairs={{0,8},{8,0},{16,24},{24,16},{1,9},{9,1},{17,25},{25,17},{2,10},{10... | collective-permute-start | bytes 3145736 | tf_op jit(solution)/shard_map/ppermute | solution.py:40
  433.9 56.4 %collective-permute-start.40 = (bf16[1024,512]{1,0:T(8,128)(2,1)}, bf16[1024,512]{1,0:T(8,128)(2,1)}, u32[]{:S(2)}, u32[]{:S(2)}) collective-permute-start(bf16[1024,512]{1,0:T(8,128)(2,1)} %get-tuple-element.150), channel_id=1, source_target_pairs={{0,16},{8,24},{16,0},{24,8},{1,17},{9,25},{17,1},{25,9},{2,18},{10... | collective-permute-start | bytes 3145736 | tf_op jit(solution)/shard_map/ppermute | solution.py:40
  434.7 55.6 %collective-permute-start.41 = (bf16[1024,512]{1,0:T(8,128)(2,1)}, bf16[1024,512]{1,0:T(8,128)(2,1)}, u32[]{:S(2)}, u32[]{:S(2)}) collective-permute-start(bf16[1024,512]{1,0:T(8,128)(2,1)} %get-tuple-element.151), channel_id=1, source_target_pairs={{0,24},{8,16},{16,8},{24,0},{1,25},{9,17},{17,9},{25,1},{2,26},{10... | collective-permute-start | bytes 3145736 | tf_op jit(solution)/shard_map/ppermute | solution.py:40
  441.8 45.1 %collective-permute-start.37 = (bf16[256,512]{1,0:T(8,128)(2,1)}, bf16[256,512]{1,0:T(8,128)(2,1)}, u32[]{:S(2)}, u32[]{:S(2)}) collective-permute-start(bf16[256,512]{1,0:T(8,128)(2,1)} %get-tuple-element.145), channel_id=1, source_target_pairs={{0,4},{2,6},{4,0},{6,2},{1,5},{3,7},{5,1},{7,3},{8,12},{10,14},{12... | collective-permute-start | bytes 786440 | tf_op jit(solution)/shard_map/ppermute | solution.py:45
  456.2 30.7 %collective-permute-start.38 = (bf16[256,512]{1,0:T(8,128)(2,1)}, bf16[256,512]{1,0:T(8,128)(2,1)}, u32[]{:S(2)}, u32[]{:S(2)}) collective-permute-start(bf16[256,512]{1,0:T(8,128)(2,1)} %get-tuple-element.146), channel_id=1, source_target_pairs={{0,2},{2,4},{4,6},{6,0},{1,3},{3,5},{5,7},{7,1},{8,10},{10,12},{12... | collective-permute-start | bytes 786440 | tf_op jit(solution)/shard_map/ppermute | solution.py:45
  498.4 90.6 %all-gather.6.cloned.1.call-start = ((), (), s32[]{:S(2)}) async-start(), calls=%async_computation.7 | async-start | bytes 1310720 | tf_op jit(solution)/shard_map/all_gather | solution.py:504
  500.2 33.4 %collective-permute-start.42 = (bf16[512,512]{1,0:T(8,128)(2,1)S(1)}, bf16[512,512]{1,0:T(8,128)(2,1)S(1)}, u32[]{:S(2)}, u32[]{:S(2)}) collective-permute-start(bf16[512,512]{1,0:T(8,128)(2,1)S(1)} %pad_maximum_fusion.7), channel_id=1, source_target_pairs={{0,8},{8,0},{16,24},{24,16},{1,9},{9,1},{17,25},{25,17},{2,10},{10... | collective-permute-start | bytes 1572872 | tf_op jit(solution)/shard_map/ppermute | solution.py:40
  501.3 32.2 %collective-permute-start.43 = (bf16[512,512]{1,0:T(8,128)(2,1)S(1)}, bf16[512,512]{1,0:T(8,128)(2,1)S(1)}, u32[]{:S(2)}, u32[]{:S(2)}) collective-permute-start(bf16[512,512]{1,0:T(8,128)(2,1)S(1)} %pad_maximum_fusion.8), channel_id=1, source_target_pairs={{0,16},{8,24},{16,0},{24,8},{1,17},{9,25},{17,1},{25,9},{2,18},{10... | collective-permute-start | bytes 1572872 | tf_op jit(solution)/shard_map/ppermute | solution.py:40
  502.9 30.7 %collective-permute-start.44 = (bf16[512,512]{1,0:T(8,128)(2,1)S(1)}, bf16[512,512]{1,0:T(8,128)(2,1)S(1)}, u32[]{:S(2)}, u32[]{:S(2)}) collective-permute-start(bf16[512,512]{1,0:T(8,128)(2,1)S(1)} %pad_maximum_fusion.9), channel_id=1, source_target_pairs={{0,24},{8,16},{16,8},{24,0},{1,25},{9,17},{17,9},{25,1},{2,26},{10... | collective-permute-start | bytes 1572872 | tf_op jit(solution)/shard_map/ppermute | solution.py:40
  545.0 44.7 %collective-permute-start.46 = (bf16[4,256,512]{2,1,0:T(8,128)(2,1)}, bf16[4,256,512]{2,1,0:T(8,128)(2,1)}, u32[]{:S(2)}, u32[]{:S(2)}) collective-permute-start(bf16[4,256,512]{2,1,0:T(8,128)(2,1)} %fusion.53), channel_id=1, source_target_pairs={{2,0},{4,2},{6,4},{3,1},{5,3},{7,5},{10,8},{12,10},{14,12},{11,9},... | collective-permute-start | bytes 3145736 | tf_op jit(solution)/shard_map/ppermute | solution.py:51
  546.3 43.4 %collective-permute-start.45 = (bf16[4,256,512]{2,1,0:T(8,128)(2,1)}, bf16[4,256,512]{2,1,0:T(8,128)(2,1)}, u32[]{:S(2)}, u32[]{:S(2)}) collective-permute-start(bf16[4,256,512]{2,1,0:T(8,128)(2,1)} %fusion.53), channel_id=1, source_target_pairs={{0,2},{2,4},{4,6},{1,3},{3,5},{5,7},{8,10},{10,12},{12,14},{9,11},... | collective-permute-start | bytes 3145736 | tf_op jit(solution)/shard_map/ppermute | solution.py:50
  551.9 146.3 %reduce-scatter.11.cloned.1.call-start = ((), (), s32[]{:S(2)}) async-start(), calls=%async_computation.8 | async-start | bytes 5570560 | tf_op jit(solution)/shard_map/reduce_scatter | solution.py:538
  594.1 206.4 %all-gather.8.cloned.1.call-start = ((), (), s32[]{:S(2)}) async-start(), calls=%async_computation.9 | async-start | bytes 5242880 | tf_op jit(solution)/shard_map/all_gather | solution.py:541
  626.7 51.2 %collective-permute-start.51 = (bf16[4,256,512]{2,1,0:T(8,128)(2,1)}, bf16[4,256,512]{2,1,0:T(8,128)(2,1)}, u32[]{:S(2)}, u32[]{:S(2)}) collective-permute-start(bf16[4,256,512]{2,1,0:T(8,128)(2,1)} %get-tuple-element.160), channel_id=1, source_target_pairs={{2,4},{4,6},{3,5},{5,7},{10,12},{12,14},{11,13},{13,15},{18,20},{2... | collective-permute-start | bytes 3145736 | tf_op jit(solution)/shard_map/ppermute | solution.py:50
  628.3 69.8 %collective-permute-start.52 = (bf16[4,256,512]{2,1,0:T(8,128)(2,1)}, bf16[4,256,512]{2,1,0:T(8,128)(2,1)}, u32[]{:S(2)}, u32[]{:S(2)}) collective-permute-start(bf16[4,256,512]{2,1,0:T(8,128)(2,1)} %get-tuple-element.161), channel_id=1, source_target_pairs={{2,0},{4,2},{3,1},{5,3},{10,8},{12,10},{11,9},{13,11},{18,16},{20,... | collective-permute-start | bytes 3145736 | tf_op jit(solution)/shard_map/ppermute | solution.py:51
  631.4 236.9 %all-gather.10.cloned.1.call-start = ((), (), s32[]{:S(2)}) async-start(), calls=%async_computation.10 | async-start | bytes 3932160 | tf_op jit(solution)/shard_map/all_gather | solution.py:571
  638.6 35.9 %collective-permute-start.50 = (bf16[512,768]{0,1:T(8,128)(2,1)S(1)}, bf16[512,768]{0,1:T(8,128)(2,1)S(1)}, u32[]{:S(2)}, u32[]{:S(2)}) collective-permute-start(bf16[512,768]{0,1:T(8,128)(2,1)S(1)} %get-tuple-element.194), channel_id=1, source_target_pairs={{0,24},{8,16},{16,8},{24,0},{1,25},{9,17},{17,9},{25,1},{2,26},{10... | collective-permute-start | bytes 2359304 | tf_op jit(solution)/shard_map/ppermute | solution.py:40
  640.0 35.9 %collective-permute-start.49 = (bf16[512,768]{0,1:T(8,128)(2,1)S(1)}, bf16[512,768]{0,1:T(8,128)(2,1)S(1)}, u32[]{:S(2)}, u32[]{:S(2)}) collective-permute-start(bf16[512,768]{0,1:T(8,128)(2,1)S(1)} %get-tuple-element.195), channel_id=1, source_target_pairs={{0,16},{8,24},{16,0},{24,8},{1,17},{9,25},{17,1},{25,9},{2,18},{10... | collective-permute-start | bytes 2359304 | tf_op jit(solution)/shard_map/ppermute | solution.py:40
  709.7 26.4 %collective-permute-start.53 = (bf16[256,2048]{1,0:T(8,128)(2,1)}, bf16[256,2048]{1,0:T(8,128)(2,1)}, u32[]{:S(2)}, u32[]{:S(2)}) collective-permute-start(bf16[256,2048]{1,0:T(8,128)(2,1)} %copy-done.63), channel_id=1, source_target_pairs={{0,8},{8,0},{16,24},{24,16},{1,9},{9,1},{17,25},{25,17},{2,10},{10... | collective-permute-start | bytes 3145736 | tf_op jit(solution)/shard_map/ppermute | solution.py:40
  711.2 47.0 %collective-permute-start.54 = (bf16[256,2048]{1,0:T(8,128)(2,1)}, bf16[256,2048]{1,0:T(8,128)(2,1)}, u32[]{:S(2)}, u32[]{:S(2)}) collective-permute-start(bf16[256,2048]{1,0:T(8,128)(2,1)} %copy-done.61), channel_id=1, source_target_pairs={{0,16},{8,24},{16,0},{24,8},{1,17},{9,25},{17,1},{25,9},{2,18},{10... | collective-permute-start | bytes 3145736 | tf_op jit(solution)/shard_map/ppermute | solution.py:40
  718.3 39.9 %collective-permute-start.55 = (bf16[256,2048]{1,0:T(8,128)(2,1)}, bf16[256,2048]{1,0:T(8,128)(2,1)}, u32[]{:S(2)}, u32[]{:S(2)}) collective-permute-start(bf16[256,2048]{1,0:T(8,128)(2,1)} %get-tuple-element.165), channel_id=1, source_target_pairs={{0,24},{8,16},{16,8},{24,0},{1,25},{9,17},{17,9},{25,1},{2,26},{10... | collective-permute-start | bytes 3145736 | tf_op jit(solution)/shard_map/ppermute | solution.py:40
  718.9 43.6 %collective-permute-start.62 = (bf16[4,256,512]{2,1,0:T(8,128)(2,1)}, bf16[4,256,512]{2,1,0:T(8,128)(2,1)}, u32[]{:S(2)}, u32[]{:S(2)}) collective-permute-start(bf16[4,256,512]{2,1,0:T(8,128)(2,1)} %get-tuple-element.168), channel_id=1, source_target_pairs={{4,6},{5,7},{12,14},{13,15},{20,22},{21,23},{28,30},{29,31}} | collective-permute-start | bytes 3145736 | tf_op jit(solution)/shard_map/ppermute | solution.py:50
  721.9 77.2 %collective-permute-start.63 = (bf16[4,256,512]{2,1,0:T(8,128)(2,1)}, bf16[4,256,512]{2,1,0:T(8,128)(2,1)}, u32[]{:S(2)}, u32[]{:S(2)}) collective-permute-start(bf16[4,256,512]{2,1,0:T(8,128)(2,1)} %get-tuple-element.169), channel_id=1, source_target_pairs={{2,0},{3,1},{10,8},{11,9},{18,16},{19,17},{26,24},{27,25}} | collective-permute-start | bytes 3145736 | tf_op jit(solution)/shard_map/ppermute | solution.py:51
  736.1 86.8 %collective-permute-start.57 = (bf16[256,2048]{1,0:T(8,128)(2,1)}, bf16[256,2048]{1,0:T(8,128)(2,1)}, u32[]{:S(2)}, u32[]{:S(2)}) collective-permute-start(bf16[256,2048]{1,0:T(8,128)(2,1)} %fusion.32), channel_id=1, source_target_pairs={{0,1},{1,0},{2,3},{3,2},{4,5},{5,4},{6,7},{7,6},{8,9},{9,8},{10,11... | collective-permute-start | bytes 3145736 | tf_op jit(solution)/shard_map/ppermute | solution.py:35
  762.6 67.5 %collective-permute-start.56 = (bf16[256,2048]{1,0:T(8,128)(2,1)}, bf16[256,2048]{1,0:T(8,128)(2,1)}, u32[]{:S(2)}, u32[]{:S(2)}) collective-permute-start(bf16[256,2048]{1,0:T(8,128)(2,1)} %add_convert_fusion.5), channel_id=1, source_target_pairs={{0,1},{1,0},{2,3},{3,2},{4,5},{5,4},{6,7},{7,6},{8,9},{9,8},{10,11... | collective-permute-start | bytes 3145736 | tf_op jit(solution)/shard_map/ppermute | solution.py:35
  (145 other events, 1594.1 us)
Sparse Core Ops, SparseCore 0:
  10.4 83.4 all-gather.11
  306.8 78.4 reduce-scatter.4
  388.3 93.7 reduce-scatter.6
  498.5 26.2 reduce-scatter.8
  552.0 36.9 all-gather.5
  594.2 101.6 reduce-scatter.10
  697.5 102.9 all-gather.7
  804.8 63.4 all-gather.9

commit v6 on v4

--- a/solution.py
+++ b/solution.py
@@ -345,11 +345,10 @@
 
     tree = lax.all_gather(mine, "context", axis=0, tiled=True)
     head_first = gather_first(chosen)
-    rest = gate([*head_first, *up_pieces[1:]])
-    head_first, up_pieces[1:] = rest[: len(head_first)], rest[len(head_first) :]
+    up_pieces[1:] = gate(up_pieces[1:], *head_first)
     head_second = gather_second(head_first)
     up_blocks = up_pieces[:1] + send_blocks(up_pieces[1:])
-    tree, mine_cot, *down_pieces = gate([tree, mine_cot, *down_pieces], *head_second)
+    (mine_cot,) = gate([mine_cot], tree, *head_second)
     head_blocks = gather_blocks(chosen, head_first, head_second)
     heads_own = place([block[:part] for block in head_blocks], 0)
     w_heads = jnp.concatenate([heads_own, swap_cores(heads_own)], axis=1)
@@ -393,9 +392,8 @@
     out_second = gather_second(out_first)
     mixed = attend(order, slopes, qkv)
     mixed, mine_cot, *rest = gate(
-        [mixed, mine_cot, *down_pieces, *out_first, *out_second, *up_blocks]
-    )
-    down_pieces, rest = rest[:groups], rest[groups:]
+        [mixed, mine_cot, *out_first, *out_second, *up_blocks]
+    )
     out_first, rest = rest[: len(out_first)], rest[len(out_first) :]
     out_second, up_blocks = rest[: len(out_second)], rest[len(out_second) :]
     out_own = place(gather_blocks(mine_out, out_first, out_second), 1)
@@ -458,7 +456,7 @@
     grad_up = (dot_tn(all_two, back_own) + grad_up.astype(F32)).astype(BF16)
     grad_up = grad_up.reshape(groups, planes, part // planes, hidden).transpose(1, 0, 2, 3)
     grad_up = grad_up.reshape(width, hidden)
-    grad_down, *grad_two = gate([grad_down, *grad_two], grad_up)
+    grad_down, own_two = gate([grad_down, own_two], grad_up, *grad_two)
     grad_up = lax.psum_scatter(grad_up, "context", scatter_dimension=0, tiled=True)
 
     grad_two = add_up(own_two, grad_two)

time: 873 us -> 875 us (level)
  local copies, waits for them, and re-layouts: 174 us -> 157 us
  waiting for transfers between devices: 348 us -> 364 us
    ppermute x40, waiting for transfers between devices: 196 us -> 213 us  [xor_send(): return lax.ppermute(value, 'fsdp', [(i, i ^ step) for i in range(size)])]
    unnamed x264 -> x230, local copies, waits for them, and re-layouts: 83 us -> 70.5 us
  transfers between devices with their start and end apart: 72 -> 72, of which waited for: 32 -> 31; matrix products, arithmetic and copies ran while one was open for 33% -> 33% of each run, Pallas kernels for 5% -> 5%
where the time goes in v6:
time: 875 us; the launch traced here: 869 us
  waiting for transfers between devices  364 us (42%)
  local copies, waits for them, and re-layouts  157 us (18%)
  matrix products  134 us (15%)
  starting transfers between devices  78.8 us (9%)
  other arithmetic  71.1 us (8%)
  Pallas kernels  46.2 us (5%)
  between operations  17.2 us (2%)
    ppermute x40, waiting for transfers between devices, xor_send(): return lax.ppermute(value, 'fsdp', [(i, i ^ step) for i in range(size)])  213 us
    unnamed x230, local copies, waits for them, and re-layouts  70.5 us
    dot_general x7, matrix products, dot_nn(): lax.dot_general(left, right, (((1,), (0,)), ((), ())), preferred_element_...  49.5 us
    ppermute x6, waiting for transfers between devices, ring_send(): lax.ppermute(value, 'context', [(i, (i + step) % size) for i in range(siz...  48.9 us
    dot_general x7, matrix products, dot_nt(): lax.dot_general(left, right, (((1,), (1,)), ((), ())), preferred_element_...  48.8 us
    ppermute x40, starting transfers between devices, xor_send(): return lax.ppermute(value, 'fsdp', [(i, i ^ step) for i in range(size)])  45 us
    ppermute x3, waiting for transfers between devices, line_step(): lax.ppermute(downward[-1], 'context', [(i + 1, i) for i in range(0, size...  43.7 us
    all_gather x1, waiting for transfers between devices, per_device(): g_heads = lax.all_gather(grad_heads, 'context', axis=1, tiled=True)  39.8 us
  transfers between devices with their start and end apart: 72, of which 31 were waited for; matrix products, arithmetic and copies ran while one was open for 33% of the time, Pallas kernels for 5%

profile of v6, /device:TPU:0, one launch (start us, length us, event | category | flops | bytes accessed | tf_op | source)
XLA Modules:
  0.0 868.7 jit_solution(11796904766847295976)
XLA Ops:
  26.4 14.2 %collective-permute-done.1 = bf16[544,768]{1,0:T(8,128)(2,1)S(1)} collective-permute-done((bf16[544,768]{1,0:T(8,128)(2,1)}, bf16[544,768]{1,0:T(8,128)(2,1)S(1)}, u32[]{:S(2)}, u32[]{:S(2)}) %collective-permute-start.1) | collective-permute-done | bytes 835616 | tf_op jit(solution)/shard_map/ppermute | solution.py:40
  46.2 26.4 %collective-permute-done.3 = bf16[272,768]{1,0:T(8,128)(2,1)S(1)} collective-permute-done((bf16[272,768]{1,0:T(8,128)(2,1)S(1)}, bf16[272,768]{1,0:T(8,128)(2,1)S(1)}, u32[]{:S(2)}, u32[]{:S(2)}) %collective-permute-start.3) | collective-permute-done | bytes 417824 | tf_op jit(solution)/shard_map/ppermute | solution.py:40
  87.6 6.4 all-gather.12.cloned.1.call-done
  101.2 9.6 %add_convert_fusion.4.refs_0_ = bf16[1024,1536]{1,0:T(8,128)(2,1)S(1)} fusion(bf16[2048,768]{1,0:T(8,128)(2,1)} %collective-permute-done.4, bf16[2048,768]{1,0:T(8,128)(2,1)} %fusion.50, f32[1536]{0:T(1024)S(1)} %add.508, f32[2048]{0:T(1024)S(1)} %bitcast.317, f32[2048]{0:T(1024)S(1)} %bitcast.301, f32[1024]{0:T(1024)S(1)} %add_rsqrt_fusion, ...), kind=kOutput, calls=%fused_computation.21 | convolution fusion | flops 6470762496 | bytes 13662208 | tf_op jit(solution)/shard_map/dot_general | solution.py:23
  115.3 17.9 %attend.1 = bf16[8,128,512]{2,1,0:T(8,128)(2,1)S(1)} custom-call(s32[8]{0:T(128)S(1)} %select_reduce_fusion.order, f32[8]{0:T(128)S(1)} %fusion.70.slopes, bf16[8,128,1536]{2,1,0:T(8,128)(2,1)S(1)} %bitcast.258), custom_call_target="tpu_custom_call" | custom-call | flops 17179869184 | bytes 1 | tf_op jit(solution)/shard_map/attend/pallas_call | solution.py:223
  135.7 6.7 collective-permute-done.8.refs_4_
  179.9 9.6 %collective-permute-done.15.refs_3_ = bf16[256,512]{1,0:T(8,128)(2,1)S(1)} collective-permute-done((bf16[256,512]{1,0:T(8,128)(2,1)S(1)}, bf16[256,512]{1,0:T(8,128)(2,1)S(1)}, u32[]{:S(2)}, u32[]{:S(2)}) %collective-permute-start.15) | collective-permute-done | bytes 262176 | tf_op jit(solution)/shard_map/ppermute | solution.py:45
  209.5 6.4 collective-permute-done.21
  217.4 8.7 collective-permute-done.20
  230.4 19.2 %collective-permute-done.24.refs_1_ = bf16[256,2048]{1,0:T(8,128)(2,1)S(1)} collective-permute-done((bf16[256,2048]{1,0:T(8,128)(2,1)S(1)}, bf16[256,2048]{1,0:T(8,128)(2,1)S(1)}, u32[]{:S(2)}, u32[]{:S(2)}) %collective-permute-start.24) | collective-permute-done | bytes 1048608 | tf_op jit(solution)/shard_map/ppermute | solution.py:40
  253.2 8.9 %collective-permute-done.25 = bf16[128,2048]{1,0:T(8,128)(2,1)S(1)} collective-permute-done((bf16[128,2048]{1,0:T(8,128)(2,1)S(1)}, bf16[128,2048]{1,0:T(8,128)(2,1)S(1)}, u32[]{:S(2)}, u32[]{:S(2)}) %collective-permute-start.25) | collective-permute-done | bytes 524320 | tf_op jit(solution)/shard_map/ppermute | solution.py:40
  262.2 10.0 %multiply_convert_fusion = (bf16[1024,1024]{1,0:T(8,128)(2,1)S(1)}, f32[1024,1024]{1,0:T(8,128)}) fusion(f32[1024]{0:T(1024)S(1)} %bitcast.323, bf16[1024,2048]{1,0:T(8,128)(2,1)S(1)} %constant_dynamic-update-slice_fusion, bf16[2048,1024]{1,0:T(8,128)(2,1)} %collective-permute-done.27), kind=kOutput, calls=%fused_computation.36 | convolution fusion | flops 4301258752 | bytes 14684160 | tf_op jit(solution)/shard_map/dot_general | solution.py:23
  273.5 4.8 convolution_convert_fusion.2
  282.3 6.6 fusion.90
  290.9 6.4 add_convert_fusion.3
  297.9 9.8 %collective-permute-done.29.refs_0_ = bf16[1024,512]{1,0:T(8,128)(2,1)S(1)} collective-permute-done((bf16[1024,512]{1,0:T(8,128)(2,1)S(1)}, bf16[1024,512]{1,0:T(8,128)(2,1)S(1)}, u32[]{:S(2)}, u32[]{:S(2)}) %collective-permute-start.29) | collective-permute-done | bytes 1048608 | tf_op jit(solution)/shard_map/ppermute | solution.py:40
  311.1 10.6 %convert_reduce_fusion.3 = (bf16[1024]{0:T(1024)(128)(2,1)S(1)}, bf16[1024,1024]{1,0:T(8,128)(2,1)S(1)}) fusion(f32[1024,1024]{1,0:T(8,128)} %copy-done.93, f32[1024]{0:T(1024)S(1)} %bitcast.321, bf16[1024,2048]{1,0:T(8,128)(2,1)} %copy-done.76, bf16[1024,2048]{1,0:T(8,128)(2,1)} %constant_dynamic-update-slice_fusion.16), kind=kOutput, calls=%fused_computation.35 | convolution fusion | flops 4308597760 | bytes 14686208 | tf_op jit(solution)/shard_map/dot_general | solution.py:31
  321.8 7.7 convert_reduce_fusion.2
  329.5 6.4 fusion.91
  335.9 7.1 add_convert_fusion.2
  347.2 5.1 convolution_convert_fusion.1
  356.3 22.5 %collective-permute-done.32 = bf16[256,2048]{1,0:T(8,128)(2,1)S(1)} collective-permute-done((bf16[256,2048]{1,0:T(8,128)(2,1)S(1)}, bf16[256,2048]{1,0:T(8,128)(2,1)S(1)}, u32[]{:S(2)}, u32[]{:S(2)}) %collective-permute-start.32) | collective-permute-done | bytes 1048608 | tf_op jit(solution)/shard_map/ppermute | solution.py:40
  379.9 5.0 add_convert_fusion.1
  387.5 14.0 %collective-permute-done.33 = bf16[256,2048]{1,0:T(8,128)(2,1)} collective-permute-done((bf16[256,2048]{1,0:T(8,128)(2,1)}, bf16[256,2048]{1,0:T(8,128)(2,1)}, u32[]{:S(2)}, u32[]{:S(2)}) %collective-permute-start.33) | collective-permute-done | bytes 1048608 | tf_op jit(solution)/shard_map/ppermute | solution.py:40
  403.4 4.2 multiply_reduce_fusion
  440.5 5.6 collective-permute-start.36
  446.2 13.7 %collective-permute-done.36 = bf16[256,512]{1,0:T(8,128)(2,1)S(1)} collective-permute-done((bf16[256,512]{1,0:T(8,128)(2,1)S(1)}, bf16[256,512]{1,0:T(8,128)(2,1)S(1)}, u32[]{:S(2)}, u32[]{:S(2)}) %collective-permute-start.36) | collective-permute-done | bytes 262176 | tf_op jit(solution)/shard_map/ppermute | solution.py:45
  460.6 8.6 collective-permute-start.38
  469.2 22.0 %collective-permute-done.37 = bf16[256,512]{1,0:T(8,128)(2,1)} collective-permute-done((bf16[256,512]{1,0:T(8,128)(2,1)}, bf16[256,512]{1,0:T(8,128)(2,1)}, u32[]{:S(2)}, u32[]{:S(2)}) %collective-permute-start.37) | collective-permute-done | bytes 262176 | tf_op jit(solution)/shard_map/ppermute | solution.py:45
  509.6 28.3 %attend_back.1 = bf16[8,128,1536]{2,1,0:T(8,128)(2,1)S(1)} custom-call(s32[8]{0:T(128)S(1)} %copy-done.44, f32[8]{0:T(128)S(1)} %copy-done.42, bf16[8,128,1536]{2,1,0:T(8,128)(2,1)} %bitcast.259, bf16[8,128,512]{2,1,0:T(8,128)(2,1)S(1)} %bitcast.257), custom_call_target="tpu_custom_call" | custom-call | flops 32212254720 | bytes 1 | tf_op jit(solution)/shard_map/attend_back/pallas_call | solution.py:245
  553.0 5.5 collective-permute-start.45
  563.3 10.0 %fusion.76 = (bf16[2048]{0:T(1024)(128)(2,1)S(1)}, bf16[2048]{0:T(1024)(128)(2,1)S(1)}, bf16[1024,2048]{1,0:T(8,128)(2,1)S(1)}) fusion(f32[1024]{0:T(1024)S(1)} %copy-done.87, f32[1024]{0:T(1024)S(1)} %copy-done.82, bf16[1,1024,2048]{2,1,0:T(8,128)(2,1)} %all-gather.12.cloned.1.call-done, bf16[1024,1536]{1,0:T(8,128)(2,1)S(1)} %get-tuple-element.128.refs_1_, ...), kind=kOutput, calls=%fused_computation.309 | convolution fusion | flops 6469709824 | bytes 17842176 | tf_op jit(solution)/shard_map/dot_general | solution.py:31
  586.6 4.5 collective-permute-done.46.refs_3_
  597.5 8.0 fusion.73
  605.5 4.6 copy-done.55
  612.3 9.2 %fusion.92 = f32[1024,2048]{1,0:T(8,128)} fusion(bf16[1024,1024]{1,0:T(8,128)(2,1)S(1)} %copy-done.92, bf16[1024,2048]{1,0:T(8,128)(2,1)} %collective-permute-done.30), kind=kOutput, calls=%fused_computation.325 | convolution fusion | flops 4294967296 | bytes 14680064 | tf_op jit(solution)/shard_map/dot_general | solution.py:23
  623.5 4.8 slice_add_fusion
  632.2 6.9 add_convert_fusion
  640.9 8.1 collective-permute-done.48
  649.1 17.6 %collective-permute-done.50 = bf16[512,768]{0,1:T(8,128)(2,1)S(1)} collective-permute-done((bf16[512,768]{0,1:T(8,128)(2,1)S(1)}, bf16[512,768]{0,1:T(8,128)(2,1)S(1)}, u32[]{:S(2)}, u32[]{:S(2)}) %collective-permute-start.50) | collective-permute-done | bytes 786464 | tf_op jit(solution)/shard_map/ppermute | solution.py:40
  674.7 9.8 %collective-permute-done.52.refs_2_ = bf16[4,256,512]{2,1,0:T(8,128)(2,1)S(1)} collective-permute-done((bf16[4,256,512]{2,1,0:T(8,128)(2,1)}, bf16[4,256,512]{2,1,0:T(8,128)(2,1)S(1)}, u32[]{:S(2)}, u32[]{:S(2)}) %collective-permute-start.52) | collective-permute-done | bytes 1048608 | tf_op jit(solution)/shard_map/ppermute | solution.py:51
  694.3 16.5 %collective-permute-done.53 = bf16[256,2048]{1,0:T(8,128)(2,1)} collective-permute-done((bf16[256,2048]{1,0:T(8,128)(2,1)}, bf16[256,2048]{1,0:T(8,128)(2,1)}, u32[]{:S(2)}, u32[]{:S(2)}) %collective-permute-start.53) | collective-permute-done | bytes 1048608 | tf_op jit(solution)/shard_map/ppermute | solution.py:40
  710.9 22.8 %collective-permute-done.54 = bf16[256,2048]{1,0:T(8,128)(2,1)} collective-permute-done((bf16[256,2048]{1,0:T(8,128)(2,1)}, bf16[256,2048]{1,0:T(8,128)(2,1)}, u32[]{:S(2)}, u32[]{:S(2)}) %collective-permute-start.54) | collective-permute-done | bytes 1048608 | tf_op jit(solution)/shard_map/ppermute | solution.py:40
  738.5 4.4 copy.211
  742.9 29.5 %collective-permute-done.58 = bf16[4,256,512]{2,1,0:T(8,128)(2,1)S(1)} collective-permute-done((bf16[4,256,512]{2,1,0:T(8,128)(2,1)S(1)}, bf16[4,256,512]{2,1,0:T(8,128)(2,1)S(1)}, u32[]{:S(2)}, u32[]{:S(2)}) %collective-permute-start.58) | collective-permute-done | bytes 1048608 | tf_op jit(solution)/shard_map/ppermute | solution.py:51
  776.4 10.5 %reduce-scatter.11.cloned.1.call-done.refs_0_ = bf16[272,2048]{1,0:T(8,128)(2,1)} async-done(((bf16[1088,2048]{1,0:T(8,128)(2,1)}), bf16[272,2048]{1,0:T(8,128)(2,1)}) %reduce-scatter.11.cloned.1.call-update) | async-done | bytes 1114128 | tf_op jit(solution)/shard_map/reduce_scatter | solution.py:537
  816.1 39.8 %all-gather.10.cloned.1.call-done = bf16[1536,1024]{1,0:T(8,128)(2,1)} async-done(((bf16[1536,256]{1,0:T(8,128)(2,1)}), bf16[1536,1024]{1,0:T(8,128)(2,1)}) %all-gather.10.cloned.1.call-update) | async-done | bytes 3145744 | tf_op jit(solution)/shard_map/all_gather | solution.py:567
  855.9 5.5 convert.42
  (571 shorter events, 300.9 us)
Async XLA Ops:
  7.2 86.8 %all-gather.12.cloned.1.call-start = ((), (), s32[]{:S(2)}) async-start(), calls=%async_computation.11 | async-start | bytes 5242880 | tf_op jit(solution)/shard_map/all_gather | solution.py:346
  10.3 391.9 %reduce-scatter.5.cloned.1.call-start = ((), (), s32[]{:S(2)}) async-start(), calls=%async_computation.4 | async-start | bytes 5242880 | tf_op jit(solution)/shard_map/reduce_scatter | solution.py:452
  22.4 88.4 %collective-permute-start.7 = (bf16[1024,512]{1,0:T(8,128)(2,1)}, bf16[1024,512]{1,0:T(8,128)(2,1)}, u32[]{:S(2)}, u32[]{:S(2)}) collective-permute-start(bf16[1024,512]{1,0:T(8,128)(2,1)} %param.23), channel_id=1, source_target_pairs={{0,16},{8,24},{16,0},{24,8},{1,17},{9,25},{17,1},{25,9},{2,18},{10... | collective-permute-start | bytes 3145736 | tf_op jit(solution)/shard_map/ppermute | solution.py:40
  22.9 87.9 %collective-permute-start.6 = (bf16[1024,512]{1,0:T(8,128)(2,1)}, bf16[1024,512]{1,0:T(8,128)(2,1)}, u32[]{:S(2)}, u32[]{:S(2)}) collective-permute-start(bf16[1024,512]{1,0:T(8,128)(2,1)} %param.23), channel_id=1, source_target_pairs={{0,8},{8,0},{16,24},{24,16},{1,9},{9,1},{17,25},{25,17},{2,10},{10... | collective-permute-start | bytes 3145736 | tf_op jit(solution)/shard_map/ppermute | solution.py:40
  40.6 32.0 %collective-permute-start.3 = (bf16[272,768]{1,0:T(8,128)(2,1)S(1)}, bf16[272,768]{1,0:T(8,128)(2,1)S(1)}, u32[]{:S(2)}, u32[]{:S(2)}) collective-permute-start(bf16[272,768]{1,0:T(8,128)(2,1)S(1)} %slice.544), channel_id=1, source_target_pairs={{0,8},{8,0},{16,24},{24,16},{1,9},{9,1},{17,25},{25,17},{2,10},{10... | collective-permute-start | bytes 1253384 | tf_op jit(solution)/shard_map/ppermute | solution.py:40
  42.7 29.9 %collective-permute-start.2 = (bf16[272,768]{1,0:T(8,128)(2,1)S(1)}, bf16[272,768]{1,0:T(8,128)(2,1)S(1)}, u32[]{:S(2)}, u32[]{:S(2)}) collective-permute-start(bf16[272,768]{1,0:T(8,128)(2,1)S(1)} %slice.537), channel_id=1, source_target_pairs={{0,16},{8,24},{16,0},{24,8},{1,17},{9,25},{17,1},{25,9},{2,18},{10... | collective-permute-start | bytes 1253384 | tf_op jit(solution)/shard_map/ppermute | solution.py:40
  82.8 50.4 %collective-permute-start.10 = (bf16[512,1024]{1,0:T(8,128)(2,1)}, bf16[512,1024]{1,0:T(8,128)(2,1)}, u32[]{:S(2)}, u32[]{:S(2)}) collective-permute-start(bf16[512,1024]{1,0:T(8,128)(2,1)} %get-tuple-element.82), channel_id=1, source_target_pairs={{0,8},{8,0},{16,24},{24,16},{1,9},{9,1},{17,25},{25,17},{2,10},{10... | collective-permute-start | bytes 3145736 | tf_op jit(solution)/shard_map/ppermute | solution.py:40
  86.9 48.8 %collective-permute-start.11 = (bf16[512,1024]{1,0:T(8,128)(2,1)}, bf16[512,1024]{1,0:T(8,128)(2,1)}, u32[]{:S(2)}, u32[]{:S(2)}) collective-permute-start(bf16[512,1024]{1,0:T(8,128)(2,1)} %get-tuple-element.83), channel_id=1, source_target_pairs={{0,16},{8,24},{16,0},{24,8},{1,17},{9,25},{17,1},{25,9},{2,18},{10... | collective-permute-start | bytes 3145736 | tf_op jit(solution)/shard_map/ppermute | solution.py:40
  98.7 36.9 %collective-permute-start.12 = (bf16[512,1024]{1,0:T(8,128)(2,1)}, bf16[512,1024]{1,0:T(8,128)(2,1)S(1)}, u32[]{:S(2)}, u32[]{:S(2)}) collective-permute-start(bf16[512,1024]{1,0:T(8,128)(2,1)} %get-tuple-element.84), channel_id=1, source_target_pairs={{0,24},{8,16},{16,8},{24,0},{1,25},{9,17},{17,9},{25,1},{2,26},{10... | collective-permute-start | bytes 3145736 | tf_op jit(solution)/shard_map/ppermute | solution.py:40
  113.4 29.0 %collective-permute-start.8 = (bf16[512,512]{1,0:T(8,128)(2,1)S(1)}, bf16[512,512]{1,0:T(8,128)(2,1)S(1)}, u32[]{:S(2)}, u32[]{:S(2)}) collective-permute-start(bf16[512,512]{1,0:T(8,128)(2,1)S(1)} %slice.435), channel_id=1, source_target_pairs={{0,8},{8,0},{16,24},{24,16},{1,9},{9,1},{17,25},{25,17},{2,10},{10... | collective-permute-start | bytes 1572872 | tf_op jit(solution)/shard_map/ppermute | solution.py:40
  114.0 32.0 %collective-permute-start.9 = (bf16[512,512]{1,0:T(8,128)(2,1)S(1)}, bf16[512,512]{1,0:T(8,128)(2,1)S(1)}, u32[]{:S(2)}, u32[]{:S(2)}) collective-permute-start(bf16[512,512]{1,0:T(8,128)(2,1)S(1)} %slice.436), channel_id=1, source_target_pairs={{0,16},{8,24},{16,0},{24,8},{1,17},{9,25},{17,1},{25,9},{2,18},{10... | collective-permute-start | bytes 1572872 | tf_op jit(solution)/shard_map/ppermute | solution.py:40
  154.6 37.9 %collective-permute-start.13 = (bf16[1024,2048]{1,0:T(8,128)(2,1)}, bf16[1024,2048]{1,0:T(8,128)(2,1)}, u32[]{:S(2)}, u32[]{:S(2)}) collective-permute-start(bf16[1024,2048]{1,0:T(8,128)(2,1)} %maximum_dynamic-update-slice_fusion), channel_id=1, source_target_pairs={{0,1},{1,0},{2,3},{3,2},{4,5},{5,4},{6,7},{7,6},{8,9},{9,8},{10,11... | collective-permute-start | bytes 12582920 | tf_op jit(solution)/shard_map/ppermute | solution.py:35
  158.6 32.4 %collective-permute-start.18 = (bf16[256,2048]{1,0:T(8,128)(2,1)S(1)}, bf16[256,2048]{1,0:T(8,128)(2,1)S(1)}, u32[]{:S(2)}, u32[]{:S(2)}) collective-permute-start(bf16[256,2048]{1,0:T(8,128)(2,1)S(1)} %get-tuple-element.90), channel_id=1, source_target_pairs={{0,16},{8,24},{16,0},{24,8},{1,17},{9,25},{17,1},{25,9},{2,18},{10... | collective-permute-start | bytes 3145736 | tf_op jit(solution)/shard_map/ppermute | solution.py:40
  159.2 33.3 %collective-permute-start.17 = (bf16[256,2048]{1,0:T(8,128)(2,1)S(1)}, bf16[256,2048]{1,0:T(8,128)(2,1)S(1)}, u32[]{:S(2)}, u32[]{:S(2)}) collective-permute-start(bf16[256,2048]{1,0:T(8,128)(2,1)S(1)} %get-tuple-element.90), channel_id=1, source_target_pairs={{0,8},{8,0},{16,24},{24,16},{1,9},{9,1},{17,25},{25,17},{2,10},{10... | collective-permute-start | bytes 3145736 | tf_op jit(solution)/shard_map/ppermute | solution.py:40
  179.9 82.3 %collective-permute-start.27 = (bf16[2048,1024]{1,0:T(8,128)(2,1)}, bf16[2048,1024]{1,0:T(8,128)(2,1)}, u32[]{:S(2)}, u32[]{:S(2)}) collective-permute-start(bf16[2048,1024]{1,0:T(8,128)(2,1)} %constant_dynamic-update-slice_fusion.20), channel_id=1, source_target_pairs={{0,1},{1,0},{2,3},{3,2},{4,5},{5,4},{6,7},{7,6},{8,9},{9,8},{10,11... | collective-permute-start | bytes 12582920 | tf_op jit(solution)/shard_map/ppermute | solution.py:35
  189.5 26.4 %collective-permute-start.21 = (bf16[1024,512]{1,0:T(8,128)(2,1)}, bf16[1024,512]{1,0:T(8,128)(2,1)}, u32[]{:S(2)}, u32[]{:S(2)}) collective-permute-start(bf16[1024,512]{1,0:T(8,128)(2,1)} %get-tuple-element.98.refs_3_), channel_id=1, source_target_pairs={{0,8},{8,0},{16,24},{24,16},{1,9},{9,1},{17,25},{25,17},{2,10},{10... | collective-permute-start | bytes 3145736 | tf_op jit(solution)/shard_map/ppermute | solution.py:40
  191.0 26.4 %collective-permute-start.22 = (bf16[1024,512]{1,0:T(8,128)(2,1)}, bf16[1024,512]{1,0:T(8,128)(2,1)}, u32[]{:S(2)}, u32[]{:S(2)}) collective-permute-start(bf16[1024,512]{1,0:T(8,128)(2,1)} %get-tuple-element.99.refs_4_), channel_id=1, source_target_pairs={{0,16},{8,24},{16,0},{24,8},{1,17},{9,25},{17,1},{25,9},{2,18},{10... | collective-permute-start | bytes 3145736 | tf_op jit(solution)/shard_map/ppermute | solution.py:40
  281.2 26.5 %collective-permute-start.29 = (bf16[1024,512]{1,0:T(8,128)(2,1)S(1)}, bf16[1024,512]{1,0:T(8,128)(2,1)S(1)}, u32[]{:S(2)}, u32[]{:S(2)}) collective-permute-start(bf16[1024,512]{1,0:T(8,128)(2,1)S(1)} %get-tuple-element.108), channel_id=1, source_target_pairs={{0,24},{8,16},{16,8},{24,0},{1,25},{9,17},{17,9},{25,1},{2,26},{10... | collective-permute-start | bytes 3145736 | tf_op jit(solution)/shard_map/ppermute | solution.py:40
  311.1 187.0 %reduce-scatter.7.cloned.1.call-start = ((), (), s32[]{:S(2)}) async-start(), calls=%async_computation.5 | async-start | bytes 5242880 | tf_op jit(solution)/shard_map/reduce_scatter | solution.py:460
  352.3 26.6 %collective-permute-start.31 = (bf16[2048,1024]{1,0:T(8,128)(2,1)S(1)}, bf16[2048,1024]{1,0:T(8,128)(2,1)S(1)}, u32[]{:S(2)}, u32[]{:S(2)}) collective-permute-start(bf16[2048,1024]{1,0:T(8,128)(2,1)S(1)} %convolution_convert_fusion.1), channel_id=1, source_target_pairs={{0,1},{1,0},{2,3},{3,2},{4,5},{5,4},{6,7},{7,6},{8,9},{9,8},{10,11... | collective-permute-start | bytes 12582920 | tf_op jit(solution)/shard_map/ppermute | solution.py:35
  352.8 26.0 %collective-permute-start.32 = (bf16[256,2048]{1,0:T(8,128)(2,1)S(1)}, bf16[256,2048]{1,0:T(8,128)(2,1)S(1)}, u32[]{:S(2)}, u32[]{:S(2)}) collective-permute-start(bf16[256,2048]{1,0:T(8,128)(2,1)S(1)} %get-tuple-element.111), channel_id=1, source_target_pairs={{0,8},{8,0},{16,24},{24,16},{1,9},{9,1},{17,25},{25,17},{2,10},{10... | collective-permute-start | bytes 3145736 | tf_op jit(solution)/shard_map/ppermute | solution.py:40
  353.9 47.6 %collective-permute-start.33 = (bf16[256,2048]{1,0:T(8,128)(2,1)}, bf16[256,2048]{1,0:T(8,128)(2,1)}, u32[]{:S(2)}, u32[]{:S(2)}) collective-permute-start(bf16[256,2048]{1,0:T(8,128)(2,1)} %get-tuple-element.112), channel_id=1, source_target_pairs={{0,16},{8,24},{16,0},{24,8},{1,17},{9,25},{17,1},{25,9},{2,18},{10... | collective-permute-start | bytes 3145736 | tf_op jit(solution)/shard_map/ppermute | solution.py:40
  354.4 47.1 %collective-permute-start.34 = (bf16[256,2048]{1,0:T(8,128)(2,1)}, bf16[256,2048]{1,0:T(8,128)(2,1)}, u32[]{:S(2)}, u32[]{:S(2)}) collective-permute-start(bf16[256,2048]{1,0:T(8,128)(2,1)} %get-tuple-element.113), channel_id=1, source_target_pairs={{0,24},{8,16},{16,8},{24,0},{1,25},{9,17},{17,9},{25,1},{2,26},{10... | collective-permute-start | bytes 3145736 | tf_op jit(solution)/shard_map/ppermute | solution.py:40
  387.4 152.9 %reduce-scatter.9.cloned.1.call-start = ((), (), s32[]{:S(2)}) async-start(), calls=%async_computation.6 | async-start | bytes 1310720 | tf_op jit(solution)/shard_map/reduce_scatter | solution.py:490
  437.0 57.6 %collective-permute-start.39 = (bf16[1024,512]{1,0:T(8,128)(2,1)S(1)}, bf16[1024,512]{1,0:T(8,128)(2,1)}, u32[]{:S(2)}, u32[]{:S(2)}) collective-permute-start(bf16[1024,512]{1,0:T(8,128)(2,1)S(1)} %get-tuple-element.121), channel_id=1, source_target_pairs={{0,8},{8,0},{16,24},{24,16},{1,9},{9,1},{17,25},{25,17},{2,10},{10... | collective-permute-start | bytes 3145736 | tf_op jit(solution)/shard_map/ppermute | solution.py:40
  438.1 56.6 %collective-permute-start.40 = (bf16[1024,512]{1,0:T(8,128)(2,1)}, bf16[1024,512]{1,0:T(8,128)(2,1)}, u32[]{:S(2)}, u32[]{:S(2)}) collective-permute-start(bf16[1024,512]{1,0:T(8,128)(2,1)} %get-tuple-element.122), channel_id=1, source_target_pairs={{0,16},{8,24},{16,0},{24,8},{1,17},{9,25},{17,1},{25,9},{2,18},{10... | collective-permute-start | bytes 3145736 | tf_op jit(solution)/shard_map/ppermute | solution.py:40
  438.6 56.1 %collective-permute-start.41 = (bf16[1024,512]{1,0:T(8,128)(2,1)}, bf16[1024,512]{1,0:T(8,128)(2,1)}, u32[]{:S(2)}, u32[]{:S(2)}) collective-permute-start(bf16[1024,512]{1,0:T(8,128)(2,1)} %get-tuple-element.123), channel_id=1, source_target_pairs={{0,24},{8,16},{16,8},{24,0},{1,25},{9,17},{17,9},{25,1},{2,26},{10... | collective-permute-start | bytes 3145736 | tf_op jit(solution)/shard_map/ppermute | solution.py:40
  446.2 45.0 %collective-permute-start.37 = (bf16[256,512]{1,0:T(8,128)(2,1)}, bf16[256,512]{1,0:T(8,128)(2,1)}, u32[]{:S(2)}, u32[]{:S(2)}) collective-permute-start(bf16[256,512]{1,0:T(8,128)(2,1)} %get-tuple-element.117), channel_id=1, source_target_pairs={{0,4},{2,6},{4,0},{6,2},{1,5},{3,7},{5,1},{7,3},{8,12},{10,14},{12... | collective-permute-start | bytes 786440 | tf_op jit(solution)/shard_map/ppermute | solution.py:45
  460.6 30.6 %collective-permute-start.38 = (bf16[256,512]{1,0:T(8,128)(2,1)}, bf16[256,512]{1,0:T(8,128)(2,1)}, u32[]{:S(2)}, u32[]{:S(2)}) collective-permute-start(bf16[256,512]{1,0:T(8,128)(2,1)} %get-tuple-element.118), channel_id=1, source_target_pairs={{0,2},{2,4},{4,6},{6,0},{1,3},{3,5},{5,7},{7,1},{8,10},{10,12},{12... | collective-permute-start | bytes 786440 | tf_op jit(solution)/shard_map/ppermute | solution.py:45
  502.8 83.2 %all-gather.6.cloned.1.call-start = ((), (), s32[]{:S(2)}) async-start(), calls=%async_computation.7 | async-start | bytes 1310720 | tf_op jit(solution)/shard_map/all_gather | solution.py:502
  504.6 34.0 %collective-permute-start.42 = (bf16[512,512]{1,0:T(8,128)(2,1)S(1)}, bf16[512,512]{1,0:T(8,128)(2,1)S(1)}, u32[]{:S(2)}, u32[]{:S(2)}) collective-permute-start(bf16[512,512]{1,0:T(8,128)(2,1)S(1)} %pad_maximum_fusion.6), channel_id=1, source_target_pairs={{0,8},{8,0},{16,24},{24,16},{1,9},{9,1},{17,25},{25,17},{2,10},{10... | collective-permute-start | bytes 1572872 | tf_op jit(solution)/shard_map/ppermute | solution.py:40
  505.8 32.8 %collective-permute-start.43 = (bf16[512,512]{1,0:T(8,128)(2,1)S(1)}, bf16[512,512]{1,0:T(8,128)(2,1)S(1)}, u32[]{:S(2)}, u32[]{:S(2)}) collective-permute-start(bf16[512,512]{1,0:T(8,128)(2,1)S(1)} %pad_maximum_fusion.7), channel_id=1, source_target_pairs={{0,16},{8,24},{16,0},{24,8},{1,17},{9,25},{17,1},{25,9},{2,18},{10... | collective-permute-start | bytes 1572872 | tf_op jit(solution)/shard_map/ppermute | solution.py:40
  507.4 31.2 %collective-permute-start.44 = (bf16[512,512]{1,0:T(8,128)(2,1)S(1)}, bf16[512,512]{1,0:T(8,128)(2,1)S(1)}, u32[]{:S(2)}, u32[]{:S(2)}) collective-permute-start(bf16[512,512]{1,0:T(8,128)(2,1)S(1)} %pad_maximum_fusion.8), channel_id=1, source_target_pairs={{0,24},{8,16},{16,8},{24,0},{1,25},{9,17},{17,9},{25,1},{2,26},{10... | collective-permute-start | bytes 1572872 | tf_op jit(solution)/shard_map/ppermute | solution.py:40
  542.0 234.3 %all-gather.8.cloned.1.call-start = ((), (), s32[]{:S(2)}) async-start(), calls=%async_computation.9 | async-start | bytes 5242880 | tf_op jit(solution)/shard_map/all_gather | solution.py:505
  551.7 39.3 %collective-permute-start.46 = (bf16[4,256,512]{2,1,0:T(8,128)(2,1)}, bf16[4,256,512]{2,1,0:T(8,128)(2,1)}, u32[]{:S(2)}, u32[]{:S(2)}) collective-permute-start(bf16[4,256,512]{2,1,0:T(8,128)(2,1)} %fusion.51), channel_id=1, source_target_pairs={{2,0},{4,2},{6,4},{3,1},{5,3},{7,5},{10,8},{12,10},{14,12},{11,9},... | collective-permute-start | bytes 3145736 | tf_op jit(solution)/shard_map/ppermute | solution.py:51
  553.0 38.0 %collective-permute-start.45 = (bf16[4,256,512]{2,1,0:T(8,128)(2,1)}, bf16[4,256,512]{2,1,0:T(8,128)(2,1)}, u32[]{:S(2)}, u32[]{:S(2)}) collective-permute-start(bf16[4,256,512]{2,1,0:T(8,128)(2,1)} %fusion.51), channel_id=1, source_target_pairs={{0,2},{2,4},{4,6},{1,3},{3,5},{5,7},{8,10},{10,12},{12,14},{9,11},... | collective-permute-start | bytes 3145736 | tf_op jit(solution)/shard_map/ppermute | solution.py:50
  562.6 224.2 %reduce-scatter.11.cloned.1.call-start = ((), (), s32[]{:S(2)}) async-start(), calls=%async_computation.8 | async-start | bytes 5570560 | tf_op jit(solution)/shard_map/reduce_scatter | solution.py:537
  612.2 243.7 %all-gather.10.cloned.1.call-start = ((), (), s32[]{:S(2)}) async-start(), calls=%async_computation.10 | async-start | bytes 3932160 | tf_op jit(solution)/shard_map/all_gather | solution.py:567
  621.4 53.3 %collective-permute-start.51 = (bf16[4,256,512]{2,1,0:T(8,128)(2,1)}, bf16[4,256,512]{2,1,0:T(8,128)(2,1)S(1)}, u32[]{:S(2)}, u32[]{:S(2)}) collective-permute-start(bf16[4,256,512]{2,1,0:T(8,128)(2,1)} %get-tuple-element.131), channel_id=1, source_target_pairs={{2,4},{4,6},{3,5},{5,7},{10,12},{12,14},{11,13},{13,15},{18,20},{2... | collective-permute-start | bytes 3145736 | tf_op jit(solution)/shard_map/ppermute | solution.py:50
  622.2 62.4 %collective-permute-start.52 = (bf16[4,256,512]{2,1,0:T(8,128)(2,1)}, bf16[4,256,512]{2,1,0:T(8,128)(2,1)S(1)}, u32[]{:S(2)}, u32[]{:S(2)}) collective-permute-start(bf16[4,256,512]{2,1,0:T(8,128)(2,1)} %get-tuple-element.132), channel_id=1, source_target_pairs={{2,0},{4,2},{3,1},{5,3},{10,8},{12,10},{11,9},{13,11},{18,16},{20,... | collective-permute-start | bytes 3145736 | tf_op jit(solution)/shard_map/ppermute | solution.py:51
  630.2 36.4 %collective-permute-start.50 = (bf16[512,768]{0,1:T(8,128)(2,1)S(1)}, bf16[512,768]{0,1:T(8,128)(2,1)S(1)}, u32[]{:S(2)}, u32[]{:S(2)}) collective-permute-start(bf16[512,768]{0,1:T(8,128)(2,1)S(1)} %get-tuple-element.164), channel_id=1, source_target_pairs={{0,24},{8,16},{16,8},{24,0},{1,25},{9,17},{17,9},{25,1},{2,26},{10... | collective-permute-start | bytes 2359304 | tf_op jit(solution)/shard_map/ppermute | solution.py:40
  631.7 36.3 %collective-permute-start.49 = (bf16[512,768]{0,1:T(8,128)(2,1)S(1)}, bf16[512,768]{0,1:T(8,128)(2,1)S(1)}, u32[]{:S(2)}, u32[]{:S(2)}) collective-permute-start(bf16[512,768]{0,1:T(8,128)(2,1)S(1)} %get-tuple-element.165), channel_id=1, source_target_pairs={{0,16},{8,24},{16,0},{24,8},{1,17},{9,25},{17,1},{25,9},{2,18},{10... | collective-permute-start | bytes 2359304 | tf_op jit(solution)/shard_map/ppermute | solution.py:40
  684.5 26.3 %collective-permute-start.53 = (bf16[256,2048]{1,0:T(8,128)(2,1)}, bf16[256,2048]{1,0:T(8,128)(2,1)}, u32[]{:S(2)}, u32[]{:S(2)}) collective-permute-start(bf16[256,2048]{1,0:T(8,128)(2,1)} %get-tuple-element.134), channel_id=1, source_target_pairs={{0,8},{8,0},{16,24},{24,16},{1,9},{9,1},{17,25},{25,17},{2,10},{10... | collective-permute-start | bytes 3145736 | tf_op jit(solution)/shard_map/ppermute | solution.py:40
  686.0 47.7 %collective-permute-start.54 = (bf16[256,2048]{1,0:T(8,128)(2,1)}, bf16[256,2048]{1,0:T(8,128)(2,1)}, u32[]{:S(2)}, u32[]{:S(2)}) collective-permute-start(bf16[256,2048]{1,0:T(8,128)(2,1)} %get-tuple-element.135), channel_id=1, source_target_pairs={{0,16},{8,24},{16,0},{24,8},{1,17},{9,25},{17,1},{25,9},{2,18},{10... | collective-permute-start | bytes 3145736 | tf_op jit(solution)/shard_map/ppermute | solution.py:40
  687.5 46.2 %collective-permute-start.55 = (bf16[256,2048]{1,0:T(8,128)(2,1)}, bf16[256,2048]{1,0:T(8,128)(2,1)}, u32[]{:S(2)}, u32[]{:S(2)}) collective-permute-start(bf16[256,2048]{1,0:T(8,128)(2,1)} %get-tuple-element.136), channel_id=1, source_target_pairs={{0,24},{8,16},{16,8},{24,0},{1,25},{9,17},{17,9},{25,1},{2,26},{10... | collective-permute-start | bytes 3145736 | tf_op jit(solution)/shard_map/ppermute | solution.py:40
  688.5 48.0 %collective-permute-start.57 = (bf16[4,256,512]{2,1,0:T(8,128)(2,1)S(1)}, bf16[4,256,512]{2,1,0:T(8,128)(2,1)}, u32[]{:S(2)}, u32[]{:S(2)}) collective-permute-start(bf16[4,256,512]{2,1,0:T(8,128)(2,1)S(1)} %get-tuple-element.139), channel_id=1, source_target_pairs={{4,6},{5,7},{12,14},{13,15},{20,22},{21,23},{28,30},{29,31}} | collective-permute-start | bytes 3145736 | tf_op jit(solution)/shard_map/ppermute | solution.py:50
  692.7 79.6 %collective-permute-start.58 = (bf16[4,256,512]{2,1,0:T(8,128)(2,1)S(1)}, bf16[4,256,512]{2,1,0:T(8,128)(2,1)S(1)}, u32[]{:S(2)}, u32[]{:S(2)}) collective-permute-start(bf16[4,256,512]{2,1,0:T(8,128)(2,1)S(1)} %get-tuple-element.140), channel_id=1, source_target_pairs={{2,0},{3,1},{10,8},{11,9},{18,16},{19,17},{26,24},{27,25}} | collective-permute-start | bytes 3145736 | tf_op jit(solution)/shard_map/ppermute | solution.py:51
  736.4 38.3 %collective-permute-start.56 = (bf16[256,2048]{1,0:T(8,128)(2,1)S(1)}, bf16[256,2048]{1,0:T(8,128)(2,1)S(1)}, u32[]{:S(2)}, u32[]{:S(2)}) collective-permute-start(bf16[256,2048]{1,0:T(8,128)(2,1)S(1)} %add_convert_fusion.5), channel_id=1, source_target_pairs={{0,1},{1,0},{2,3},{3,2},{4,5},{5,4},{6,7},{7,6},{8,9},{9,8},{10,11... | collective-permute-start | bytes 3145736 | tf_op jit(solution)/shard_map/ppermute | solution.py:35
  (120 other events, 1447.7 us)
Sparse Core Ops, SparseCore 0:
  10.5 83.5 all-gather.11
  311.2 78.5 reduce-scatter.4
  392.7 93.7 reduce-scatter.6
  502.9 26.2 reduce-scatter.8
  542.1 35.1 all-gather.5
  578.8 102.0 all-gather.7
  683.9 102.8 reduce-scatter.10
  792.5 63.3 all-gather.9
